TPU v7x, 256 devices: a whole 4x4x8 slice. The times are simulated.
256 devices in a mesh: span: 64 (over x, z, core), row: 4 (over y).
Axes of the slice: x: 4, y: 4, z: 8, core: 2. Of those that a mesh axis runs over, the one named last changes fastest.
Arguments:
- features: bfloat16 [64, 4, 32, 32, 128], P('span', None, 'row'), may hold values from -6 to 6
- clip_lengths: int32 [16], replicated, may hold values from 1 to 32, 64 in all
- clip_order: int32 [16], replicated, may hold values from 0 to 15, each once
- weight_a: bfloat16 [3, 3, 3, 128, 128], replicated, may hold values from -0.109375 to 0.109375
- bias_a: float32 [128], replicated, may hold values from -3 to 3
- weight_b: bfloat16 [3, 3, 3, 128, 128], replicated, may hold values from -0.109375 to 0.109375
- bias_b: float32 [128], replicated, may hold values from -3 to 3
- weight_down: bfloat16 [3, 3, 3, 128, 128], replicated, may hold values from -0.109375 to 0.109375
- bias_down: float32 [128], replicated, may hold values from -3 to 3
Outputs:
- patch_tokens: bfloat16 [64, 2, 8, 8, 512], P('span', None, 'row')
Inputs may be any that keep to these rules, and one draw needn't show every extreme that they name: `clip_lengths`: the lengths sum to 64. `clip_order`: each clip appears once.
All inputs are finite; a program needn't handle non-finite values.
Results may differ from a plain program's by a relative error of at most 0.0051.
Values may be sent and summed in bfloat16 or wider, within the bound.
No kernel may reach another device: no remote copies, remote signals or barrier semaphores. Data moves between devices by JAX's collectives and lax.ppermute only.
A program may use at most 64 MiB of HBM per device.

v0:
```python
import jax
import jax.numpy as jnp
from jax import lax
from jax.sharding import PartitionSpec as P


def padded_2(block, sides, width):
    for axis, dim in sides:
        count = lax.axis_size(axis)
        forward = [(i, i + 1) for i in range(count - 1)]
        backward = [(target, source) for source, target in forward]
        low = lax.ppermute(
            lax.slice_in_dim(block, block.shape[dim] - width, None, axis=dim), axis, forward
        )
        high = lax.ppermute(lax.slice_in_dim(block, 0, width, axis=dim), axis, backward)
        block = jnp.concatenate([low, block, high], axis=dim)
    return block


def passed_along(x, axis, by):
    peers = lax.axis_size(axis)
    pairs = [(i, i + by) for i in range(peers) if 0 <= i + by < peers]
    return lax.ppermute(x, axis, pairs)


def positions(clip_lengths, clip_order, slots):
    clips = clip_lengths.shape[0]
    pick = clip_order[:, None] == jnp.arange(clips, dtype=jnp.int32)[None, :]
    ordered = jnp.sum(jnp.where(pick, clip_lengths[None, :], 0), axis=1)
    ends = jnp.cumsum(ordered)
    starts = ends - ordered
    began = jnp.where(starts[None, :] <= slots[:, None], starts[None, :], 0)
    return slots - jnp.max(began, axis=1)


def with_rim(field):
    padded = padded_2(field, (("row", 1),), 1)
    return jnp.pad(padded, ((0, 0), (0, 0), (1, 1), (0, 0)))


def conv_plain(padded, weight):
    chans = padded.shape[3]
    out_frames = padded.shape[0] - 2
    height = padded.shape[1] - 2
    width = padded.shape[2] - 2
    total = jnp.zeros((out_frames * height * width, weight.shape[4]), jnp.float32)
    for tap_t in range(3):
        for tap_h in range(3):
            slab = padded[tap_t : tap_t + out_frames, tap_h : tap_h + height]
            stacked = jnp.concatenate(
                [slab[:, :, tap_w : tap_w + width] for tap_w in range(3)], axis=-1
            )
            total = total + jnp.dot(
                stacked.reshape(-1, 3 * chans),
                weight[tap_t, tap_h].reshape(3 * chans, -1),
                preferred_element_type=jnp.float32,
            )
    return total.reshape(out_frames, height, width, -1)


def conv_strided(padded, weight):
    chans = padded.shape[3]
    out_frames = (padded.shape[0] - 1) // 2
    out_rows = (padded.shape[1] - 1) // 2
    out_cols = (padded.shape[2] - 1) // 2
    total = jnp.zeros((out_frames * out_rows * out_cols, weight.shape[4]), jnp.float32)
    for tap_t in range(3):
        for tap_h in range(3):
            slab = padded[
                tap_t : tap_t + 2 * out_frames - 1 : 2, tap_h : tap_h + 2 * out_rows - 1 : 2
            ]
            stacked = jnp.concatenate(
                [slab[:, :, tap_w : tap_w + 2 * out_cols - 1 : 2] for tap_w in range(3)], axis=-1
            )
            total = total + jnp.dot(
                stacked.reshape(-1, 3 * chans),
                weight[tap_t, tap_h].reshape(3 * chans, -1),
                preferred_element_type=jnp.float32,
            )
    return total.reshape(out_frames, out_rows, out_cols, -1)


def per_device(
    features, clip_lengths, clip_order, weight_a, bias_a, weight_b, bias_b, weight_down, bias_down
):
    slot = jnp.reshape(lax.axis_index("span"), (1,))
    position = positions(clip_lengths, clip_order, slot)[0]
    frames = features[0]
    length = frames.shape[0]

    def prepare(field):
        return with_rim(field)

    keep = (position > 0).astype(jnp.bfloat16)

    def context(field):
        earlier = passed_along(field[length - 2 :], "span", 1)
        return jnp.concatenate([earlier * keep, field], axis=0)

    hidden = jax.nn.silu(conv_plain(prepare(context(frames)), weight_a) + bias_a).astype(
        jnp.bfloat16
    )
    mixed = (
        frames.astype(jnp.float32) + conv_plain(prepare(context(hidden)), weight_b) + bias_b
    ).astype(jnp.bfloat16)
    mixed_ext = context(mixed)
    height = mixed_ext.shape[1]
    above = passed_along(mixed_ext[:, height - 1 :], "row", 1)
    padded = jnp.concatenate([above, mixed_ext], axis=1)
    padded = jnp.pad(padded, ((0, 0), (0, 0), (1, 0), (0, 0)))
    latent = (conv_strided(padded, weight_down) + bias_down).astype(jnp.bfloat16)
    frames_n, rows_n, cols_n, chans = latent.shape
    grouped = latent.reshape(frames_n, rows_n // 2, 2, cols_n // 2, 2, chans)
    grouped = jnp.transpose(grouped, (0, 1, 3, 2, 4, 5))
    return grouped.reshape(1, frames_n, rows_n // 2, cols_n // 2, 4 * chans)


def solution(mesh):
    placed = (P("span", None, "row", None, None), P(), P(), P(), P(), P(), P(), P(), P())
    return jax.shard_map(
        per_device,
        mesh=mesh,
        in_specs=placed,
        out_specs=P("span", None, "row", None, None),
        check_vma=False,
    )
```

profile of v0, /device:TPU:14, one launch (start us, length us, event | category | flops | bytes accessed | tf_op | source)
XLA Modules:
  0.0 70.9 jit_solution(6612463564133090498)
XLA Ops:
  0.0 0.9 %slice_bitcast_fusion = bf16[2,8,32,128]{3,2,1,0:T(8,128)(2,1)S(1)} fusion(bf16[1,4,8,32,128]{4,3,2,1,0:T(8,128)(2,1)} %param.9), kind=kLoop, calls=%fused_computation.83 | loop fusion | bytes 262144 | tf_op jit(solution)/shard_map/slice | solution.py:97
  0.9 1.9 %collective-permute-start = (bf16[2,8,32,128]{3,2,1,0:T(8,128)(2,1)S(1)}, bf16[2,8,32,128]{3,2,1,0:T(8,128)(2,1)S(1)}, u32[]{:S(2)}, u32[]{:S(2)}) collective-permute-start(bf16[2,8,32,128]{3,2,1,0:T(8,128)(2,1)S(1)} %slice_bitcast_fusion), channel_id=1, source_target_pairs={{0,4},{4,8},{8,12},{12,16},{16,20},{20,24},{24,28},{28,32},{32,36}... | collective-permute-start | bytes 393224 | tf_op jit(solution)/shard_map/ppermute | solution.py:23
  2.8 0.9 %select_reduce_fusion = s32[16]{0:T(128)S(1)} fusion(s32[16]{0:T(128)} %param.10, s32[16]{0:T(128)} %param.11), kind=kLoop, calls=%fused_computation.103 | loop fusion | flops 752 | bytes 192 | tf_op jit(solution)/shard_map/reduce_sum | solution.py:29
  3.9 0.6 fusion.28
  5.3 1.4 %fusion.32 = (bf16[1,1,3,128,128]{4,3,2,1,0:T(8,128)(2,1)S(1)}, bf16[1,1,3,128,128]{4,3,2,1,0:T(8,128)(2,1)S(1)}, bf16[1,1,3,128,128]{4,3,2,1,0:T(8,128)(2,1)S(1...) fusion(bf16[3,3,3,128,128]{4,3,2,1,0:T(8,128)(2,1)} %param.12), kind=kLoop, calls=%fused_computation.110 | loop fusion | bytes 1769472 | tf_op jit(solution)/shard_map/slice | solution.py:55
  6.6 4.4 %collective-permute-done = bf16[2,8,32,128]{3,2,1,0:T(8,128)(2,1)S(1)} collective-permute-done((bf16[2,8,32,128]{3,2,1,0:T(8,128)(2,1)S(1)}, bf16[2,8,32,128]{3,2,1,0:T(8,128)(2,1)S(1)}, u32[]{:S(2)}, u32[]{:S(2)}) %collective-permute-start) | collective-permute-done | bytes 131104 | tf_op jit(solution)/shard_map/ppermute | solution.py:23
  11.1 3.5 %collective-permute-start.1 = (bf16[6,1,32,128]{3,2,1,0:T(8,128)(2,1)S(1)}, bf16[6,1,32,128]{3,2,1,0:T(8,128)(2,1)S(1)}, u32[]{:S(2)}, u32[]{:S(2)}) collective-permute-start(bf16[6,1,32,128]{3,2,1,0:T(8,128)(2,1)S(1)} %get-tuple-element.95), channel_id=1, source_target_pairs={{0,1},{1,2},{2,3},{4,5},{5,6},{6,7},{8,9},{9,10},{10,11},{12,13},{... | collective-permute-start | bytes 147464 | tf_op jit(solution)/shard_map/ppermute | solution.py:12
  14.6 2.4 %collective-permute-start.2 = (bf16[6,1,32,128]{3,2,1,0:T(8,128)(2,1)S(1)}, bf16[6,1,32,128]{3,2,1,0:T(8,128)(2,1)S(1)}, u32[]{:S(2)}, u32[]{:S(2)}) collective-permute-start(bf16[6,1,32,128]{3,2,1,0:T(8,128)(2,1)S(1)} %get-tuple-element.96), channel_id=1, source_target_pairs={{1,0},{2,1},{3,2},{5,4},{6,5},{7,6},{9,8},{10,9},{11,10},{13,12},{... | collective-permute-start | bytes 147464 | tf_op jit(solution)/shard_map/ppermute | solution.py:15
  17.1 3.5 %collective-permute-done.2 = bf16[6,1,32,128]{3,2,1,0:T(8,128)(2,1)S(1)} collective-permute-done((bf16[6,1,32,128]{3,2,1,0:T(8,128)(2,1)S(1)}, bf16[6,1,32,128]{3,2,1,0:T(8,128)(2,1)S(1)}, u32[]{:S(2)}, u32[]{:S(2)}) %collective-permute-start.2) | collective-permute-done | bytes 49184 | tf_op jit(solution)/shard_map/ppermute | solution.py:15
  20.8 0.8 %fusion.34 = (bf16[4,8,32,128]{3,2,1,0:T(8,128)(2,1)S(1)}, bf16[4,8,32,128]{3,2,1,0:T(8,128)(2,1)S(1)}, bf16[4,8,32,128]{3,2,1,0:T(8,128)(2,1)S(1)}, bf16[4,8,32...) fusion(bf16[6,10,34,128]{3,2,1,0:T(8,128)(2,1)S(1)} %fusion.20), kind=kLoop, calls=%fused_computation.112 | loop fusion | bytes 9437184 | tf_op jit(solution)/shard_map/slice | solution.py:51
  22.9 0.4 convolution_add_fusion.15
  23.3 0.4 convolution_add_fusion.14
  23.9 0.4 convolution_add_fusion.13
  24.3 0.4 convolution_add_fusion.12
  25.3 0.4 convolution_add_fusion.10
  26.9 1.9 %collective-permute-start.3 = (bf16[2,8,32,128]{3,2,1,0:T(8,128)(2,1)S(1)}, bf16[2,8,32,128]{3,2,1,0:T(8,128)(2,1)S(1)}, u32[]{:S(2)}, u32[]{:S(2)}) collective-permute-start(bf16[2,8,32,128]{3,2,1,0:T(8,128)(2,1)S(1)} %slice.632), channel_id=1, source_target_pairs={{0,4},{4,8},{8,12},{12,16},{16,20},{20,24},{24,28},{28,32},{32,36}... | collective-permute-start | bytes 393224 | tf_op jit(solution)/shard_map/ppermute | solution.py:23
  28.9 6.4 %collective-permute-done.3 = bf16[2,8,32,128]{3,2,1,0:T(8,128)(2,1)S(1)} collective-permute-done((bf16[2,8,32,128]{3,2,1,0:T(8,128)(2,1)S(1)}, bf16[2,8,32,128]{3,2,1,0:T(8,128)(2,1)S(1)}, u32[]{:S(2)}, u32[]{:S(2)}) %collective-permute-start.3) | collective-permute-done | bytes 131104 | tf_op jit(solution)/shard_map/ppermute | solution.py:23
  35.4 3.2 %collective-permute-start.4 = (bf16[6,1,32,128]{3,2,1,0:T(8,128)(2,1)S(1)}, bf16[6,1,32,128]{3,2,1,0:T(8,128)(2,1)S(1)}, u32[]{:S(2)}, u32[]{:S(2)}) collective-permute-start(bf16[6,1,32,128]{3,2,1,0:T(8,128)(2,1)S(1)} %get-tuple-element.91), channel_id=1, source_target_pairs={{0,1},{1,2},{2,3},{4,5},{5,6},{6,7},{8,9},{9,10},{10,11},{12,13},{... | collective-permute-start | bytes 147464 | tf_op jit(solution)/shard_map/ppermute | solution.py:12
  38.6 2.6 %collective-permute-start.5 = (bf16[6,1,32,128]{3,2,1,0:T(8,128)(2,1)S(1)}, bf16[6,1,32,128]{3,2,1,0:T(8,128)(2,1)S(1)}, u32[]{:S(2)}, u32[]{:S(2)}) collective-permute-start(bf16[6,1,32,128]{3,2,1,0:T(8,128)(2,1)S(1)} %get-tuple-element.92), channel_id=1, source_target_pairs={{1,0},{2,1},{3,2},{5,4},{6,5},{7,6},{9,8},{10,9},{11,10},{13,12},{... | collective-permute-start | bytes 147464 | tf_op jit(solution)/shard_map/ppermute | solution.py:15
  41.3 3.2 %collective-permute-done.5 = bf16[6,1,32,128]{3,2,1,0:T(8,128)(2,1)S(1)} collective-permute-done((bf16[6,1,32,128]{3,2,1,0:T(8,128)(2,1)S(1)}, bf16[6,1,32,128]{3,2,1,0:T(8,128)(2,1)S(1)}, u32[]{:S(2)}, u32[]{:S(2)}) %collective-permute-start.5) | collective-permute-done | bytes 49184 | tf_op jit(solution)/shard_map/ppermute | solution.py:15
  45.0 0.8 %fusion.33 = (bf16[4,8,32,128]{3,2,1,0:T(8,128)(2,1)S(1)}, bf16[4,8,32,128]{3,2,1,0:T(8,128)(2,1)S(1)}, bf16[4,8,32,128]{3,2,1,0:T(8,128)(2,1)S(1)}, bf16[4,8,32...) fusion(bf16[6,10,34,128]{3,2,1,0:T(8,128)(2,1)S(1)} %select_max, ...), kind=kLoop, calls=%fused_computation.111 | loop fusion | bytes 9437184 | tf_op jit(solution)/shard_map/slice | solution.py:51
  46.0 0.4 fusion.41
  47.1 0.4 convolution_add_fusion.7
  47.5 0.4 convolution_add_fusion.6
  47.9 0.4 convolution_add_fusion.5
  48.5 0.4 convolution_add_fusion.4
  50.0 0.4 convolution_add_fusion
  50.8 2.1 %collective-permute-start.6 = (bf16[2,8,32,128]{3,2,1,0:T(8,128)(2,1)S(1)}, bf16[2,8,32,128]{3,2,1,0:T(8,128)(2,1)S(1)}, u32[]{:S(2)}, u32[]{:S(2)}) collective-permute-start(bf16[2,8,32,128]{3,2,1,0:T(8,128)(2,1)S(1)} %slice.659), channel_id=1, source_target_pairs={{0,4},{4,8},{8,12},{12,16},{16,20},{20,24},{24,28},{28,32},{32,36}... | collective-permute-start | bytes 393224 | tf_op jit(solution)/shard_map/ppermute | solution.py:23
  52.8 6.5 %collective-permute-done.6 = bf16[2,8,32,128]{3,2,1,0:T(8,128)(2,1)S(1)} collective-permute-done((bf16[2,8,32,128]{3,2,1,0:T(8,128)(2,1)S(1)}, bf16[2,8,32,128]{3,2,1,0:T(8,128)(2,1)S(1)}, u32[]{:S(2)}, u32[]{:S(2)}) %collective-permute-start.6) | collective-permute-done | bytes 131104 | tf_op jit(solution)/shard_map/ppermute | solution.py:23
  59.3 1.9 %collective-permute-start.7 = (bf16[6,1,32,128]{3,2,1,0:T(8,128)(2,1)S(1)}, bf16[6,1,32,128]{3,2,1,0:T(8,128)(2,1)S(1)}, u32[]{:S(2)}, u32[]{:S(2)}) collective-permute-start(bf16[6,1,32,128]{3,2,1,0:T(8,128)(2,1)S(1)} %pad_maximum_fusion.28), channel_id=1, source_target_pairs={{0,1},{1,2},{2,3},{4,5},{5,6},{6,7},{8,9},{9,10},{10,11},{12,13},{... | collective-permute-start | bytes 147464 | tf_op jit(solution)/shard_map/ppermute | solution.py:23
  61.4 4.0 %collective-permute-done.7 = bf16[6,1,32,128]{3,2,1,0:T(8,128)(2,1)S(1)} collective-permute-done((bf16[6,1,32,128]{3,2,1,0:T(8,128)(2,1)S(1)}, bf16[6,1,32,128]{3,2,1,0:T(8,128)(2,1)S(1)}, u32[]{:S(2)}, u32[]{:S(2)}) %collective-permute-start.7) | collective-permute-done | bytes 49184 | tf_op jit(solution)/shard_map/ppermute | solution.py:23
  70.3 0.6 copy.15
  (106 shorter events, 11.9 us)
Async XLA Ops:
  0.9 10.1 %collective-permute-start = (bf16[2,8,32,128]{3,2,1,0:T(8,128)(2,1)S(1)}, bf16[2,8,32,128]{3,2,1,0:T(8,128)(2,1)S(1)}, u32[]{:S(2)}, u32[]{:S(2)}) collective-permute-start(bf16[2,8,32,128]{3,2,1,0:T(8,128)(2,1)S(1)} %slice_bitcast_fusion), channel_id=1, source_target_pairs={{0,4},{4,8},{8,12},{12,16},{16,20},{20,24},{24,28},{28,32},{32,36}... | collective-permute-start | bytes 393224 | tf_op jit(solution)/shard_map/ppermute | solution.py:23
  5.2 5.8 %copy-start = (bf16[1,4,8,32,128]{4,3,2,1,0:T(8,128)(2,1)S(1)}, bf16[1,4,8,32,128]{4,3,2,1,0:T(8,128)(2,1)}, u32[]{:S(2)}) copy-start(bf16[1,4,8,32,128]{4,3,2,1,0:T(8,128)(2,1)} %param.9) | copy-start | bytes 786436
  11.1 6.0 %collective-permute-start.1 = (bf16[6,1,32,128]{3,2,1,0:T(8,128)(2,1)S(1)}, bf16[6,1,32,128]{3,2,1,0:T(8,128)(2,1)S(1)}, u32[]{:S(2)}, u32[]{:S(2)}) collective-permute-start(bf16[6,1,32,128]{3,2,1,0:T(8,128)(2,1)S(1)} %get-tuple-element.95), channel_id=1, source_target_pairs={{0,1},{1,2},{2,3},{4,5},{5,6},{6,7},{8,9},{9,10},{10,11},{12,13},{... | collective-permute-start | bytes 147464 | tf_op jit(solution)/shard_map/ppermute | solution.py:12
  14.6 6.0 %collective-permute-start.2 = (bf16[6,1,32,128]{3,2,1,0:T(8,128)(2,1)S(1)}, bf16[6,1,32,128]{3,2,1,0:T(8,128)(2,1)S(1)}, u32[]{:S(2)}, u32[]{:S(2)}) collective-permute-start(bf16[6,1,32,128]{3,2,1,0:T(8,128)(2,1)S(1)} %get-tuple-element.96), channel_id=1, source_target_pairs={{1,0},{2,1},{3,2},{5,4},{6,5},{7,6},{9,8},{10,9},{11,10},{13,12},{... | collective-permute-start | bytes 147464 | tf_op jit(solution)/shard_map/ppermute | solution.py:15
  26.1 0.7 copy-start.5
  26.5 2.4 %copy-start.1 = (bf16[3,3,3,128,128]{4,3,2,1,0:T(8,128)(2,1)S(1)}, bf16[3,3,3,128,128]{4,3,2,1,0:T(8,128)(2,1)}, u32[]{:S(2)}) copy-start(bf16[3,3,3,128,128]{4,3,2,1,0:T(8,128)(2,1)} %param.14) | copy-start | bytes 2654212
  26.9 8.4 %collective-permute-start.3 = (bf16[2,8,32,128]{3,2,1,0:T(8,128)(2,1)S(1)}, bf16[2,8,32,128]{3,2,1,0:T(8,128)(2,1)S(1)}, u32[]{:S(2)}, u32[]{:S(2)}) collective-permute-start(bf16[2,8,32,128]{3,2,1,0:T(8,128)(2,1)S(1)} %slice.632), channel_id=1, source_target_pairs={{0,4},{4,8},{8,12},{12,16},{16,20},{20,24},{24,28},{28,32},{32,36}... | collective-permute-start | bytes 393224 | tf_op jit(solution)/shard_map/ppermute | solution.py:23
  35.4 6.0 %collective-permute-start.4 = (bf16[6,1,32,128]{3,2,1,0:T(8,128)(2,1)S(1)}, bf16[6,1,32,128]{3,2,1,0:T(8,128)(2,1)S(1)}, u32[]{:S(2)}, u32[]{:S(2)}) collective-permute-start(bf16[6,1,32,128]{3,2,1,0:T(8,128)(2,1)S(1)} %get-tuple-element.91), channel_id=1, source_target_pairs={{0,1},{1,2},{2,3},{4,5},{5,6},{6,7},{8,9},{9,10},{10,11},{12,13},{... | collective-permute-start | bytes 147464 | tf_op jit(solution)/shard_map/ppermute | solution.py:12
  38.6 6.0 %collective-permute-start.5 = (bf16[6,1,32,128]{3,2,1,0:T(8,128)(2,1)S(1)}, bf16[6,1,32,128]{3,2,1,0:T(8,128)(2,1)S(1)}, u32[]{:S(2)}, u32[]{:S(2)}) collective-permute-start(bf16[6,1,32,128]{3,2,1,0:T(8,128)(2,1)S(1)} %get-tuple-element.92), channel_id=1, source_target_pairs={{1,0},{2,1},{3,2},{5,4},{6,5},{7,6},{9,8},{10,9},{11,10},{13,12},{... | collective-permute-start | bytes 147464 | tf_op jit(solution)/shard_map/ppermute | solution.py:15
  50.0 0.7 copy-start.3
  50.7 10.6 %copy-start.2 = (bf16[3,3,3,128,128]{4,3,2,1,0:T(8,128)(2,1)S(1)}, bf16[3,3,3,128,128]{4,3,2,1,0:T(8,128)(2,1)}, u32[]{:S(2)}) copy-start(bf16[3,3,3,128,128]{4,3,2,1,0:T(8,128)(2,1)} %param.16) | copy-start | bytes 2654212
  50.8 8.5 %collective-permute-start.6 = (bf16[2,8,32,128]{3,2,1,0:T(8,128)(2,1)S(1)}, bf16[2,8,32,128]{3,2,1,0:T(8,128)(2,1)S(1)}, u32[]{:S(2)}, u32[]{:S(2)}) collective-permute-start(bf16[2,8,32,128]{3,2,1,0:T(8,128)(2,1)S(1)} %slice.659), channel_id=1, source_target_pairs={{0,4},{4,8},{8,12},{12,16},{16,20},{20,24},{24,28},{28,32},{32,36}... | collective-permute-start | bytes 393224 | tf_op jit(solution)/shard_map/ppermute | solution.py:23
  59.3 6.0 %collective-permute-start.7 = (bf16[6,1,32,128]{3,2,1,0:T(8,128)(2,1)S(1)}, bf16[6,1,32,128]{3,2,1,0:T(8,128)(2,1)S(1)}, u32[]{:S(2)}, u32[]{:S(2)}) collective-permute-start(bf16[6,1,32,128]{3,2,1,0:T(8,128)(2,1)S(1)} %pad_maximum_fusion.28), channel_id=1, source_target_pairs={{0,1},{1,2},{2,3},{4,5},{5,6},{6,7},{8,9},{9,10},{10,11},{12,13},{... | collective-permute-start | bytes 147464 | tf_op jit(solution)/shard_map/ppermute | solution.py:23
  69.3 0.9 %copy-start.4 = (f32[128]{0:T(128)S(1)}, f32[128]{0:T(128)}, u32[]{:S(2)}) copy-start(f32[128]{0:T(128)} %param.17) | copy-start | bytes 1540
where the time goes:
time: 71.3 us; the launch traced here: 70.9 us
  waiting for transfers between devices  28.1 us (39%)
  starting transfers between devices  19.5 us (27%)
  local copies, waits for them, and re-layouts  8.4 us (12%)
  matrix products  8.21 us (12%)
  other arithmetic  5.15 us (7%)
  between operations  1.57 us (2%)
    ppermute x4, waiting for transfers between devices, passed_along(): return lax.ppermute(x, axis, pairs)  21.2 us
    ppermute x4, starting transfers between devices, passed_along(): return lax.ppermute(x, axis, pairs)  7.81 us
    ppermute x2, waiting for transfers between devices, padded_2(): lax.ppermute(lax.slice_in_dim(block, 0, width, axis=dim), axis, backward)  6.69 us
    ppermute x2, starting transfers between devices, padded_2(): lax.ppermute(lax.slice_in_dim(block, block.shape[dim] - width, None, axis...  6.68 us
    dot_general x18, matrix products, conv_plain(): jnp.dot(stacked.reshape(-1, 3 * chans), weight[tap_t, tap_h].reshape(3 *...  6.65 us
    ppermute x2, starting transfers between devices, padded_2(): lax.ppermute(lax.slice_in_dim(block, 0, width, axis=dim), axis, backward)  5.01 us
    slice x27, local copies, waits for them, and re-layouts, conv_strided(): slab[:, :, tap_w:tap_w + 2 * out_cols - 1:2]  2.59 us
    concatenate x12, other arithmetic, conv_plain(): jnp.concatenate([slab[:, :, tap_w:tap_w + width] for tap_w in range(3)],...  2.12 us
  transfers between devices with their start and end apart: 8, of which 8 were waited for; matrix products, arithmetic and copies ran while one was open for 5% of the time, Pallas kernels for 0%

commit v1 on v0

--- a/solution.py
+++ b/solution.py
@@ -4,20 +4,7 @@
 from jax.sharding import PartitionSpec as P
 
 
-def padded_2(block, sides, width):
-    for axis, dim in sides:
-        count = lax.axis_size(axis)
-        forward = [(i, i + 1) for i in range(count - 1)]
-        backward = [(target, source) for source, target in forward]
-        low = lax.ppermute(
-            lax.slice_in_dim(block, block.shape[dim] - width, None, axis=dim), axis, forward
-        )
-        high = lax.ppermute(lax.slice_in_dim(block, 0, width, axis=dim), axis, backward)
-        block = jnp.concatenate([low, block, high], axis=dim)
-    return block
-
-
-def passed_along(x, axis, by):
+def shifted(x, axis, by):
     peers = lax.axis_size(axis)
     pairs = [(i, i + by) for i in range(peers) if 0 <= i + by < peers]
     return lax.ppermute(x, axis, pairs)
@@ -31,11 +18,6 @@
     starts = ends - ordered
     began = jnp.where(starts[None, :] <= slots[:, None], starts[None, :], 0)
     return slots - jnp.max(began, axis=1)
-
-
-def with_rim(field):
-    padded = padded_2(field, (("row", 1),), 1)
-    return jnp.pad(padded, ((0, 0), (0, 0), (1, 1), (0, 0)))
 
 
 def conv_plain(padded, weight):
@@ -83,31 +65,33 @@
 def per_device(
     features, clip_lengths, clip_order, weight_a, bias_a, weight_b, bias_b, weight_down, bias_down
 ):
-    slot = jnp.reshape(lax.axis_index("span"), (1,))
-    position = positions(clip_lengths, clip_order, slot)[0]
+    slot = lax.axis_index("span")
+    block = lax.axis_index("row")
+    position = positions(clip_lengths, clip_order, jnp.stack([slot, slot - 1]))
+    keep = (position > 0).astype(jnp.bfloat16)
     frames = features[0]
-    length = frames.shape[0]
+    height = frames.shape[1]
+    near = shifted(frames, "span", 1) * keep[0]
+    far = shifted(frames[2:], "span", 2) * (keep[0] * keep[1])
+    field = jnp.concatenate([far, near, frames[:3]], axis=0)
+    above = shifted(field[:, height - 3 :], "row", 1)
+    below = shifted(field[:, :2], "row", -1)
+    field = jnp.concatenate([above, field, below], axis=1)
+    prior = jnp.where(jnp.arange(7) < 4, keep[0], 1).astype(jnp.bfloat16)
 
-    def prepare(field):
-        return with_rim(field)
+    def inside(first, count):
+        rows = block * height + first + jnp.arange(count)
+        limit = height * lax.axis_size("row")
+        return ((rows >= 0) & (rows < limit)).astype(jnp.bfloat16)
 
-    keep = (position > 0).astype(jnp.bfloat16)
-
-    def context(field):
-        earlier = passed_along(field[length - 2 :], "span", 1)
-        return jnp.concatenate([earlier * keep, field], axis=0)
-
-    hidden = jax.nn.silu(conv_plain(prepare(context(frames)), weight_a) + bias_a).astype(
-        jnp.bfloat16
-    )
+    cols = ((0, 0), (0, 0), (1, 1), (0, 0))
+    hidden = jax.nn.silu(conv_plain(jnp.pad(field, cols), weight_a) + bias_a).astype(jnp.bfloat16)
+    hidden = hidden * (prior[:, None, None, None] * inside(-2, 11)[None, :, None, None])
     mixed = (
-        frames.astype(jnp.float32) + conv_plain(prepare(context(hidden)), weight_b) + bias_b
+        field[4:, 2:11].astype(jnp.float32) + conv_plain(jnp.pad(hidden, cols), weight_b) + bias_b
     ).astype(jnp.bfloat16)
-    mixed_ext = context(mixed)
-    height = mixed_ext.shape[1]
-    above = passed_along(mixed_ext[:, height - 1 :], "row", 1)
-    padded = jnp.concatenate([above, mixed_ext], axis=1)
-    padded = jnp.pad(padded, ((0, 0), (0, 0), (1, 0), (0, 0)))
+    mixed = mixed * (prior[2:, None, None, None] * inside(-1, 9)[None, :, None, None])
+    padded = jnp.pad(mixed, ((0, 0), (0, 0), (1, 0), (0, 0)))
     latent = (conv_strided(padded, weight_down) + bias_down).astype(jnp.bfloat16)
     frames_n, rows_n, cols_n, chans = latent.shape
     grouped = latent.reshape(frames_n, rows_n // 2, 2, cols_n // 2, 2, chans)

time: 71.3 us -> 62.8 us (0.88); the launches traced: 70.9 us -> 61.6 us
  waiting for transfers between devices: 28.1 us -> 7.14 us
  local copies, waits for them, and re-layouts: 8.4 us -> 18.6 us
  starting transfers between devices: 19.5 us -> 11.7 us
  other arithmetic: 5.15 us -> 10.3 us
  matrix products: 8.21 us -> 11.8 us
    ppermute x8 -> x4, waiting for transfers between devices: 28.1 us -> 7.14 us  [shifted(): return lax.ppermute(x, axis, pairs)]
    ppermute x8 -> x4, starting transfers between devices: 19.5 us -> 11.7 us  [shifted(): return lax.ppermute(x, axis, pairs)]
    slice x6 -> x5, local copies, waits for them, and re-layouts: 2.01 us -> 7.39 us  [conv_plain(): slab[:, :, tap_w:tap_w + width]]
    dot_general x18, matrix products: 6.65 us -> 10.3 us  [conv_plain(): jnp.dot(stacked.reshape(-1, 3 * chans), weight[tap_t, tap_h].reshape(3 *...]
    mul x3 -> x6, other arithmetic: 0.04 us -> 3.11 us  [the longest x1 1.52 us: per_device(): near = shifted(frames, 'span', 1) * keep[0]]
    concatenate x12 -> x14, other arithmetic: 2.12 us -> 4.77 us  [conv_plain(): jnp.concatenate([slab[:, :, tap_w:tap_w + width] for tap_w in range(3)],...]
    slice x3 -> x4, local copies, waits for them, and re-layouts: 0.93 us -> 3.16 us  [the longest x2 2.14 us: per_device(): far = shifted(frames[2:], 'span', 2) * (keep[0] * keep[1])]
    unnamed x12 -> x26, local copies, waits for them, and re-layouts: 0.56 us -> 2.25 us
  transfers between devices with their start and end apart: 8 -> 4, of which waited for: 8 -> 3; matrix products, arithmetic and copies ran while one was open for 5% -> 14% of each run, Pallas kernels for 0% -> 0%
where the time goes in v1:
time: 62.8 us; the launch traced here: 61.6 us
  local copies, waits for them, and re-layouts  18.6 us (30%)
  matrix products  11.8 us (19%)
  starting transfers between devices  11.7 us (19%)
  other arithmetic  10.3 us (16%)
  waiting for transfers between devices  7.14 us (11%)
  between operations  2 us (3%)
    ppermute x4, starting transfers between devices, shifted(): return lax.ppermute(x, axis, pairs)  11.7 us
    dot_general x18, matrix products, conv_plain(): jnp.dot(stacked.reshape(-1, 3 * chans), weight[tap_t, tap_h].reshape(3 *...  10.3 us
    slice x5, local copies, waits for them, and re-layouts, conv_plain(): slab[:, :, tap_w:tap_w + width]  7.39 us
    ppermute x4, waiting for transfers between devices, shifted(): return lax.ppermute(x, axis, pairs)  7.14 us
    concatenate x14, other arithmetic, conv_plain(): jnp.concatenate([slab[:, :, tap_w:tap_w + width] for tap_w in range(3)],...  4.77 us
    slice x27, local copies, waits for them, and re-layouts, conv_strided(): slab[:, :, tap_w:tap_w + 2 * out_cols - 1:2]  2.59 us
    unnamed x26, local copies, waits for them, and re-layouts  2.25 us
    slice x2, local copies, waits for them, and re-layouts, conv_plain(): weight[tap_t, tap_h].reshape(3 * chans, -1)  2.24 us
  transfers between devices with their start and end apart: 4, of which 3 were waited for; matrix products, arithmetic and copies ran while one was open for 14% of the time, Pallas kernels for 0%

profile of v1, /device:TPU:14, one launch (start us, length us, event | category | flops | bytes accessed | tf_op | source)
XLA Modules:
  0.0 61.6 jit_solution(4870571516462387057)
XLA Ops:
  0.0 2.0 %collective-permute-start.1 = (bf16[4,8,32,128]{3,2,1,0:T(8,128)(2,1)}, bf16[4,8,32,128]{3,2,1,0:T(8,128)(2,1)}, u32[]{:S(2)}, u32[]{:S(2)}) collective-permute-start(bf16[4,8,32,128]{3,2,1,0:T(8,128)(2,1)} %bitcast.144), channel_id=1, source_target_pairs={{0,4},{4,8},{8,12},{12,16},{16,20},{20,24},{24,28},{28,32},{32,36}... | collective-permute-start | bytes 786440 | tf_op jit(solution)/shard_map/ppermute | solution.py:10
  2.1 1.6 %slice_bitcast_fusion.1 = bf16[2,8,32,128]{3,2,1,0:T(8,128)(2,1)} fusion(bf16[1,4,8,32,128]{4,3,2,1,0:T(8,128)(2,1)} %param.9), kind=kLoop, calls=%fused_computation.98 | loop fusion | bytes 262144 | tf_op jit(solution)/shard_map/slice | solution.py:75
  3.6 3.8 %collective-permute-start = (bf16[2,8,32,128]{3,2,1,0:T(8,128)(2,1)}, bf16[2,8,32,128]{3,2,1,0:T(8,128)(2,1)}, u32[]{:S(2)}, u32[]{:S(2)}) collective-permute-start(bf16[2,8,32,128]{3,2,1,0:T(8,128)(2,1)} %slice_bitcast_fusion.1), channel_id=1, source_target_pairs={{0,8},{4,12},{8,16},{12,20},{16,24},{20,28},{24,32},{28,36},{32,40... | collective-permute-start | bytes 393224 | tf_op jit(solution)/shard_map/ppermute | solution.py:10
  7.4 0.9 %slice_bitcast_fusion = bf16[3,8,32,128]{3,2,1,0:T(8,128)(2,1)S(1)} fusion(bf16[1,4,8,32,128]{4,3,2,1,0:T(8,128)(2,1)} %param.9), kind=kLoop, calls=%fused_computation.94 | loop fusion | bytes 393216 | tf_op jit(solution)/shard_map/slice | solution.py:76
  8.4 0.9 %select_reduce_fusion = s32[16]{0:T(128)S(1)} fusion(s32[16]{0:T(128)} %param.10, s32[16]{0:T(128)} %param.11), kind=kLoop, calls=%fused_computation.111 | loop fusion | flops 752 | bytes 192 | tf_op jit(solution)/shard_map/reduce_sum | solution.py:16
  9.9 0.6 fusion.10
  10.5 2.2 %fusion.7 = (bf16[1,1,3,128,128]{4,3,2,1,0:T(8,128)(2,1)}, bf16[1,1,3,128,128]{4,3,2,1,0:T(8,128)(2,1)}, bf16[1,1,3,128,128]{4,3,2,1,0:T(8,128)(2,1)}, bf16[1,1,...) fusion(bf16[3,3,3,128,128]{4,3,2,1,0:T(8,128)(2,1)} %param.12), kind=kLoop, calls=%fused_computation.125 | loop fusion | bytes 1769472 | tf_op jit(solution)/shard_map/slice | solution.py:37
  14.8 0.6 %collective-permute-done = bf16[2,8,32,128]{3,2,1,0:T(8,128)(2,1)} collective-permute-done((bf16[2,8,32,128]{3,2,1,0:T(8,128)(2,1)}, bf16[2,8,32,128]{3,2,1,0:T(8,128)(2,1)}, u32[]{:S(2)}, u32[]{:S(2)}) %collective-permute-start) | collective-permute-done | bytes 131104 | tf_op jit(solution)/shard_map/ppermute | solution.py:10
  15.4 0.9 %broadcast_multiply_fusion.1 = bf16[2,8,32,128]{3,2,1,0:T(8,128)(2,1)S(1)} fusion(bf16[2,8,32,128]{3,2,1,0:T(8,128)(2,1)} %collective-permute-done, bf16[]{:T(256)S(6)} %mul.75), kind=kLoop, calls=%fused_computation.109 | loop fusion | flops 65536 | bytes 262146 | tf_op jit(solution)/shard_map/mul | solution.py:75
  16.4 1.5 %broadcast_multiply_fusion = bf16[4,8,32,128]{3,2,1,0:T(8,128)(2,1)S(1)} fusion(bf16[4,8,32,128]{3,2,1,0:T(8,128)(2,1)} %collective-permute-done.1, bf16[]{:T(256)} %bitcast.4), kind=kLoop, calls=%fused_computation.97 | loop fusion | flops 131072 | bytes 524290 | tf_op jit(solution)/shard_map/mul | solution.py:74
  18.0 2.4 %collective-permute-start.3 = (bf16[9,2,32,128]{3,2,1,0:T(8,128)(2,1)S(1)}, bf16[9,2,32,128]{3,2,1,0:T(8,128)(2,1)S(1)}, u32[]{:S(2)}, u32[]{:S(2)}) collective-permute-start(bf16[9,2,32,128]{3,2,1,0:T(8,128)(2,1)S(1)} %pad_maximum_fusion.20), channel_id=1, source_target_pairs={{1,0},{2,1},{3,2},{5,4},{6,5},{7,6},{9,8},{10,9},{11,10},{13,12},{... | collective-permute-start | bytes 442376 | tf_op jit(solution)/shard_map/ppermute | solution.py:10
  20.3 3.5 %collective-permute-start.2 = (bf16[9,3,32,128]{3,2,1,0:T(8,128)(2,1)S(1)}, bf16[9,3,32,128]{3,2,1,0:T(8,128)(2,1)S(1)}, u32[]{:S(2)}, u32[]{:S(2)}) collective-permute-start(bf16[9,3,32,128]{3,2,1,0:T(8,128)(2,1)S(1)} %pad_maximum_fusion.19), channel_id=1, source_target_pairs={{0,1},{1,2},{2,3},{4,5},{5,6},{6,7},{8,9},{9,10},{10,11},{12,13},{... | collective-permute-start | bytes 663560 | tf_op jit(solution)/shard_map/ppermute | solution.py:10
  23.9 2.5 %collective-permute-done.3 = bf16[9,2,32,128]{3,2,1,0:T(8,128)(2,1)S(1)} collective-permute-done((bf16[9,2,32,128]{3,2,1,0:T(8,128)(2,1)S(1)}, bf16[9,2,32,128]{3,2,1,0:T(8,128)(2,1)S(1)}, u32[]{:S(2)}, u32[]{:S(2)}) %collective-permute-start.3) | collective-permute-done | bytes 147488 | tf_op jit(solution)/shard_map/ppermute | solution.py:10
  26.4 4.0 %collective-permute-done.2 = bf16[9,3,32,128]{3,2,1,0:T(8,128)(2,1)S(1)} collective-permute-done((bf16[9,3,32,128]{3,2,1,0:T(8,128)(2,1)S(1)}, bf16[9,3,32,128]{3,2,1,0:T(8,128)(2,1)S(1)}, u32[]{:S(2)}, u32[]{:S(2)}) %collective-permute-start.2) | collective-permute-done | bytes 221216 | tf_op jit(solution)/shard_map/ppermute | solution.py:10
  30.5 4.5 %pad_slice_fusion.1 = (bf16[7,11,32,128]{3,2,1,0:T(8,128)(2,1)S(1)}, bf16[7,11,32,128]{3,2,1,0:T(8,128)(2,1)S(1)}, bf16[7,11,32,128]{3,2,1,0:T(8,128)(2,1)S(1)},...) fusion(bf16[9,13,32,128]{3,2,1,0:T(8,128)(2,1)S(1)} %pad_maximu, ...), kind=kLoop, calls=%fused_computation.45 | loop fusion | bytes 14204928 | tf_op jit(solution)/shard_map/slice | solution.py:33
  35.0 0.6 fusion.4
  36.0 0.6 %pad_maximum_fusion = (bf16[7,11,32,384]{3,2,1,0:T(8,128)(2,1)S(1)}, bf16[7,11,32,384]{3,2,1,0:T(8,128)(2,1)S(1)}) fusion(bf16[7,11,32,128]{3,2,1,0:T(8,128)(2,1)S(1)} %get-tuple-element.6, bf16[7,11,32,128]{3,2,1,0:T(8,128)(2,1)S(1)} %get-tuple-element.58, bf16[7,11,32,128]{3,2,1,0:T(8,128)(2,1)S(1)} %get-tuple-element.28, ...), kind=kLoop, calls=%fused_computation.16 | loop fusion | flops 11354112 | bytes 7569408 | tf_op jit(solution)/shard_map/concatenate | solution.py:32
  36.6 0.7 %fusion.11 = f32[2464,128]{1,0:T(8,128)S(1)} fusion(bf16[2464,384]{1,0:T(8,128)(2,1)S(1)} %bitcast.124, bf16[384,128]{1,0:T(8,128)(2,1)S(1)} %bitcast.145), kind=kOutput, calls=%fused_computation.129 | convolution fusion | flops 242221056 | bytes 3252224 | tf_op jit(solution)/shard_map/dot_general | solution.py:35
  37.5 0.7 %convolution_add_fusion.7 = f32[2464,128]{1,0:T(8,128)S(1)} fusion(f32[2464,128]{1,0:T(8,128)S(1)} %fusion.11, bf16[2464,384]{1,0:T(8,128)(2,1)S(1)} %bitcast.129, bf16[384,128]{1,0:T(8,128)(2,1)S(1)} %bitcast.180), kind=kOutput, calls=%fused_computation.7 | convolution fusion | flops 242536448 | bytes 4513792 | tf_op jit(solution)/shard_map/dot_general | solution.py:35
  38.2 0.6 pad_maximum_fusion.2
  39.1 0.7 %convolution_add_fusion.6 = f32[2464,128]{1,0:T(8,128)S(1)} fusion(f32[2464,128]{1,0:T(8,128)S(1)} %convolution_add_fusion.7, bf16[2464,384]{1,0:T(8,128)(2,1)S(1)} %bitcast.130, bf16[384,128]{1,0:T(8,128)(2,1)S(1)} %bitcast.179), kind=kOutput, calls=%fused_computation.6 | convolution fusion | flops 242536448 | bytes 4513792 | tf_op jit(solution)/shard_map/dot_general | solution.py:35
  40.0 0.7 %convolution_add_fusion.5 = f32[2464,128]{1,0:T(8,128)S(1)} fusion(f32[2464,128]{1,0:T(8,128)S(1)} %convolution_add_fusion.6, bf16[2464,384]{1,0:T(8,128)(2,1)S(1)} %bitcast.126, bf16[384,128]{1,0:T(8,128)(2,1)S(1)} %bitcast.178), kind=kOutput, calls=%fused_computation.5 | convolution fusion | flops 242536448 | bytes 4513792 | tf_op jit(solution)/shard_map/dot_general | solution.py:35
  40.7 0.6 pad_maximum_fusion.4
  41.6 0.7 %convolution_add_fusion.4 = f32[2464,128]{1,0:T(8,128)S(1)} fusion(f32[2464,128]{1,0:T(8,128)S(1)} %convolution_add_fusion.5, bf16[2464,384]{1,0:T(8,128)(2,1)S(1)} %bitcast.131, bf16[384,128]{1,0:T(8,128)(2,1)S(1)} %bitcast.177), kind=kOutput, calls=%fused_computation.4 | convolution fusion | flops 242536448 | bytes 4513792 | tf_op jit(solution)/shard_map/dot_general | solution.py:35
  42.4 0.7 %convolution_add_fusion.3 = f32[2464,128]{1,0:T(8,128)S(1)} fusion(f32[2464,128]{1,0:T(8,128)S(1)} %convolution_add_fusion.4, bf16[2464,384]{1,0:T(8,128)(2,1)S(1)} %bitcast.127, bf16[384,128]{1,0:T(8,128)(2,1)S(1)} %bitcast.176), kind=kOutput, calls=%fused_computation.3 | convolution fusion | flops 242536448 | bytes 4513792 | tf_op jit(solution)/shard_map/dot_general | solution.py:35
  43.1 0.8 %pad_maximum_fusion.6 = (bf16[7,11,32,384]{3,2,1,0:T(8,128)(2,1)S(1)}, bf16[7,11,32,384]{3,2,1,0:T(8,128)(2,1)S(1)}) fusion(bf16[7,11,32,128]{3,2,1,0:T(8,128)(2,1)S(1)} %get-tuple-element.18, bf16[7,11,32,128]{3,2,1,0:T(8,128)(2,1)S(1)} %get-tuple-element.56, bf16[7,11,32,128]{3,2,1,0:T(8,128)(2,1)S(1)} %get-tuple-element.17, ...), kind=kLoop, calls=%fused_computation.22 | loop fusion | flops 11354112 | bytes 7569408 | tf_op jit(solution)/shard_map/concatenate | solution.py:32
  44.0 0.7 %convolution_add_fusion.2 = f32[2464,128]{1,0:T(8,128)S(1)} fusion(f32[2464,128]{1,0:T(8,128)S(1)} %convolution_add_fusion.3, bf16[2464,384]{1,0:T(8,128)(2,1)S(1)} %bitcast.132, bf16[384,128]{1,0:T(8,128)(2,1)S(1)} %bitcast.175), kind=kOutput, calls=%fused_computation.2 | convolution fusion | flops 242536448 | bytes 4513792 | tf_op jit(solution)/shard_map/dot_general | solution.py:35
  44.9 0.7 %convolution_add_fusion.1 = f32[2464,128]{1,0:T(8,128)S(1)} fusion(f32[2464,128]{1,0:T(8,128)S(1)} %convolution_add_fusion.2, bf16[2464,384]{1,0:T(8,128)(2,1)S(1)} %bitcast.128, bf16[384,128]{1,0:T(8,128)(2,1)S(1)} %bitcast.174), kind=kOutput, calls=%fused_computation.1 | convolution fusion | flops 242536448 | bytes 4513792 | tf_op jit(solution)/shard_map/dot_general | solution.py:35
  45.9 0.6 copy-done.2
  46.5 0.7 %convolution_add_fusion = f32[2464,128]{1,0:T(8,128)S(1)} fusion(f32[2464,128]{1,0:T(8,128)S(1)} %convolution_add_fusion.1, bf16[2464,384]{1,0:T(8,128)(2,1)S(1)} %bitcast.125, bf16[384,128]{1,0:T(8,128)(2,1)S(1)} %bitcast.173), kind=kOutput, calls=%fused_computation | convolution fusion | flops 242536448 | bytes 4513792 | tf_op jit(solution)/shard_map/dot_general | solution.py:35
  47.6 1.6 %pad_slice_fusion.19 = (bf16[5,9,32,128]{3,2,1,0:T(8,128)(2,1)S(1)}, bf16[5,9,32,128]{3,2,1,0:T(8,128)(2,1)S(1)}, bf16[5,9,32,128]{3,2,1,0:T(8,128)(2,1)S(1)}, b...) fusion(bf16[7,11,32,128]{3,2,1,0:T(8,128)(2,1)S(1)} %fusion), kind=kLoop, calls=%fused_computation.66 | loop fusion | bytes 8372224 | tf_op jit(solution)/shard_map/slice | solution.py:33
  61.0 0.6 %copy.15 = bf16[2,2,8,2,2,128]{5,2,4,3,1,0:T(8,128)(2,1)} copy(bf16[2,2,8,2,2,128]{5,4,2,3,1,0:T(2,128)(2,1)S(1)} %fusion.2) | data formatting | bytes 65536 | tf_op jit(solution)/shard_map/transpose | solution.py:98
  (115 shorter events, 15.6 us)
Async XLA Ops:
  0.0 13.2 %copy-start = (bf16[3,3,3,128,128]{4,3,2,1,0:T(8,128)(2,1)S(1)}, bf16[3,3,3,128,128]{4,3,2,1,0:T(8,128)(2,1)}, u32[]{:S(2)}) copy-start(bf16[3,3,3,128,128]{4,3,2,1,0:T(8,128)(2,1)} %param.14) | copy-start | bytes 2654212
  0.0 16.4 %collective-permute-start.1 = (bf16[4,8,32,128]{3,2,1,0:T(8,128)(2,1)}, bf16[4,8,32,128]{3,2,1,0:T(8,128)(2,1)}, u32[]{:S(2)}, u32[]{:S(2)}) collective-permute-start(bf16[4,8,32,128]{3,2,1,0:T(8,128)(2,1)} %bitcast.144), channel_id=1, source_target_pairs={{0,4},{4,8},{8,12},{12,16},{16,20},{20,24},{24,28},{28,32},{32,36}... | collective-permute-start | bytes 786440 | tf_op jit(solution)/shard_map/ppermute | solution.py:10
  3.6 11.8 %collective-permute-start = (bf16[2,8,32,128]{3,2,1,0:T(8,128)(2,1)}, bf16[2,8,32,128]{3,2,1,0:T(8,128)(2,1)}, u32[]{:S(2)}, u32[]{:S(2)}) collective-permute-start(bf16[2,8,32,128]{3,2,1,0:T(8,128)(2,1)} %slice_bitcast_fusion.1), channel_id=1, source_target_pairs={{0,8},{4,12},{8,16},{12,20},{16,24},{20,28},{24,32},{28,36},{32,40... | collective-permute-start | bytes 393224 | tf_op jit(solution)/shard_map/ppermute | solution.py:10
  8.4 5.0 %copy-start.1 = (bf16[3,3,3,128,128]{4,3,2,1,0:T(8,128)(2,1)S(1)}, bf16[3,3,3,128,128]{4,3,2,1,0:T(8,128)(2,1)}, u32[]{:S(2)}) copy-start(bf16[3,3,3,128,128]{4,3,2,1,0:T(8,128)(2,1)} %param.16) | copy-start | bytes 2654212
  18.0 8.5 %collective-permute-start.3 = (bf16[9,2,32,128]{3,2,1,0:T(8,128)(2,1)S(1)}, bf16[9,2,32,128]{3,2,1,0:T(8,128)(2,1)S(1)}, u32[]{:S(2)}, u32[]{:S(2)}) collective-permute-start(bf16[9,2,32,128]{3,2,1,0:T(8,128)(2,1)S(1)} %pad_maximum_fusion.20), channel_id=1, source_target_pairs={{1,0},{2,1},{3,2},{5,4},{6,5},{7,6},{9,8},{10,9},{11,10},{13,12},{... | collective-permute-start | bytes 442376 | tf_op jit(solution)/shard_map/ppermute | solution.py:10
  20.3 10.1 %collective-permute-start.2 = (bf16[9,3,32,128]{3,2,1,0:T(8,128)(2,1)S(1)}, bf16[9,3,32,128]{3,2,1,0:T(8,128)(2,1)S(1)}, u32[]{:S(2)}, u32[]{:S(2)}) collective-permute-start(bf16[9,3,32,128]{3,2,1,0:T(8,128)(2,1)S(1)} %pad_maximum_fusion.19), channel_id=1, source_target_pairs={{0,1},{1,2},{2,3},{4,5},{5,6},{6,7},{8,9},{9,10},{10,11},{12,13},{... | collective-permute-start | bytes 663560 | tf_op jit(solution)/shard_map/ppermute | solution.py:10
  36.6 0.9 %copy-start.9 = (bf16[1,1,3,128,128]{4,3,2,1,0:T(8,128)(2,1)S(1)}, bf16[1,1,3,128,128]{4,3,2,1,0:T(8,128)(2,1)}, u32[]{:S(2)}) copy-start(bf16[1,1,3,128,128]{4,3,2,1,0:T(8,128)(2,1)} %get-tuple-element.53) | copy-start | bytes 294916
  38.2 0.9 %copy-start.8 = (bf16[1,1,3,128,128]{4,3,2,1,0:T(8,128)(2,1)S(1)}, bf16[1,1,3,128,128]{4,3,2,1,0:T(8,128)(2,1)}, u32[]{:S(2)}) copy-start(bf16[1,1,3,128,128]{4,3,2,1,0:T(8,128)(2,1)} %get-tuple-element.52) | copy-start | bytes 294916
  39.1 0.9 %copy-start.7 = (bf16[1,1,3,128,128]{4,3,2,1,0:T(8,128)(2,1)S(1)}, bf16[1,1,3,128,128]{4,3,2,1,0:T(8,128)(2,1)}, u32[]{:S(2)}) copy-start(bf16[1,1,3,128,128]{4,3,2,1,0:T(8,128)(2,1)} %get-tuple-element.51) | copy-start | bytes 294916
  40.7 0.9 %copy-start.6 = (bf16[1,1,3,128,128]{4,3,2,1,0:T(8,128)(2,1)S(1)}, bf16[1,1,3,128,128]{4,3,2,1,0:T(8,128)(2,1)}, u32[]{:S(2)}) copy-start(bf16[1,1,3,128,128]{4,3,2,1,0:T(8,128)(2,1)} %get-tuple-element.50) | copy-start | bytes 294916
  41.6 0.9 %copy-start.5 = (bf16[1,1,3,128,128]{4,3,2,1,0:T(8,128)(2,1)S(1)}, bf16[1,1,3,128,128]{4,3,2,1,0:T(8,128)(2,1)}, u32[]{:S(2)}) copy-start(bf16[1,1,3,128,128]{4,3,2,1,0:T(8,128)(2,1)} %get-tuple-element.49) | copy-start | bytes 294916
  43.1 0.9 %copy-start.4 = (bf16[1,1,3,128,128]{4,3,2,1,0:T(8,128)(2,1)S(1)}, bf16[1,1,3,128,128]{4,3,2,1,0:T(8,128)(2,1)}, u32[]{:S(2)}) copy-start(bf16[1,1,3,128,128]{4,3,2,1,0:T(8,128)(2,1)} %get-tuple-element.48) | copy-start | bytes 294916
  44.0 0.9 %copy-start.3 = (bf16[1,1,3,128,128]{4,3,2,1,0:T(8,128)(2,1)S(1)}, bf16[1,1,3,128,128]{4,3,2,1,0:T(8,128)(2,1)}, u32[]{:S(2)}) copy-start(bf16[1,1,3,128,128]{4,3,2,1,0:T(8,128)(2,1)} %get-tuple-element.55) | copy-start | bytes 294916
  45.6 0.9 %copy-start.2 = (bf16[1,1,3,128,128]{4,3,2,1,0:T(8,128)(2,1)S(1)}, bf16[1,1,3,128,128]{4,3,2,1,0:T(8,128)(2,1)}, u32[]{:S(2)}) copy-start(bf16[1,1,3,128,128]{4,3,2,1,0:T(8,128)(2,1)} %get-tuple-element.47) | copy-start | bytes 294916
  46.5 0.7 %copy-start.10 = (f32[128]{0:T(128)S(1)}, f32[128]{0:T(128)}, u32[]{:S(2)}) copy-start(f32[128]{0:T(128)} %param.13) | copy-start | bytes 1540
  55.3 0.7 %copy-start.11 = (f32[128]{0:T(128)S(1)}, f32[128]{0:T(128)}, u32[]{:S(2)}) copy-start(f32[128]{0:T(128)} %param.15) | copy-start | bytes 1540
  59.5 1.4 %copy-start.12 = (f32[128]{0:T(128)S(1)}, f32[128]{0:T(128)}, u32[]{:S(2)}) copy-start(f32[128]{0:T(128)} %param.17) | copy-start | bytes 1540

commit v2 on v1

v2 whole, which is shorter than its diff:
```python
import jax
import jax.numpy as jnp
from jax import lax
from jax.experimental import pallas as pl
from jax.experimental.pallas import tpu as pltpu
from jax.sharding import PartitionSpec as P

BF = jnp.bfloat16
F32 = jnp.float32
C = 128
VMEM = pl.BlockSpec(memory_space=pltpu.VMEM)
SMEM = pl.BlockSpec(memory_space=pltpu.SMEM)


def shifted(x, axis, by):
    peers = lax.axis_size(axis)
    pairs = [(i, i + by) for i in range(peers) if 0 <= i + by < peers]
    return lax.ppermute(x, axis, pairs)


def continues(lengths, order, slot):
    begin = jnp.int32(0)
    first = jnp.int32(0)
    for k in range(order.shape[0]):
        first = jnp.where(begin == slot, jnp.int32(1), first)
        begin = begin + lengths[order[k]]
    return 1 - first


def pack_weights(a, b, pa, pb):
    for src, dst in ((a, pa), (b, pb)):
        for t in range(3):
            for i in range(4):
                for w in range(3):
                    for j in range(2):
                        k = i - j
                        value = src[t * 9 + k * 3 + w] if 0 <= k <= 2 else jnp.zeros((C, C), BF)
                        dst[pl.ds((t * 4 + i) * C, C), pl.ds((w * 2 + j) * C, C)] = value


def pack_halo(own, near, up, down):
    for f in range(4):
        up[f] = near[f, 5:8]
        down[f] = near[f, 0:2]
        up[4 + f] = own[f, 5:8]
        down[4 + f] = own[f, 0:2]


def feature_row(own, near, above, below, frame, row):
    f = frame + 4
    if row < 0:
        return above[f, row + 3]
    if row < 8:
        return near[f, row] if f < 4 else own[f - 4, row]
    if row < 10:
        return below[f, row - 8]
    return jnp.zeros((32, C), BF)


def fill_pairs(dst, at, refs, frame, scale):
    for pair in range(7):
        for half in range(2):
            value = feature_row(*refs, frame, 2 * pair + half - 3)
            if scale is not None:
                value = value * scale
            dst[at, pair, :, half * C : half * C + C] = value


def conv_pairs(src, first, pairs, weight):
    rows = pairs * 32
    lhs = jnp.concatenate(
        [src[first + t, h : h + pairs].reshape(rows, 2 * C) for t in range(3) for h in range(2)],
        axis=1,
    )
    y = jnp.dot(lhs, weight[...], preferred_element_type=F32)
    col = lax.broadcasted_iota(jnp.int32, (rows, 2 * C), 0) % 32
    left = jnp.where(col == 0, 0.0, pltpu.roll(y[:, : 2 * C], 1, 0))
    right = jnp.where(col == 31, 0.0, pltpu.roll(y[:, 4 * C :], rows - 1, 0))
    return (y[:, 2 * C : 4 * C] + left + right).reshape(pairs, 32, 2 * C)


def hidden_frame(dst, at, src, first, weight, bias, top, bottom, scale):
    v = conv_pairs(src, first, 6, weight) + bias
    v = v / (1.0 + jnp.exp(-v))
    if scale is not None:
        v = v * scale
    v = v.astype(BF)
    dst[at, 0] = v[0] * top
    dst[at, 1:5] = v[1:5]
    dst[at, 5] = v[5] * bottom


def mixed_frame(dst, at, src, first, weight, bias, residual, top):
    v = residual.astype(F32) + conv_pairs(src, first, 5, weight) + bias
    v = v.astype(BF).astype(F32)
    for pair in range(5):
        dst[at, 2 * pair] = v[pair, :, :C] * top if pair == 0 else v[pair, :, :C]
        dst[at, 2 * pair + 1] = v[pair, :, C:]


def strided_taps(mixed, at):
    taps = []
    zero_first = lax.broadcasted_iota(jnp.int32, (8, C), 0) == 0
    for r in range(9):
        m = [mixed[at, r, pl.ds(k, 8, stride=4), :] for k in range(4)]
        before = jnp.where(zero_first, 0.0, pltpu.roll(m[3], 1, 0))
        taps.append(
            jnp.concatenate(
                [
                    jnp.concatenate(pair, axis=0).astype(BF)
                    for pair in ((before, m[1]), (m[0], m[2]), (m[1], m[3]))
                ],
                axis=1,
            )
        )
    return jnp.concatenate(
        [jnp.concatenate([taps[2 * j + k] for k in range(3)], axis=1) for j in range(4)], axis=0
    )


def down_dot(taps, weight, t):
    return jnp.dot(taps, weight[pl.ds(t * 9 * C, 9 * C), :], preferred_element_type=F32)


def forward_part(
    lengths, order, own, near, above, below, wa, ba, wb, bb, wd, part, late, kept, x, h, m
):
    slot = lax.axis_index("span")
    block = lax.axis_index("row")
    keep = continues(lengths, order, slot).astype(F32).astype(BF)
    top = (block > 0).astype(F32)
    bottom = (block < lax.axis_size("row") - 1).astype(F32).astype(BF)
    refs = (own, near, above, below)
    for i in range(6):
        fill_pairs(x, i, refs, i - 2, keep if i < 2 else None)
    bias = jnp.concatenate([ba[...], ba[...]], axis=1)
    for i in range(4):
        hidden_frame(h, i, x, i, wa, bias, top.astype(BF), bottom, None)
    kept[...] = h[0:2]
    bias = jnp.concatenate([bb[...], bb[...]], axis=1)
    for i in range(2):
        mixed_frame(m, i, h, i, wb, bias, x[4 + i, 1:6], top)
    taps = strided_taps(m, 0)
    part[...] = down_dot(taps, wd, 0) + down_dot(strided_taps(m, 1), wd, 1)
    late[...] = down_dot(taps, wd, 2)


def context_part(
    lengths, order, own, near, above, below, wa, ba, wb, bb, wd, late, kept, early, out, x, h, m
):
    slot = lax.axis_index("span")
    block = lax.axis_index("row")
    keep = continues(lengths, order, slot).astype(F32)
    top = (block > 0).astype(F32)
    bottom = (block < lax.axis_size("row") - 1).astype(F32).astype(BF)
    refs = (own, near, above, below)
    for i in range(6):
        fill_pairs(x, i, refs, i - 4, None)
    bias = jnp.concatenate([ba[...], ba[...]], axis=1)
    for i in range(2):
        hidden_frame(h, i, x, i, wa, bias, top.astype(BF), bottom, keep)
    h[2:4] = kept[...]
    bias = jnp.concatenate([bb[...], bb[...]], axis=1)
    for i in range(2):
        mixed_frame(m, i, h, i, wb, bias, x[4 + i, 1:6], top)
    taps = strided_taps(m, 0)
    early[...] = down_dot(taps, wd, 2)
    out[...] = late[...] + down_dot(taps, wd, 0) + down_dot(strided_taps(m, 1), wd, 1)


def finish(lengths, order, early, late, part, bd, out):
    keep = continues(lengths, order, lax.axis_index("span")).astype(F32)
    for t in range(2):
        v = early[...] + part[...] * keep if t == 0 else late[...]
        v = (v + bd[...]).astype(BF)
        for i in range(2):
            out[t, i] = jnp.concatenate(
                [v[(2 * i + a) * 16 + b * 8 : (2 * i + a) * 16 + b * 8 + 8] for a in range(2) for b in range(2)],
                axis=1,
            )


def kernel(body, name, outs, ins, scratch=(), flops=0):
    return pl.pallas_call(
        body,
        name=name,
        out_shape=[jax.ShapeDtypeStruct(*o) for o in outs],
        in_specs=ins,
        out_specs=[VMEM] * len(outs),
        scratch_shapes=list(scratch),
        compiler_params=pltpu.CompilerParams(vmem_limit_bytes=24 << 20),
        cost_estimate=pl.CostEstimate(flops=flops, bytes_accessed=1 << 20, transcendentals=0),
    )


def per_device(
    features, clip_lengths, clip_order, weight_a, bias_a, weight_b, bias_b, weight_down, bias_down
):
    own = features[0]
    near = shifted(own, "span", 1)
    packed = kernel(pack_weights, "pack_weights", [((12 * C, 6 * C), BF)] * 2, [VMEM] * 2, flops=1 << 30)
    wa, wb = packed(weight_a.reshape(27, C, C), weight_b.reshape(27, C, C))
    wd = weight_down.reshape(27 * C, C)
    ba, bb, bd = (b.reshape(1, C) for b in (bias_a, bias_b, bias_down))
    up, down = kernel(
        pack_halo, "pack_halo", [((8, 3, 32, C), BF), ((8, 2, 32, C), BF)], [VMEM] * 2
    )(own, near)
    above = shifted(up, "row", 1)
    below = shifted(down, "row", -1)
    scratch = [
        pltpu.VMEM((6, 7, 32, 2 * C), BF),
        pltpu.VMEM((4, 6, 32, 2 * C), BF),
        pltpu.VMEM((2, 10, 32, C), F32),
    ]
    common = (clip_lengths, clip_order, own, near, above, below, wa, ba, wb, bb, wd)
    latent = ((64, C), F32)
    part, late, kept = kernel(
        forward_part,
        "forward_part",
        [latent, latent, ((2, 6, 32, 2 * C), BF)],
        [SMEM] * 2 + [VMEM] * 9,
        scratch,
        flops=3 << 30,
    )(*common)
    part = shifted(part, "span", 1)
    early, late = kernel(
        context_part,
        "context_part",
        [latent, latent],
        [SMEM] * 2 + [VMEM] * 11,
        scratch,
        flops=2 << 30,
    )(*common, late, kept)
    (out,) = kernel(
        finish, "finish", [((2, 2, 8, 4 * C), BF)], [SMEM] * 2 + [VMEM] * 4
    )(clip_lengths, clip_order, early, late, part, bd)
    return out[None]


def solution(mesh):
    placed = (P("span", None, "row", None, None), P(), P(), P(), P(), P(), P(), P(), P())
    return jax.shard_map(
        per_device,
        mesh=mesh,
        in_specs=placed,
        out_specs=P("span", None, "row", None, None),
        check_vma=False,
    )
```

time: 62.8 us -> 35.9 us (0.57); the launches traced: 61.6 us -> 35.5 us
  local copies, waits for them, and re-layouts: 18.6 us -> 3.31 us
  matrix products: 11.8 us -> 0 us
  other arithmetic: 10.3 us -> 0 us
  Pallas kernels: 0 us -> 8.07 us
  waiting for transfers between devices: 7.14 us -> 14.1 us
  between operations: 2 us -> 0.12 us
  starting transfers between devices: 11.7 us -> 9.95 us
    slice x40 -> x0, local copies, waits for them, and re-layouts: 15.6 us -> none  [the longest x5 7.39 us: conv_plain(): slab[:, :, tap_w:tap_w + width]]
    dot_general x27 -> x0, matrix products: 11.8 us -> none  [the longest x18 10.3 us: conv_plain(): jnp.dot(stacked.reshape(-1, 3 * chans), weight[tap_t, tap_h].reshape(3 *...]
    pallas_call x0 -> x5, Pallas kernels: none -> 8.07 us  [the longest x1 3.6 us: per_device(): kernel(forward_part, 'forward_part', [latent, latent, ((2, 6, 32, 2 * C),...]
    ppermute x4, waiting for transfers between devices: 7.14 us -> 14.1 us  [shifted(): return lax.ppermute(x, axis, pairs)]
    concatenate x26 -> x0, other arithmetic: 5.18 us -> none  [the longest x14 4.77 us: conv_plain(): jnp.concatenate([slab[:, :, tap_w:tap_w + width] for tap_w in range(3)],...]
    mul x6 -> x0, other arithmetic: 3.11 us -> none  [the longest x1 1.52 us: per_device(): near = shifted(frames, 'span', 1) * keep[0]]
    ppermute x4, starting transfers between devices: 11.7 us -> 9.95 us  [shifted(): return lax.ppermute(x, axis, pairs)]
    unnamed x26 -> x20, local copies, waits for them, and re-layouts: 2.25 us -> 3.31 us
  transfers between devices with their start and end apart: 4 -> 4, of which waited for: 3 -> 3; matrix products, arithmetic and copies ran while one was open for 14% -> 0% of each run, Pallas kernels for 0% -> 9%
where the time goes in v2:
time: 35.9 us; the launch traced here: 35.5 us
  waiting for transfers between devices  14.1 us (39%)
  starting transfers between devices  9.95 us (28%)
  Pallas kernels  8.07 us (22%)
  local copies, waits for them, and re-layouts  3.31 us (9%)
    ppermute x4, waiting for transfers between devices, shifted(): return lax.ppermute(x, axis, pairs)  14.1 us
    ppermute x4, starting transfers between devices, shifted(): return lax.ppermute(x, axis, pairs)  9.95 us
    pallas_call x1, Pallas kernels, per_device(): kernel(forward_part, 'forward_part', [latent, latent, ((2, 6, 32, 2 * C),...  3.6 us
    unnamed x20, local copies, waits for them, and re-layouts  3.31 us
    pallas_call x1, Pallas kernels, per_device(): kernel(context_part, 'context_part', [latent, latent], [SMEM] * 2 + [VMEM...  2.65 us
    pallas_call x1, Pallas kernels, per_device(): kernel(finish, 'finish', [((2, 2, 8, 4 * C), BF)], [SMEM] * 2 + [VMEM] * 4)  1.19 us
  transfers between devices with their start and end apart: 4, of which 3 were waited for; matrix products, arithmetic and copies ran while one was open for 0% of the time, Pallas kernels for 9%

profile of v2, /device:TPU:14, one launch (start us, length us, event | category | flops | bytes accessed | tf_op | source)
XLA Modules:
  0.0 35.5 jit_solution(6831351894917045733)
XLA Ops:
  0.0 0.0 copy-start.3
  0.0 0.0 copy-start.2
  0.0 0.0 copy-start.8
  0.0 2.1 %collective-permute-start = (bf16[4,8,32,128]{3,2,1,0:T(8,128)(2,1)}, bf16[4,8,32,128]{3,2,1,0:T(8,128)(2,1)S(1)}, u32[]{:S(2)}, u32[]{:S(2)}) collective-permute-start(bf16[4,8,32,128]{3,2,1,0:T(8,128)(2,1)} %bitcast.8), channel_id=1, source_target_pairs={{0,4},{4,8},{8,12},{12,16},{16,20},{20,24},{24,28},{28,32},{32,36}... | collective-permute-start | bytes 786440 | tf_op jit(solution)/shard_map/ppermute | solution.py:18
  2.1 9.8 %collective-permute-done.near = bf16[4,8,32,128]{3,2,1,0:T(8,128)(2,1)S(1)} collective-permute-done((bf16[4,8,32,128]{3,2,1,0:T(8,128)(2,1)}, bf16[4,8,32,128]{3,2,1,0:T(8,128)(2,1)S(1)}, u32[]{:S(2)}, u32[]{:S(2)}) %collective-permute-start) | collective-permute-done | bytes 262176 | tf_op jit(solution)/shard_map/ppermute | solution.py:18
  11.9 0.0 copy-start
  11.9 0.9 %copy-done = bf16[1,4,8,32,128]{4,3,2,1,0:T(8,128)(2,1)S(1)} copy-done((bf16[1,4,8,32,128]{4,3,2,1,0:T(8,128)(2,1)S(1)}, bf16[1,4,8,32,128]{4,3,2,1,0:T(8,128)(2,1)}, u32[]{:S(2)}) %copy-start) | copy-done | bytes 262168
  12.8 0.0 copy-start.1
  12.8 0.0 copy-start.9
  12.9 3.6 %collective-permute-start.1 = (bf16[8,3,32,128]{3,2,1,0:T(8,128)(2,1)S(1)}, bf16[8,3,32,128]{3,2,1,0:T(8,128)(2,1)S(1)}, u32[]{:S(2)}, u32[]{:S(2)}) collective-permute-start(bf16[8,3,32,128]{3,2,1,0:T(8,128)(2,1)S(1)} %get-tuple-element.14), channel_id=1, source_target_pairs={{0,1},{1,2},{2,3},{4,5},{5,6},{6,7},{8,9},{9,10},{10,11},{12,13},{... | collective-permute-start | bytes 589832 | tf_op jit(solution)/shard_map/ppermute | solution.py:18
  16.5 2.4 %collective-permute-start.2 = (bf16[8,2,32,128]{3,2,1,0:T(8,128)(2,1)S(1)}, bf16[8,2,32,128]{3,2,1,0:T(8,128)(2,1)S(1)}, u32[]{:S(2)}, u32[]{:S(2)}) collective-permute-start(bf16[8,2,32,128]{3,2,1,0:T(8,128)(2,1)S(1)} %get-tuple-element.15), channel_id=1, source_target_pairs={{1,0},{2,1},{3,2},{5,4},{6,5},{7,6},{9,8},{10,9},{11,10},{13,12},{... | collective-permute-start | bytes 393224 | tf_op jit(solution)/shard_map/ppermute | solution.py:18
  18.8 0.0 copy-start.5
  18.9 1.2 %copy-done.5 = bf16[3,3,3,128,128]{4,3,2,1,0:T(8,128)(2,1)S(1)} copy-done((bf16[3,3,3,128,128]{4,3,2,1,0:T(8,128)(2,1)S(1)}, bf16[3,3,3,128,128]{4,3,2,1,0:T(8,128)(2,1)}, u32[]{:S(2)}) %copy-start.5) | copy-done | bytes 884760
  20.0 0.0 copy-start.6
  20.0 1.2 %copy-done.6 = bf16[3,3,3,128,128]{4,3,2,1,0:T(8,128)(2,1)S(1)} copy-done((bf16[3,3,3,128,128]{4,3,2,1,0:T(8,128)(2,1)S(1)}, bf16[3,3,3,128,128]{4,3,2,1,0:T(8,128)(2,1)}, u32[]{:S(2)}) %copy-start.6) | copy-done | bytes 884760
  21.2 0.0 copy-start.7
  21.2 0.6 %pack_weights.1 = (bf16[1536,768]{1,0:T(8,128)(2,1)S(1)}, bf16[1536,768]{1,0:T(8,128)(2,1)S(1)}) custom-call(bf16[27,128,128]{2,1,0:T(8,128)(2,1)S(1)} %bitcast.13, bf16[27,128,128]{2,1,0:T(8,128)(2,1)S(1)} %bitcast.14), custom_call_target="tpu_custom_call" | custom-call | flops 1073741824 | bytes 1048576 | tf_op jit(solution)/shard_map/pack_weights/pallas_call | solution.py:202
  21.8 1.5 %collective-permute-done.2.below = bf16[8,2,32,128]{3,2,1,0:T(8,128)(2,1)S(1)} collective-permute-done((bf16[8,2,32,128]{3,2,1,0:T(8,128)(2,1)S(1)}, bf16[8,2,32,128]{3,2,1,0:T(8,128)(2,1)S(1)}, u32[]{:S(2)}, u32[]{:S(2)}) %collective-permute-start.2) | collective-permute-done | bytes 131104 | tf_op jit(solution)/shard_map/ppermute | solution.py:18
  23.3 0.0 collective-permute-done.1.above
  23.3 0.0 copy-done.3
  23.3 0.0 copy-done.2
  23.3 0.0 copy-done.8
  23.4 0.0 copy-done.1
  23.4 0.0 copy-done.9
  23.4 0.0 copy-done.7
  23.4 3.6 %forward_part.1 = (f32[64,128]{1,0:T(8,128)S(1)}, f32[64,128]{1,0:T(8,128)S(1)}, bf16[2,6,32,256]{3,2,1,0:T(8,128)(2,1)S(1)}) custom-call(s32[16]{0:T(128)S(1)} %copy-done.2, s32[16]{0:T(128)S(1)} %copy-done.3, bf16[4,8,32,128]{3,2,1,0:T(8,128)(2,1)S(1)} %bitcast.10, bf16[4,8,32,128]{3,2,1,0:T(8,128)(2,1)S(1)} %collective-permute-done.near, ...), custom_call_target="tpu_custom_call" | custom-call | flops 3221225472 | bytes 1048576 | tf_op jit(solution)/shard_map/forward_part/pallas_call | solution.py:217
  27.0 1.9 %collective-permute-start.3 = (f32[64,128]{1,0:T(8,128)S(1)}, f32[64,128]{1,0:T(8,128)S(1)}, u32[]{:S(2)}, u32[]{:S(2)}) collective-permute-start(f32[64,128]{1,0:T(8,128)S(1)} %get-tuple-element.22), channel_id=1, source_target_pairs={{0,4},{4,8},{8,12},{12,16},{16,20},{20,24},{24,28},{28,32},{32,36}... | collective-permute-start | bytes 98312 | tf_op jit(solution)/shard_map/ppermute | solution.py:18
  28.9 0.0 copy-start.4
  28.9 2.6 %context_part.1 = (f32[64,128]{1,0:T(8,128)S(1)}, f32[64,128]{1,0:T(8,128)S(1)}) custom-call(s32[16]{0:T(128)S(1)} %copy-done.2, s32[16]{0:T(128)S(1)} %copy-done.3, bf16[4,8,32,128]{3,2,1,0:T(8,128)(2,1)S(1)} %bitcast.11, bf16[4,8,32,128]{3,2,1,0:T(8,128)(2,1)S(1)} %collective-permute-done.near, bf16[8,3,32,128]{3,2,1,0:T(8,128)(2,1)S(1)} %collective-permute-done.1.above, ...), custom_call_target="tpu_custom_call" | custom-call | flops 2147483648 | bytes 1048576 | tf_op jit(solution)/shard_map/context_part/pallas_call | solution.py:226
  31.6 2.7 %collective-permute-done.3.part = f32[64,128]{1,0:T(8,128)S(1)} collective-permute-done((f32[64,128]{1,0:T(8,128)S(1)}, f32[64,128]{1,0:T(8,128)S(1)}, u32[]{:S(2)}, u32[]{:S(2)}) %collective-permute-start.3) | collective-permute-done | bytes 32800 | tf_op jit(solution)/shard_map/ppermute | solution.py:18
  34.3 0.0 copy-done.4
  34.3 1.2 %finish.1 = bf16[2,2,8,512]{3,2,1,0:T(8,128)(2,1)} custom-call(s32[16]{0:T(128)S(1)} %copy-done.2, s32[16]{0:T(128)S(1)} %copy-done.3, f32[64,128]{1,0:T(8,128)S(1)} %get-tuple-element.20.early, f32[64,128]{1,0:T(8,128)S(1)} %get-tuple-element.21.late, f32[64,128]{1,0:T(8,128)S(1)} %collective-permute-done.3.part, f32[1,128]{1,0:T(1,128)S(1)} %bitcast.12), custom_call_target="tpu_custom_call" | custom-call | bytes 1048576 | tf_op jit(solution)/shard_map/finish/pallas_call | solution.py:234
  (1 shorter events, 0.0 us)
Async XLA Ops:
  0.0 23.3 %copy-start.3 = (s32[16]{0:T(128)S(1)}, s32[16]{0:T(128)}, u32[]{:S(2)}) copy-start(s32[16]{0:T(128)} %order.5) | copy-start | bytes 196
  0.0 23.3 %copy-start.2 = (s32[16]{0:T(128)S(1)}, s32[16]{0:T(128)}, u32[]{:S(2)}) copy-start(s32[16]{0:T(128)} %lengths.5) | copy-start | bytes 196
  0.0 23.3 %copy-start.8 = (f32[128]{0:T(128)S(1)}, f32[128]{0:T(128)}, u32[]{:S(2)}) copy-start(f32[128]{0:T(128)} %param.13) | copy-start | bytes 1540
  0.0 11.9 %collective-permute-start = (bf16[4,8,32,128]{3,2,1,0:T(8,128)(2,1)}, bf16[4,8,32,128]{3,2,1,0:T(8,128)(2,1)S(1)}, u32[]{:S(2)}, u32[]{:S(2)}) collective-permute-start(bf16[4,8,32,128]{3,2,1,0:T(8,128)(2,1)} %bitcast.8), channel_id=1, source_target_pairs={{0,4},{4,8},{8,12},{12,16},{16,20},{20,24},{24,28},{28,32},{32,36}... | collective-permute-start | bytes 786440 | tf_op jit(solution)/shard_map/ppermute | solution.py:18
  11.9 1.0 %copy-start = (bf16[1,4,8,32,128]{4,3,2,1,0:T(8,128)(2,1)S(1)}, bf16[1,4,8,32,128]{4,3,2,1,0:T(8,128)(2,1)}, u32[]{:S(2)}) copy-start(bf16[1,4,8,32,128]{4,3,2,1,0:T(8,128)(2,1)} %param.9) | copy-start | bytes 786436
  12.8 10.5 %copy-start.1 = (bf16[1,4,8,32,128]{4,3,2,1,0:T(8,128)(2,1)S(1)}, bf16[1,4,8,32,128]{4,3,2,1,0:T(8,128)(2,1)}, u32[]{:S(2)}) copy-start(bf16[1,4,8,32,128]{4,3,2,1,0:T(8,128)(2,1)} %param.9) | copy-start | bytes 786436
  12.8 10.5 %copy-start.9 = (f32[128]{0:T(128)S(1)}, f32[128]{0:T(128)}, u32[]{:S(2)}) copy-start(f32[128]{0:T(128)} %param.15) | copy-start | bytes 1540
  12.9 10.5 %collective-permute-start.1 = (bf16[8,3,32,128]{3,2,1,0:T(8,128)(2,1)S(1)}, bf16[8,3,32,128]{3,2,1,0:T(8,128)(2,1)S(1)}, u32[]{:S(2)}, u32[]{:S(2)}) collective-permute-start(bf16[8,3,32,128]{3,2,1,0:T(8,128)(2,1)S(1)} %get-tuple-element.14), channel_id=1, source_target_pairs={{0,1},{1,2},{2,3},{4,5},{5,6},{6,7},{8,9},{9,10},{10,11},{12,13},{... | collective-permute-start | bytes 589832 | tf_op jit(solution)/shard_map/ppermute | solution.py:18
  16.5 6.9 %collective-permute-start.2 = (bf16[8,2,32,128]{3,2,1,0:T(8,128)(2,1)S(1)}, bf16[8,2,32,128]{3,2,1,0:T(8,128)(2,1)S(1)}, u32[]{:S(2)}, u32[]{:S(2)}) collective-permute-start(bf16[8,2,32,128]{3,2,1,0:T(8,128)(2,1)S(1)} %get-tuple-element.15), channel_id=1, source_target_pairs={{1,0},{2,1},{3,2},{5,4},{6,5},{7,6},{9,8},{10,9},{11,10},{13,12},{... | collective-permute-start | bytes 393224 | tf_op jit(solution)/shard_map/ppermute | solution.py:18
  18.8 1.2 %copy-start.5 = (bf16[3,3,3,128,128]{4,3,2,1,0:T(8,128)(2,1)S(1)}, bf16[3,3,3,128,128]{4,3,2,1,0:T(8,128)(2,1)}, u32[]{:S(2)}) copy-start(bf16[3,3,3,128,128]{4,3,2,1,0:T(8,128)(2,1)} %param.12) | copy-start | bytes 2654212
  20.0 1.2 %copy-start.6 = (bf16[3,3,3,128,128]{4,3,2,1,0:T(8,128)(2,1)S(1)}, bf16[3,3,3,128,128]{4,3,2,1,0:T(8,128)(2,1)}, u32[]{:S(2)}) copy-start(bf16[3,3,3,128,128]{4,3,2,1,0:T(8,128)(2,1)} %param.14) | copy-start | bytes 2654212
  21.2 2.2 %copy-start.7 = (bf16[3,3,3,128,128]{4,3,2,1,0:T(8,128)(2,1)S(1)}, bf16[3,3,3,128,128]{4,3,2,1,0:T(8,128)(2,1)}, u32[]{:S(2)}) copy-start(bf16[3,3,3,128,128]{4,3,2,1,0:T(8,128)(2,1)} %param.16) | copy-start | bytes 2654212
  27.0 7.3 %collective-permute-start.3 = (f32[64,128]{1,0:T(8,128)S(1)}, f32[64,128]{1,0:T(8,128)S(1)}, u32[]{:S(2)}, u32[]{:S(2)}) collective-permute-start(f32[64,128]{1,0:T(8,128)S(1)} %get-tuple-element.22), channel_id=1, source_target_pairs={{0,4},{4,8},{8,12},{12,16},{16,20},{20,24},{24,28},{28,32},{32,36}... | collective-permute-start | bytes 98312 | tf_op jit(solution)/shard_map/ppermute | solution.py:18
  28.9 5.4 %copy-start.4 = (f32[128]{0:T(128)S(1)}, f32[128]{0:T(128)}, u32[]{:S(2)}) copy-start(f32[128]{0:T(128)} %param.17) | copy-start | bytes 1540

commit v3 on v1

v3 whole, which is shorter than its diff:
```python
import jax
import jax.numpy as jnp
from jax import lax
from jax.experimental import pallas as pl
from jax.experimental.pallas import tpu as pltpu
from jax.sharding import PartitionSpec as P

BF = jnp.bfloat16
F32 = jnp.float32
C = 128
VMEM = pl.BlockSpec(memory_space=pltpu.VMEM)
SMEM = pl.BlockSpec(memory_space=pltpu.SMEM)

EDGE_Q = (0, 1, 5)
EDGE_P = (0, 1, 4)


def shifted(x, axis, by):
    peers = lax.axis_size(axis)
    pairs = [(i, i + by) for i in range(peers) if 0 <= i + by < peers]
    return lax.ppermute(x, axis, pairs)


def continues(lengths, order, slot):
    begin = jnp.int32(0)
    first = jnp.int32(0)
    for k in range(order.shape[0]):
        first = jnp.where(begin == slot, jnp.int32(1), first)
        begin = begin + lengths[order[k]]
    return 1 - first


def prepare(lengths, order, own, a, b, pa, pb, pairs, flags):
    slot = lax.axis_index("span")
    block = lax.axis_index("row")
    values = (
        continues(lengths, order, slot),
        continues(lengths, order, slot + 1),
        (block > 0).astype(jnp.int32),
        (block < lax.axis_size("row") - 1).astype(jnp.int32),
    )
    for i, value in enumerate(values):
        flags[i] = jnp.full((8, C), value.astype(F32), F32)
    for src, dst in ((a, pa), (b, pb)):
        for t in range(3):
            for i in range(4):
                for w in range(3):
                    for j in range(2):
                        k = i - j
                        value = src[t * 9 + k * 3 + w] if 0 <= k <= 2 else jnp.zeros((C, C), BF)
                        dst[pl.ds((t * 4 + i) * C, C), pl.ds((w * 2 + j) * C, C)] = value
    for f in range(4):
        for row in range(8):
            pairs[f, row // 2, :, pl.ds(row % 2 * C, C)] = own[f, row]


def pack_halo(near, own, flags, up, down, pairs):
    keep = flags[0, 0:1, :].astype(BF)
    for f in range(4):
        for row in range(8):
            value = near[f, row] * keep
            pairs[f, row // 2, :, pl.ds(row % 2 * C, C)] = value
            if row >= 5:
                up[f, row - 5] = value
                up[4 + f, row - 5] = own[f, row // 2 , :, pl.ds(row % 2 * C, C)]
            if row < 2:
                down[f, row] = value
                down[4 + f, row] = own[f, row // 2, :, pl.ds(row % 2 * C, C)]


def twice(bias):
    return jnp.concatenate([bias[...], bias[...]], axis=1)


def conv(blocks, fetch, weight):
    rows = len(blocks) * 32
    lhs = jnp.concatenate(
        [
            jnp.concatenate([fetch(f - 2 + t, q + h) for f, q in blocks], axis=0)
            for t in range(3)
            for h in range(2)
        ],
        axis=1,
    )
    y = jnp.dot(lhs, weight[...], preferred_element_type=F32)
    col = lax.broadcasted_iota(jnp.int32, (rows, 2 * C), 0) % 32
    left = jnp.where(col == 0, 0.0, pltpu.roll(y[:, : 2 * C], 1, 0))
    right = jnp.where(col == 31, 0.0, pltpu.roll(y[:, 4 * C :], rows - 1, 0))
    return y[:, 2 * C : 4 * C] + left + right


def hidden_blocks(blocks, fetch, weight, bias, flags, put):
    v = conv(blocks, fetch, weight) + bias
    v = v / (1.0 + jnp.exp(-v))
    keep, top, bottom = (flags[i, 0:1, :] for i in (0, 2, 3))
    one = jnp.ones_like(top)
    for i, (f, q) in enumerate(blocks):
        value = v[i * 32 : i * 32 + 32]
        if q == 0:
            value = value * jnp.concatenate([top, top], axis=1)
        elif q == 1:
            value = value * jnp.concatenate([top, one], axis=1)
        elif q == 5:
            value = value * jnp.concatenate([one, bottom], axis=1)
        if f < 0:
            value = value * jnp.concatenate([keep, keep], axis=1)
        put(f, q, value.astype(BF))


def mixed_blocks(blocks, fetch, residual, weight, bias, top, put):
    v = conv(blocks, fetch, weight) + bias
    for i, (f, p) in enumerate(blocks):
        value = residual(f, p + 1).astype(F32) + v[i * 32 : i * 32 + 32]
        value = value.astype(BF).astype(F32)
        if p == 0:
            put(f, 0, value[:, C:] * top)
        else:
            put(f, 2 * p - 1, value[:, :C])
            put(f, 2 * p, value[:, C:])


def column_taps(row):
    m = [row[pl.ds(k, 8, stride=4), :] for k in range(4)]
    first = lax.broadcasted_iota(jnp.int32, (8, C), 0) == 0
    before = jnp.where(first, 0.0, pltpu.roll(m[3], 1, 0))
    columns = ((before, m[1]), (m[0], m[2]), (m[1], m[3]))
    return jnp.concatenate([jnp.concatenate(pair, axis=0).astype(BF) for pair in columns], axis=1)


def inner_part(near, own, wa, ba, wb, bb, flags, hidden, taps, m):
    def feature(f, g):
        return near[f + 4, g - 2] if f < 0 else own[f, g - 2]

    def put_hidden(f, q, value):
        hidden[f + 2, q - 2] = value

    def put_mixed(f, r, value):
        m[f, r - 3] = value

    for pair in range(3):
        frames = (2 * pair - 2, 2 * pair - 1)
        hidden_blocks([(f, q) for f in frames for q in (2, 3, 4)], feature, wa, twice(ba), flags, put_hidden)
    mixed_blocks(
        [(f, p) for f in range(4) for p in (2, 3)],
        lambda f, q: hidden[f + 2, q - 2],
        feature,
        wb,
        twice(bb),
        None,
        put_mixed,
    )
    for f in range(4):
        for r in range(4):
            taps[f, r] = column_taps(m.at[f, r])


def edge_part(frames, hidden_frames, near, own, above, below, wa, ba, wb, bb, flags, inner, taps, x, h, m, kept):
    for f in range(min(hidden_frames) - 2, max(frames) + 1):
        i = f + 4
        x[i, 0, :, :C] = jnp.zeros((32, C), BF)
        x[i, 0, :, C:] = above[i, 0]
        x[i, 1, :, :C] = above[i, 1]
        x[i, 1, :, C:] = above[i, 2]
        x[i, 2, :, :C] = below[i, 0]
        x[i, 2, :, C:] = below[i, 1]

    def feature(f, g):
        if 2 <= g <= 5:
            return near[f + 4, g - 2] if f < 0 else own[f, g - 2]
        return x[f + 4, 2 if g == 6 else g]

    def put_hidden(f, q, value):
        h[f + 2, EDGE_Q.index(q)] = value

    def hidden(f, q):
        if 2 <= q <= 4:
            return inner[f + 2, q - 2]
        e = EDGE_Q.index(q)
        return h[f + 2, e] if f in hidden_frames else kept[f, e]

    def put_mixed(f, r, value):
        m[f % 2, r if r < 3 else r - 4] = value

    for pair in range(0, len(hidden_frames), 2):
        blocks = [(f, q) for f in hidden_frames[pair : pair + 2] for q in EDGE_Q]
        hidden_blocks(blocks, feature, wa, twice(ba), flags, put_hidden)
    top = flags[2, 0:1, :]
    mixed_blocks([(f, p) for f in frames for p in EDGE_P], hidden, feature, wb, twice(bb), top, put_mixed)
    lhs = []
    for f in frames:
        rows = [column_taps(m.at[f % 2, r]) for r in range(3)]
        rows += [taps[f, r] for r in range(4)]
        rows += [column_taps(m.at[f % 2, r]) for r in range(3, 5)]
        lhs.append(
            jnp.concatenate(
                [jnp.concatenate([rows[2 * j + k] for k in range(3)], axis=1) for j in range(4)], axis=0
            )
        )
    return lhs


def down_dots(lhs, wd):
    n = 9 * C
    both = jnp.concatenate([wd[pl.ds(0, n), :], wd[pl.ds(2 * n, n), :]], axis=1)
    y = jnp.dot(lhs[0], both, preferred_element_type=F32)
    z = jnp.dot(lhs[1], wd[pl.ds(n, n), :], preferred_element_type=F32)
    return y[:, :C] + z, y[:, C:]


def tokens(v):
    return [
        jnp.concatenate(
            [v[(2 * i + a) * 16 + b * 8 : (2 * i + a) * 16 + b * 8 + 8] for a in range(2) for b in range(2)],
            axis=1,
        )
        for i in range(2)
    ]


def forward_part(
    near, own, above, below, wa, ba, wb, bb, wd, flags, inner, taps, part, late, kept, x, h, m
):
    lhs = edge_part(
        (2, 3), (0, 1, 2, 3), near, own, above, below, wa, ba, wb, bb, flags, inner, taps, x, h, m, None
    )
    for f in range(2):
        kept[f] = h[2 + f]
    first, last = down_dots(lhs, wd)
    for i, value in enumerate(tokens(first * flags[1, 0:1, :])):
        part[i] = value
    late[...] = last


def context_part(
    near, own, above, below, wa, ba, wb, bb, wd, bd, flags, inner, taps, late, kept, early, out, x, h, m
):
    lhs = edge_part(
        (0, 1), (-2, -1), near, own, above, below, wa, ba, wb, bb, flags, inner, taps, x, h, m, kept
    )
    first, last = down_dots(lhs, wd)
    for i, value in enumerate(tokens(last + bd[...])):
        early[i] = value
    for i, value in enumerate(tokens(late[...] + first + bd[...])):
        out[i] = value.astype(BF)


def kernel(body, outs, ins, scratch=(), flops=0):
    return pl.pallas_call(
        body,
        name=body.__name__,
        out_shape=[jax.ShapeDtypeStruct(*o) for o in outs],
        in_specs=ins,
        out_specs=[VMEM] * len(outs),
        scratch_shapes=list(scratch),
        compiler_params=pltpu.CompilerParams(vmem_limit_bytes=24 << 20),
        cost_estimate=pl.CostEstimate(flops=flops, bytes_accessed=1 << 20, transcendentals=0),
    )


def per_device(
    features, clip_lengths, clip_order, weight_a, bias_a, weight_b, bias_b, weight_down, bias_down
):
    wd = weight_down.reshape(27 * C, C)
    ba, bb, bd = (b.reshape(1, C) for b in (bias_a, bias_b, bias_down))
    near = shifted(features[0], "span", 1)
    packed = ((12 * C, 6 * C), BF)
    paired = ((4, 4, 32, 2 * C), BF)
    wa, wb, own, flags = kernel(
        prepare, [packed, packed, paired, ((4, 8, C), F32)], [SMEM] * 2 + [VMEM] * 3, flops=1 << 30
    )(clip_lengths, clip_order, features[0], weight_a.reshape(27, C, C), weight_b.reshape(27, C, C))
    up, down, near = kernel(
        pack_halo, [((8, 3, 32, C), BF), ((8, 2, 32, C), BF), paired], [VMEM] * 3
    )(near, own, flags)
    above = shifted(up, "row", 1)
    below = shifted(down, "row", -1)
    inner, taps = kernel(
        inner_part,
        [((6, 3, 32, 2 * C), BF), ((4, 4, 16, 3 * C), BF)],
        [VMEM] * 7,
        [pltpu.VMEM((4, 4, 32, C), F32)],
        flops=2 << 30,
    )(near, own, wa, ba, wb, bb, flags)
    scratch = [
        pltpu.VMEM((8, 3, 32, 2 * C), BF),
        pltpu.VMEM((6, 3, 32, 2 * C), BF),
        pltpu.VMEM((2, 5, 32, C), F32),
    ]
    token = ((2, 8, 4 * C), F32)
    part, late, kept = kernel(
        forward_part,
        [token, ((64, C), F32), ((2, 3, 32, 2 * C), BF)],
        [VMEM] * 12,
        scratch,
        flops=2 << 30,
    )(near, own, above, below, wa, ba, wb, bb, wd, flags, inner, taps)
    part = shifted(part, "span", 1)
    early, late = kernel(
        context_part, [token, (token[0], BF)], [VMEM] * 15, scratch, flops=2 << 30
    )(near, own, above, below, wa, ba, wb, bb, wd, bd, flags, inner, taps, late, kept)
    return jnp.stack([(early + part).astype(BF), late])[None]


def solution(mesh):
    placed = (P("span", None, "row", None, None), P(), P(), P(), P(), P(), P(), P(), P())
    return jax.shard_map(
        per_device,
        mesh=mesh,
        in_specs=placed,
        out_specs=P("span", None, "row", None, None),
        check_vma=False,
    )
```

time: 62.8 us -> 32.5 us (0.52); the launches traced: 61.6 us -> 31.9 us
  local copies, waits for them, and re-layouts: 18.6 us -> 4.6 us
  matrix products: 11.8 us -> 0 us
  other arithmetic: 10.3 us -> 0.63 us
  Pallas kernels: 0 us -> 7.68 us
  waiting for transfers between devices: 7.14 us -> 9.1 us
  starting transfers between devices: 11.7 us -> 9.8 us
  between operations: 2 us -> 0.12 us
    slice x40 -> x0, local copies, waits for them, and re-layouts: 15.6 us -> none  [the longest x5 7.39 us: conv_plain(): slab[:, :, tap_w:tap_w + width]]
    dot_general x27 -> x0, matrix products: 11.8 us -> none  [the longest x18 10.3 us: conv_plain(): jnp.dot(stacked.reshape(-1, 3 * chans), weight[tap_t, tap_h].reshape(3 *...]
    pallas_call x0 -> x5, Pallas kernels: none -> 7.68 us  [the longest x1 2.57 us: per_device(): kernel(inner_part, [((6, 3, 32, 2 * C), BF), ((4, 4, 16, 3 * C), BF)], [V...]
    concatenate x26 -> x0, other arithmetic: 5.18 us -> none  [the longest x14 4.77 us: conv_plain(): jnp.concatenate([slab[:, :, tap_w:tap_w + width] for tap_w in range(3)],...]
    mul x6 -> x0, other arithmetic: 3.11 us -> none  [the longest x1 1.52 us: per_device(): near = shifted(frames, 'span', 1) * keep[0]]
    unnamed x26 -> x18, local copies, waits for them, and re-layouts: 2.25 us -> 4.6 us
    ppermute x4, waiting for transfers between devices: 7.14 us -> 9.1 us  [shifted(): return lax.ppermute(x, axis, pairs)]
    ppermute x4, starting transfers between devices: 11.7 us -> 9.8 us  [shifted(): return lax.ppermute(x, axis, pairs)]
  transfers between devices with their start and end apart: 4 -> 4, of which waited for: 3 -> 3; matrix products, arithmetic and copies ran while one was open for 14% -> 0% of each run, Pallas kernels for 0% -> 17%
where the time goes in v3:
time: 32.5 us; the launch traced here: 31.9 us
  starting transfers between devices  9.8 us (30%)
  waiting for transfers between devices  9.1 us (28%)
  Pallas kernels  7.68 us (24%)
  local copies, waits for them, and re-layouts  4.6 us (14%)
  other arithmetic  0.63 us (2%)
    ppermute x4, starting transfers between devices, shifted(): return lax.ppermute(x, axis, pairs)  9.8 us
    ppermute x4, waiting for transfers between devices, shifted(): return lax.ppermute(x, axis, pairs)  9.1 us
    unnamed x18, local copies, waits for them, and re-layouts  4.6 us
    pallas_call x1, Pallas kernels, per_device(): kernel(inner_part, [((6, 3, 32, 2 * C), BF), ((4, 4, 16, 3 * C), BF)], [V...  2.57 us
    pallas_call x1, Pallas kernels, per_device(): kernel(forward_part, [token, ((64, C), F32), ((2, 3, 32, 2 * C), BF)], [V...  2.08 us
    pallas_call x1, Pallas kernels, per_device(): kernel(context_part, [token, (token[0], BF)], [VMEM] * 15, scratch, flops...  1.77 us
    pallas_call x1, Pallas kernels, per_device(): kernel(prepare, [packed, packed, paired, ((4, 8, C), F32)], [SMEM] * 2 +...  1.18 us
  transfers between devices with their start and end apart: 4, of which 3 were waited for; matrix products, arithmetic and copies ran while one was open for 0% of the time, Pallas kernels for 17%

profile of v3, /device:TPU:14, one launch (start us, length us, event | category | flops | bytes accessed | tf_op | source)
XLA Modules:
  0.0 31.9 jit_solution(16085823613783504971)
XLA Ops:
  0.0 0.0 copy-start.7
  0.0 0.0 copy-start.6
  0.0 2.0 %collective-permute-start = (bf16[4,8,32,128]{3,2,1,0:T(8,128)(2,1)}, bf16[4,8,32,128]{3,2,1,0:T(8,128)(2,1)S(1)}, u32[]{:S(2)}, u32[]{:S(2)}) collective-permute-start(bf16[4,8,32,128]{3,2,1,0:T(8,128)(2,1)} %bitcast.17), channel_id=1, source_target_pairs={{0,4},{4,8},{8,12},{12,16},{16,20},{20,24},{24,28},{28,32},{32,36}... | collective-permute-start | bytes 786440 | tf_op jit(solution)/shard_map/ppermute | solution.py:21
  2.1 0.0 copy-start
  2.1 1.2 %copy-done = bf16[3,3,3,128,128]{4,3,2,1,0:T(8,128)(2,1)S(1)} copy-done((bf16[3,3,3,128,128]{4,3,2,1,0:T(8,128)(2,1)S(1)}, bf16[3,3,3,128,128]{4,3,2,1,0:T(8,128)(2,1)}, u32[]{:S(2)}) %copy-start) | copy-done | bytes 884760
  3.2 0.0 copy-start.1
  3.2 1.2 %copy-done.1 = bf16[3,3,3,128,128]{4,3,2,1,0:T(8,128)(2,1)S(1)} copy-done((bf16[3,3,3,128,128]{4,3,2,1,0:T(8,128)(2,1)S(1)}, bf16[3,3,3,128,128]{4,3,2,1,0:T(8,128)(2,1)}, u32[]{:S(2)}) %copy-start.1) | copy-done | bytes 884760
  4.4 0.0 copy-start.3
  4.4 0.9 %copy-done.3 = bf16[1,4,8,32,128]{4,3,2,1,0:T(8,128)(2,1)S(1)} copy-done((bf16[1,4,8,32,128]{4,3,2,1,0:T(8,128)(2,1)S(1)}, bf16[1,4,8,32,128]{4,3,2,1,0:T(8,128)(2,1)}, u32[]{:S(2)}) %copy-start.3) | copy-done | bytes 262168
  5.3 0.0 copy-start.4
  5.3 0.7 %copy-done.4 = s32[16]{0:T(128)S(1)} copy-done((s32[16]{0:T(128)S(1)}, s32[16]{0:T(128)}, u32[]{:S(2)}) %copy-start.4) | copy-done | bytes 88
  6.0 0.0 copy-start.5
  6.0 0.7 %copy-done.5 = s32[16]{0:T(128)S(1)} copy-done((s32[16]{0:T(128)S(1)}, s32[16]{0:T(128)}, u32[]{:S(2)}) %copy-start.5) | copy-done | bytes 88
  6.7 1.2 %prepare.1 = (bf16[1536,768]{1,0:T(8,128)(2,1)S(1)}, bf16[1536,768]{1,0:T(8,128)(2,1)S(1)}, bf16[4,4,32,256]{3,2,1,0:T(8,128)(2,1)S(1)}, f32[4,8,128]{2,1,0:T(8,128)S(1)}) custom-call(s32[16]{0:T(128)S(1)} %copy-done.4, s32[16]{0:T(128)S(1)} %copy-done.5, bf16[4,8,32,128]{3,2,1,0:T(8,128)(2,1)S(1)} %bitcast.18, bf16[27,128,128]{2,1,0:T(8,128)(2,1)S(1)} %bitcast.13, ...), custom_call_target="tpu_custom_call" | custom-call | flops 1073741824 | bytes 1048576 | tf_op jit(solution)/shard_map/prepare/pallas_call | solution.py:268
  7.8 4.0 %collective-permute-done.near = bf16[4,8,32,128]{3,2,1,0:T(8,128)(2,1)S(1)} collective-permute-done((bf16[4,8,32,128]{3,2,1,0:T(8,128)(2,1)}, bf16[4,8,32,128]{3,2,1,0:T(8,128)(2,1)S(1)}, u32[]{:S(2)}, u32[]{:S(2)}) %collective-permute-start) | collective-permute-done | bytes 262176 | tf_op jit(solution)/shard_map/ppermute | solution.py:21
  11.9 0.1 pack_halo.1
  11.9 2.4 %collective-permute-start.2 = (bf16[8,2,32,128]{3,2,1,0:T(8,128)(2,1)S(1)}, bf16[8,2,32,128]{3,2,1,0:T(8,128)(2,1)S(1)}, u32[]{:S(2)}, u32[]{:S(2)}) collective-permute-start(bf16[8,2,32,128]{3,2,1,0:T(8,128)(2,1)S(1)} %get-tuple-element.23), channel_id=1, source_target_pairs={{1,0},{2,1},{3,2},{5,4},{6,5},{7,6},{9,8},{10,9},{11,10},{13,12},{... | collective-permute-start | bytes 393224 | tf_op jit(solution)/shard_map/ppermute | solution.py:21
  14.3 3.5 %collective-permute-start.1 = (bf16[8,3,32,128]{3,2,1,0:T(8,128)(2,1)S(1)}, bf16[8,3,32,128]{3,2,1,0:T(8,128)(2,1)S(1)}, u32[]{:S(2)}, u32[]{:S(2)}) collective-permute-start(bf16[8,3,32,128]{3,2,1,0:T(8,128)(2,1)S(1)} %get-tuple-element.22), channel_id=1, source_target_pairs={{0,1},{1,2},{2,3},{4,5},{5,6},{6,7},{8,9},{9,10},{10,11},{12,13},{... | collective-permute-start | bytes 589832 | tf_op jit(solution)/shard_map/ppermute | solution.py:21
  17.8 0.0 copy-done.7
  17.8 0.0 copy-done.6
  17.8 0.0 copy-start.2
  17.8 2.6 %inner_part.1 = (bf16[6,3,32,256]{3,2,1,0:T(8,128)(2,1)S(1)}, bf16[4,4,16,384]{3,2,1,0:T(8,128)(2,1)S(1)}) custom-call(bf16[4,4,32,256]{3,2,1,0:T(8,128)(2,1)S(1)} %get-tuple-element.21.near, bf16[4,4,32,256]{3,2,1,0:T(8,128)(2,1)S(1)} %get-tuple-element.19.own, bf16[1536,768]{1,0:T(8,128)(2,1)S(1)} %get-tuple-element.24.wa, f32[1,128]{1,0:T(1,128)S(1)} %bitcast.19, ...), custom_call_target="tpu_custom_call" | custom-call | flops 2147483648 | bytes 1048576 | tf_op jit(solution)/shard_map/inner_part/pallas_call | solution.py:276
  20.4 0.0 collective-permute-done.2.below
  20.4 1.5 %collective-permute-done.1.above = bf16[8,3,32,128]{3,2,1,0:T(8,128)(2,1)S(1)} collective-permute-done((bf16[8,3,32,128]{3,2,1,0:T(8,128)(2,1)S(1)}, bf16[8,3,32,128]{3,2,1,0:T(8,128)(2,1)S(1)}, u32[]{:S(2)}, u32[]{:S(2)}) %collective-permute-start.1) | collective-permute-done | bytes 196640 | tf_op jit(solution)/shard_map/ppermute | solution.py:21
  21.9 0.0 copy-done.2
  21.9 0.0 copy-start.8
  21.9 2.1 %forward_part.1 = (f32[2,8,512]{2,1,0:T(8,128)S(1)}, f32[64,128]{1,0:T(8,128)S(1)}, bf16[2,3,32,256]{3,2,1,0:T(8,128)(2,1)S(1)}) custom-call(bf16[4,4,32,256]{3,2,1,0:T(8,128)(2,1)S(1)} %get-tuple-element.21.near, bf16[4,4,32,256]{3,2,1,0:T(8,128)(2,1)S(1)} %get-tuple-element.19.own, bf16[8,3,32,128]{3,2,1,0:T(8,128)(2,1)S(1)} %collective-permute-done.1.above, ...), custom_call_target="tpu_custom_call" | custom-call | flops 2147483648 | bytes 1048576 | tf_op jit(solution)/shard_map/forward_part/pallas_call | solution.py:289
  24.0 1.9 %collective-permute-start.3 = (f32[2,8,512]{2,1,0:T(8,128)S(1)}, f32[2,8,512]{2,1,0:T(8,128)S(1)}, u32[]{:S(2)}, u32[]{:S(2)}) collective-permute-start(f32[2,8,512]{2,1,0:T(8,128)S(1)} %get-tuple-element.31), channel_id=1, source_target_pairs={{0,4},{4,8},{8,12},{12,16},{16,20},{20,24},{24,28},{28,32},{32,36}... | collective-permute-start | bytes 98312 | tf_op jit(solution)/shard_map/ppermute | solution.py:21
  25.9 0.0 copy-done.8
  25.9 1.8 %context_part.1 = (f32[2,8,512]{2,1,0:T(8,128)S(1)}, bf16[2,8,512]{2,1,0:T(8,128)(2,1)S(1)}) custom-call(bf16[4,4,32,256]{3,2,1,0:T(8,128)(2,1)S(1)} %get-tuple-element.21.near, bf16[4,4,32,256]{3,2,1,0:T(8,128)(2,1)S(1)} %get-tuple-element.19.own, bf16[8,3,32,128]{3,2,1,0:T(8,128)(2,1)S(1)} %collective-permute-done.1.above, ...), custom_call_target="tpu_custom_call" | custom-call | flops 2147483648 | bytes 1048576 | tf_op jit(solution)/shard_map/context_part/pallas_call | solution.py:297
  27.7 3.6 %collective-permute-done.3 = f32[2,8,512]{2,1,0:T(8,128)S(1)} collective-permute-done((f32[2,8,512]{2,1,0:T(8,128)S(1)}, f32[2,8,512]{2,1,0:T(8,128)S(1)}, u32[]{:S(2)}, u32[]{:S(2)}) %collective-permute-start.3) | collective-permute-done | bytes 32800 | tf_op jit(solution)/shard_map/ppermute | solution.py:21
  31.3 0.6 %maximum_bitcast_fusion = bf16[1,2,2,8,512]{4,3,2,1,0:T(8,128)(2,1)} fusion(bf16[1,2,8,512]{3,2,1,0:T(8,128)(2,1)S(1)} %bitcast.12, bf16[1,2,8,512]{3,2,1,0:T(8,128)(2,1)S(1)} %fusion), kind=kLoop, calls=%fused_computation | loop fusion | flops 16384 | bytes 65536 | tf_op jit(solution)/shard_map/broadcast_in_dim | solution.py:300
  (1 shorter events, 0.0 us)
Async XLA Ops:
  0.0 17.8 %copy-start.7 = (f32[128]{0:T(128)S(1)}, f32[128]{0:T(128)}, u32[]{:S(2)}) copy-start(f32[128]{0:T(128)} %param.15) | copy-start | bytes 1540
  0.0 17.8 %copy-start.6 = (f32[128]{0:T(128)S(1)}, f32[128]{0:T(128)}, u32[]{:S(2)}) copy-start(f32[128]{0:T(128)} %param.13) | copy-start | bytes 1540
  0.0 11.8 %collective-permute-start = (bf16[4,8,32,128]{3,2,1,0:T(8,128)(2,1)}, bf16[4,8,32,128]{3,2,1,0:T(8,128)(2,1)S(1)}, u32[]{:S(2)}, u32[]{:S(2)}) collective-permute-start(bf16[4,8,32,128]{3,2,1,0:T(8,128)(2,1)} %bitcast.17), channel_id=1, source_target_pairs={{0,4},{4,8},{8,12},{12,16},{16,20},{20,24},{24,28},{28,32},{32,36}... | collective-permute-start | bytes 786440 | tf_op jit(solution)/shard_map/ppermute | solution.py:21
  2.1 1.2 %copy-start = (bf16[3,3,3,128,128]{4,3,2,1,0:T(8,128)(2,1)S(1)}, bf16[3,3,3,128,128]{4,3,2,1,0:T(8,128)(2,1)}, u32[]{:S(2)}) copy-start(bf16[3,3,3,128,128]{4,3,2,1,0:T(8,128)(2,1)} %param.12) | copy-start | bytes 2654212
  3.2 1.2 %copy-start.1 = (bf16[3,3,3,128,128]{4,3,2,1,0:T(8,128)(2,1)S(1)}, bf16[3,3,3,128,128]{4,3,2,1,0:T(8,128)(2,1)}, u32[]{:S(2)}) copy-start(bf16[3,3,3,128,128]{4,3,2,1,0:T(8,128)(2,1)} %param.14) | copy-start | bytes 2654212
  4.4 0.9 %copy-start.3 = (bf16[1,4,8,32,128]{4,3,2,1,0:T(8,128)(2,1)S(1)}, bf16[1,4,8,32,128]{4,3,2,1,0:T(8,128)(2,1)}, u32[]{:S(2)}) copy-start(bf16[1,4,8,32,128]{4,3,2,1,0:T(8,128)(2,1)} %param.9) | copy-start | bytes 786436
  5.3 0.7 %copy-start.4 = (s32[16]{0:T(128)S(1)}, s32[16]{0:T(128)}, u32[]{:S(2)}) copy-start(s32[16]{0:T(128)} %lengths.1) | copy-start | bytes 196
  6.0 0.7 %copy-start.5 = (s32[16]{0:T(128)S(1)}, s32[16]{0:T(128)}, u32[]{:S(2)}) copy-start(s32[16]{0:T(128)} %order.1) | copy-start | bytes 196
  11.9 8.5 %collective-permute-start.2 = (bf16[8,2,32,128]{3,2,1,0:T(8,128)(2,1)S(1)}, bf16[8,2,32,128]{3,2,1,0:T(8,128)(2,1)S(1)}, u32[]{:S(2)}, u32[]{:S(2)}) collective-permute-start(bf16[8,2,32,128]{3,2,1,0:T(8,128)(2,1)S(1)} %get-tuple-element.23), channel_id=1, source_target_pairs={{1,0},{2,1},{3,2},{5,4},{6,5},{7,6},{9,8},{10,9},{11,10},{13,12},{... | collective-permute-start | bytes 393224 | tf_op jit(solution)/shard_map/ppermute | solution.py:21
  14.3 7.6 %collective-permute-start.1 = (bf16[8,3,32,128]{3,2,1,0:T(8,128)(2,1)S(1)}, bf16[8,3,32,128]{3,2,1,0:T(8,128)(2,1)S(1)}, u32[]{:S(2)}, u32[]{:S(2)}) collective-permute-start(bf16[8,3,32,128]{3,2,1,0:T(8,128)(2,1)S(1)} %get-tuple-element.22), channel_id=1, source_target_pairs={{0,1},{1,2},{2,3},{4,5},{5,6},{6,7},{8,9},{9,10},{10,11},{12,13},{... | collective-permute-start | bytes 589832 | tf_op jit(solution)/shard_map/ppermute | solution.py:21
  17.8 4.1 %copy-start.2 = (bf16[3,3,3,128,128]{4,3,2,1,0:T(8,128)(2,1)S(1)}, bf16[3,3,3,128,128]{4,3,2,1,0:T(8,128)(2,1)}, u32[]{:S(2)}) copy-start(bf16[3,3,3,128,128]{4,3,2,1,0:T(8,128)(2,1)} %param.16) | copy-start | bytes 2654212
  21.9 4.0 %copy-start.8 = (f32[128]{0:T(128)S(1)}, f32[128]{0:T(128)}, u32[]{:S(2)}) copy-start(f32[128]{0:T(128)} %param.17) | copy-start | bytes 1540
  24.0 7.3 %collective-permute-start.3 = (f32[2,8,512]{2,1,0:T(8,128)S(1)}, f32[2,8,512]{2,1,0:T(8,128)S(1)}, u32[]{:S(2)}, u32[]{:S(2)}) collective-permute-start(f32[2,8,512]{2,1,0:T(8,128)S(1)} %get-tuple-element.31), channel_id=1, source_target_pairs={{0,4},{4,8},{8,12},{12,16},{16,20},{20,24},{24,28},{28,32},{32,36}... | collective-permute-start | bytes 98312 | tf_op jit(solution)/shard_map/ppermute | solution.py:21

commit v4 on v3

v4 whole, which is shorter than its diff:
```python
import jax
import jax.numpy as jnp
from jax import lax
from jax.experimental import pallas as pl
from jax.experimental.pallas import tpu as pltpu
from jax.sharding import PartitionSpec as P

BF = jnp.bfloat16
F32 = jnp.float32
C = 128
VMEM = pl.BlockSpec(memory_space=pltpu.VMEM)
HBM = pl.BlockSpec(memory_space=pltpu.HBM)


def shifted(x, axis, by):
    peers = lax.axis_size(axis)
    pairs = [(i, i + by) for i in range(peers) if 0 <= i + by < peers]
    return lax.ppermute(x, axis, pairs)


def continues(lengths, order, slot):
    begin = jnp.int32(0)
    first = jnp.int32(0)
    for k in range(16):
        first = jnp.where(begin == slot, jnp.int32(1), first)
        begin = begin + lengths[order[k]]
    return 1 - first


def last_frames(features, out, sem):
    copy = pltpu.make_async_copy(features.at[pl.ds(2, 2)], out, sem)
    copy.start()
    copy.wait()


def prepare(lengths, order, features, a, b, pa, pb, pairs, flags, smem, own, taps, sem):
    copies = [
        pltpu.make_async_copy(lengths, smem.at[0], sem.at[0]),
        pltpu.make_async_copy(order, smem.at[1], sem.at[1]),
        pltpu.make_async_copy(features.at[pl.ds(0, 3)], own, sem.at[2]),
    ]
    for i, src in enumerate((a, b)):
        for t in range(3):
            part = pl.ds(9 * t, 9)
            copies.append(pltpu.make_async_copy(src.at[part], taps.at[i, part], sem.at[3 + 3 * i + t]))
    for copy in copies:
        copy.start()
    for copy in copies[:3]:
        copy.wait()
    slot = lax.axis_index("span")
    block = lax.axis_index("row")
    values = (
        continues(smem.at[0], smem.at[1], slot),
        continues(smem.at[0], smem.at[1], slot - 1),
        (block > 0).astype(jnp.int32),
        (block < lax.axis_size("row") - 1).astype(jnp.int32),
    )
    for i, value in enumerate(values):
        flags[i] = jnp.full((8, C), value.astype(F32), F32)
    for f in range(3):
        for row in range(8):
            pairs[f, row // 2, :, pl.ds(row % 2 * C, C)] = own[f, row]
    for n, dst in enumerate((pa, pb)):
        for t in range(3):
            copies[3 + 3 * n + t].wait()
            for i in range(4):
                for w in range(3):
                    for j in range(2):
                        k = i - j
                        value = taps[n, t * 9 + k * 3 + w] if 0 <= k <= 2 else jnp.zeros((C, C), BF)
                        dst[pl.ds((t * 4 + i) * C, C), pl.ds((w * 2 + j) * C, C)] = value


def pack_up(far, near, own, flags, after, up, pairs):
    both = (flags[0, 0:1, :] * flags[1, 0:1, :]).astype(BF)
    for f in range(2):
        for row in range(8):
            value = far[f, row] * both
            pairs[f, row // 2, :, pl.ds(row % 2 * C, C)] = value
            if row >= 5:
                up[f, row - 5] = value
    for f in range(7):
        for row in range(5, 8):
            lanes = pl.ds(row % 2 * C, C)
            up[2 + f, row - 5] = near[f, row // 2, :, lanes] if f < 4 else own[f - 4, row // 2, :, lanes]


def pack_down(far, near, own, after, down):
    for f in range(9):
        for row in range(2):
            src, at = (far, f) if f < 2 else (near, f - 2) if f < 6 else (own, f - 6)
            down[f, row] = src[at, 0, :, pl.ds(row * C, C)]


def twice(bias):
    return jnp.concatenate([bias[...], bias[...]], axis=1)


def conv(blocks, fetch, weight):
    rows = len(blocks) * 32
    lhs = jnp.concatenate(
        [
            jnp.concatenate([fetch(f - 2 + t, q + h) for f, q in blocks], axis=0)
            for t in range(3)
            for h in range(2)
        ],
        axis=1,
    )
    y = jnp.dot(lhs, weight[...], preferred_element_type=F32)
    col = lax.broadcasted_iota(jnp.int32, (rows, 2 * C), 0) % 32
    left = jnp.where(col == 0, 0.0, pltpu.roll(y[:, : 2 * C], 1, 0))
    right = jnp.where(col == 31, 0.0, pltpu.roll(y[:, 4 * C :], rows - 1, 0))
    return y[:, 2 * C : 4 * C] + left + right


def hidden_blocks(blocks, fetch, weight, bias, flags, put):
    v = conv(blocks, fetch, weight) + bias
    v = v / (1.0 + jnp.exp(-v))
    keep, top, bottom = (flags[i, 0:1, :] for i in (0, 2, 3))
    one = jnp.ones_like(top)
    for i, (f, q) in enumerate(blocks):
        value = v[i * 32 : i * 32 + 32]
        if q == 0:
            value = value * jnp.concatenate([top, top], axis=1)
        elif q == 1:
            value = value * jnp.concatenate([top, one], axis=1)
        elif q == 5:
            value = value * jnp.concatenate([one, bottom], axis=1)
        if f < 0:
            value = value * jnp.concatenate([keep, keep], axis=1)
        put(f, q, value.astype(BF))


def mixed_blocks(blocks, fetch, residual, weight, bias, flags, put):
    v = conv(blocks, fetch, weight) + bias
    keep, top = flags[0, 0:1, :], flags[2, 0:1, :]
    for i, (f, p) in enumerate(blocks):
        value = residual(f, p + 1).astype(F32) + v[i * 32 : i * 32 + 32]
        value = value.astype(BF).astype(F32)
        if f < 0:
            value = value * jnp.concatenate([keep, keep], axis=1)
        if p == 0:
            put(f, 0, value[:, C:] * top)
        else:
            put(f, 2 * p - 1, value[:, :C])
            put(f, 2 * p, value[:, C:])


def column_taps(row):
    m = [row[pl.ds(k, 8, stride=4), :] for k in range(4)]
    first = lax.broadcasted_iota(jnp.int32, (8, C), 0) == 0
    before = jnp.where(first, 0.0, pltpu.roll(m[3], 1, 0))
    columns = ((before, m[1]), (m[0], m[2]), (m[1], m[3]))
    return jnp.concatenate([jnp.concatenate(pair, axis=0).astype(BF) for pair in columns], axis=1)


def own_feature(far, near, own):
    def feature(f, g):
        src, at = (far, f + 6) if f < -4 else (near, f + 4) if f < 0 else (own, f)
        return src[at, g - 2]

    return feature


def inner_near(arrived, own, wa, ba, wb, bb, flags, near, hidden, taps, m):
    keep = flags[0, 0:1, :].astype(BF)
    for f in range(4):
        for row in range(8):
            near[f, row // 2, :, pl.ds(row % 2 * C, C)] = arrived[f, row] * keep
    feature = own_feature(None, near, own)

    def put_hidden(f, q, value):
        hidden[f + 2, q - 2] = value

    def put_mixed(f, r, value):
        m[f, r - 3] = value

    for frames in ((-2, -1), (0, 1, 2)):
        hidden_blocks([(f, q) for f in frames for q in (2, 3, 4)], feature, wa, twice(ba), flags, put_hidden)
    blocks = [(f, p) for f in range(3) for p in (2, 3)]
    mixed_blocks(blocks, lambda f, q: hidden[f + 2, q - 2], feature, wb, twice(bb), flags, put_mixed)
    for f in range(3):
        for r in range(4):
            taps[f, r] = column_taps(m.at[f, r])


def inner_far(far, near, wa, ba, flags, hidden):
    def put_hidden(f, q, value):
        hidden[f + 4, q - 2] = value

    blocks = [(f, q) for f in (-4, -3) for q in (2, 3, 4)]
    hidden_blocks(blocks, own_feature(far, near, None), wa, twice(ba), flags, put_hidden)


def inner_mixed(near, wb, bb, flags, hidden_far, hidden_near, taps, m):
    def hidden(f, q):
        return hidden_far[f + 4, q - 2] if f < -2 else hidden_near[f + 2, q - 2]

    def put_mixed(f, r, value):
        m[f + 2, r - 3] = value

    blocks = [(f, p) for f in (-2, -1) for p in (2, 3)]
    mixed_blocks(blocks, hidden, own_feature(None, near, None), wb, twice(bb), flags, put_mixed)
    for f in range(2):
        for r in range(4):
            taps[f, r] = column_taps(m.at[f, r])


def edge(far, near, own, wa, ba, wb, bb, flags, hidden_far, hidden_near, h, m, halo, q_edge, p_edge, row):
    def feature(f, g):
        return own_feature(far, near, own)(f, g) if 2 <= g <= 5 else halo(f + 6, g)

    def put_hidden(f, q, value):
        h[f + 4, q_edge.index(q)] = value

    def hidden(f, q):
        if 2 <= q <= 4:
            return hidden_far[f + 4, q - 2] if f < -2 else hidden_near[f + 2, q - 2]
        return h[f + 4, q_edge.index(q)]

    def put_mixed(f, r, value):
        m[f + 2, r - row] = value

    split = ((-4, -3, -2), (-1, 0, 1, 2)) if len(q_edge) > 1 else (range(-4, 3),)
    for frames in split:
        hidden_blocks([(f, q) for f in frames for q in q_edge], feature, wa, twice(ba), flags, put_hidden)
    mixed_blocks([(f, p) for f in range(-2, 3) for p in p_edge], hidden, feature, wb, twice(bb), flags, put_mixed)


def top_part(far, near, own, above, wa, ba, wb, bb, flags, hidden_far, hidden_near, taps, h, m):
    def halo(i, g):
        upper = jnp.zeros((32, C), BF) if g == 0 else above[i, 1]
        return jnp.concatenate([upper, above[i, 2 * g]], axis=1)

    edge(far, near, own, wa, ba, wb, bb, flags, hidden_far, hidden_near, h, m, halo, (0, 1), (0, 1), 0)
    for f in range(5):
        for r in range(3):
            taps[f, r] = column_taps(m.at[f, r])


def bottom_part(
    far, near, own, below, wa, ba, wb, bb, wd, bd, flags, hidden_far, hidden_near, top_taps, taps_far, taps_near, out, h, m
):
    def halo(i, g):
        return jnp.concatenate([below[i, 0], below[i, 1]], axis=1)

    edge(far, near, own, wa, ba, wb, bb, flags, hidden_far, hidden_near, h, m, halo, (5,), (4,), 7)
    frames = []
    for f in range(5):
        rows = [top_taps[f, r] for r in range(3)] + [taps_far[f, r] if f < 2 else taps_near[f - 2, r] for r in range(4)]
        rows += [column_taps(m.at[f, r]) for r in range(2)]
        frames.append(
            jnp.concatenate(
                [jnp.concatenate([rows[2 * j + k] for k in range(3)], axis=1) for j in range(4)], axis=0
            )
        )
    lhs = jnp.concatenate([jnp.concatenate(frames[t : t + 3], axis=1) for t in (0, 2)], axis=0)
    v = jnp.dot(lhs, wd[...], preferred_element_type=F32) + bd[...]
    v = v.astype(BF).astype(F32)
    for t in range(2):
        for i in range(2):
            at = t * 64 + i * 32
            out[t, i] = jnp.concatenate([v[at + k * 8 : at + k * 8 + 8] for k in range(4)], axis=1).astype(BF)


def kernel(body, outs, ins, scratch=(), flops=0):
    return pl.pallas_call(
        body,
        name=body.__name__,
        out_shape=[jax.ShapeDtypeStruct(*o) for o in outs],
        in_specs=ins,
        out_specs=[VMEM] * len(outs),
        scratch_shapes=list(scratch),
        compiler_params=pltpu.CompilerParams(vmem_limit_bytes=24 << 20),
        cost_estimate=pl.CostEstimate(flops=flops, bytes_accessed=1 << 10, transcendentals=0),
    )


def per_device(
    features, clip_lengths, clip_order, weight_a, bias_a, weight_b, bias_b, weight_down, bias_down
):
    wd = weight_down.reshape(27 * C, C)
    ba, bb, bd = (b.reshape(1, C) for b in (bias_a, bias_b, bias_down))
    near = shifted(features[0], "span", 1)
    taps_a, taps_b = (w.reshape(27, C, C) for w in (weight_a, weight_b))
    stay = [
        pltpu.with_memory_space_constraint(x, pltpu.HBM)
        for x in (clip_lengths, clip_order, features[0], taps_a, taps_b)
    ]
    (tail,) = kernel(
        last_frames,
        [((2, 8, 32, C), BF)],
        [HBM],
        [pltpu.SemaphoreType.DMA],
    )(stay[2])
    far = shifted(tail, "span", 2)
    packed = ((12 * C, 6 * C), BF)
    wa, wb, own, flags = kernel(
        prepare,
        [packed, packed, ((3, 4, 32, 2 * C), BF), ((4, 8, C), F32)],
        [HBM] * 5,
        [
            pltpu.SMEM((2, 16), jnp.int32),
            pltpu.VMEM((3, 8, 32, C), BF),
            pltpu.VMEM((2, 27, C, C), BF),
            pltpu.SemaphoreType.DMA((9,)),
        ],
    )(*stay)
    near, hidden_near, taps_near = kernel(
        inner_near,
        [((4, 4, 32, 2 * C), BF), ((5, 3, 32, 2 * C), BF), ((3, 4, 16, 3 * C), BF)],
        [VMEM] * 7,
        [pltpu.VMEM((3, 4, 32, C), F32)],
    )(near, own, wa, ba, wb, bb, flags)
    up, far = kernel(
        pack_up, [((9, 3, 32, C), BF), ((2, 4, 32, 2 * C), BF)], [VMEM] * 5
    )(far, near, own, flags, taps_near)
    above = shifted(up, "row", 1)
    (hidden_far,) = kernel(inner_far, [((2, 3, 32, 2 * C), BF)], [VMEM] * 5)(far, near, wa, ba, flags)
    (down,) = kernel(pack_down, [((9, 2, 32, C), BF)], [VMEM] * 4)(far, near, own, hidden_far)
    below = shifted(down, "row", -1)
    (taps_far,) = kernel(
        inner_mixed, [((2, 4, 16, 3 * C), BF)], [VMEM] * 6, [pltpu.VMEM((2, 4, 32, C), F32)]
    )(near, wb, bb, flags, hidden_far, hidden_near)
    (top_taps,) = kernel(
        top_part,
        [((5, 3, 16, 3 * C), BF)],
        [VMEM] * 11,
        [pltpu.VMEM((7, 2, 32, 2 * C), BF), pltpu.VMEM((5, 3, 32, C), F32)],
    )(far, near, own, above, wa, ba, wb, bb, flags, hidden_far, hidden_near)
    (out,) = kernel(
        bottom_part,
        [((2, 2, 8, 4 * C), BF)],
        [VMEM] * 16,
        [pltpu.VMEM((7, 1, 32, 2 * C), BF), pltpu.VMEM((5, 2, 32, C), F32)],
    )(
        far, near, own, below, wa, ba, wb, bb, wd, bd, flags, hidden_far, hidden_near, top_taps, taps_far, taps_near
    )
    return out[None]


def solution(mesh):
    placed = (P("span", None, "row", None, None), P(), P(), P(), P(), P(), P(), P(), P())
    return jax.shard_map(
        per_device,
        mesh=mesh,
        in_specs=placed,
        out_specs=P("span", None, "row", None, None),
        check_vma=False,
    )
```

time: 32.5 us -> 28.7 us (0.88)
  local copies, waits for them, and re-layouts: 4.6 us -> 0.02 us
  waiting for transfers between devices: 9.1 us -> 5.68 us
  Pallas kernels: 7.68 us -> 10.9 us
  starting transfers between devices: 9.8 us -> 11.7 us
  other arithmetic: 0.63 us -> 0 us
    unnamed x18 -> x8, local copies, waits for them, and re-layouts: 4.6 us -> 0.02 us
    ppermute x4, waiting for transfers between devices: 9.1 us -> 5.68 us  [shifted(): return lax.ppermute(x, axis, pairs)]
    pallas_call x5 -> x9, Pallas kernels: 7.68 us -> 10.9 us  [the longest x1 2.45 us: per_device(): kernel(bottom_part, [((2, 2, 8, 4 * C), BF)], [VMEM] * 16, [pltpu.VMEM((7...]
    ppermute x4, starting transfers between devices: 9.8 us -> 11.7 us  [shifted(): return lax.ppermute(x, axis, pairs)]
    broadcast_in_dim x1 -> x0, other arithmetic: 0.62 us -> none  [per_device(): return jnp.stack([(early + part).astype(BF), late])[None]]
  transfers between devices with their start and end apart: 4 -> 4, of which waited for: 3 -> 4; matrix products, arithmetic and copies ran while one was open for 0% -> 0% of each run, Pallas kernels for 17% -> 30%
where the time goes in v4:
time: 28.7 us; the launch traced here: 28.4 us
  starting transfers between devices  11.7 us (41%)
  Pallas kernels  10.9 us (38%)
  waiting for transfers between devices  5.68 us (20%)
    ppermute x4, starting transfers between devices, shifted(): return lax.ppermute(x, axis, pairs)  11.7 us
    ppermute x4, waiting for transfers between devices, shifted(): return lax.ppermute(x, axis, pairs)  5.68 us
    pallas_call x1, Pallas kernels, per_device(): kernel(bottom_part, [((2, 2, 8, 4 * C), BF)], [VMEM] * 16, [pltpu.VMEM((7...  2.45 us
    pallas_call x1, Pallas kernels, per_device(): kernel(top_part, [((5, 3, 16, 3 * C), BF)], [VMEM] * 11, [pltpu.VMEM((7,...  2.29 us
    pallas_call x1, Pallas kernels, per_device(): kernel(inner_near, [((4, 4, 32, 2 * C), BF), ((5, 3, 32, 2 * C), BF), ((3...  2.21 us
    pallas_call x1, Pallas kernels, per_device(): kernel(prepare, [packed, packed, ((3, 4, 32, 2 * C), BF), ((4, 8, C), F32...  1.77 us
    pallas_call x1, Pallas kernels, per_device(): kernel(last_frames, [((2, 8, 32, C), BF)], [HBM], [pltpu.SemaphoreType.DMA])  0.92 us
    pallas_call x1, Pallas kernels, per_device(): kernel(inner_far, [((2, 3, 32, 2 * C), BF)], [VMEM] * 5)  0.69 us
  transfers between devices with their start and end apart: 4, of which 4 were waited for; matrix products, arithmetic and copies ran while one was open for 0% of the time, Pallas kernels for 30%

profile of v4, /device:TPU:14, one launch (start us, length us, event | category | flops | bytes accessed | tf_op | source)
XLA Modules:
  0.0 28.4 jit_solution(18396862760966972563)
XLA Ops:
  0.0 0.0 copy-start.1
  0.0 0.0 copy-start.2
  0.0 2.0 %collective-permute-start.1 = (bf16[4,8,32,128]{3,2,1,0:T(8,128)(2,1)}, bf16[4,8,32,128]{3,2,1,0:T(8,128)(2,1)S(1)}, u32[]{:S(2)}, u32[]{:S(2)}) collective-permute-start(bf16[4,8,32,128]{3,2,1,0:T(8,128)(2,1)} %bitcast.18), channel_id=1, source_target_pairs={{0,4},{4,8},{8,12},{12,16},{16,20},{20,24},{24,28},{28,32},{32,36}... | collective-permute-start | bytes 786440 | tf_op jit(solution)/shard_map/ppermute | solution.py:18
  2.1 0.9 %last_frames.1 = bf16[2,8,32,128]{3,2,1,0:T(8,128)(2,1)S(1)} custom-call(bf16[4,8,32,128]{3,2,1,0:T(8,128)(2,1)} %bitcast.19), custom_call_target="tpu_custom_call" | custom-call | bytes 1024 | tf_op jit(solution)/shard_map/last_frames/pallas_call | solution.py:290
  3.0 3.8 %collective-permute-start = (bf16[2,8,32,128]{3,2,1,0:T(8,128)(2,1)S(1)}, bf16[2,8,32,128]{3,2,1,0:T(8,128)(2,1)S(1)}, u32[]{:S(2)}, u32[]{:S(2)}) collective-permute-start(bf16[2,8,32,128]{3,2,1,0:T(8,128)(2,1)S(1)} %last_frames.1), channel_id=1, source_target_pairs={{0,8},{4,12},{8,16},{12,20},{16,24},{20,28},{24,32},{28,36},{32,40... | collective-permute-start | bytes 393224 | tf_op jit(solution)/shard_map/ppermute | solution.py:18
  6.8 1.8 %prepare.1 = (bf16[1536,768]{1,0:T(8,128)(2,1)S(1)}, bf16[1536,768]{1,0:T(8,128)(2,1)S(1)}, bf16[3,4,32,256]{3,2,1,0:T(8,128)(2,1)S(1)}, f32[4,8,128]{2,1,0:T(8,128)S(1)}) custom-call(s32[16]{0:T(128)} %lengths.1, s32[16]{0:T(128)} %order.1, bf16[4,8,32,128]{3,2,1,0:T(8,128)(2,1)} %bitcast.20, bf16[27,128,128]{2,1,0:T(8,128)(2,1)} %bitcast.21, ...), custom_call_target="tpu_custom_call" | custom-call | bytes 1024 | tf_op jit(solution)/shard_map/prepare/pallas_call | solution.py:298
  8.6 3.3 %collective-permute-done.1.arrived = bf16[4,8,32,128]{3,2,1,0:T(8,128)(2,1)S(1)} collective-permute-done((bf16[4,8,32,128]{3,2,1,0:T(8,128)(2,1)}, bf16[4,8,32,128]{3,2,1,0:T(8,128)(2,1)S(1)}, u32[]{:S(2)}, u32[]{:S(2)}) %collective-permute-start.1) | collective-permute-done | bytes 262176 | tf_op jit(solution)/shard_map/ppermute | solution.py:18
  11.9 0.0 copy-done.1
  11.9 0.0 copy-done.2
  11.9 2.2 %inner_near.1 = (bf16[4,4,32,256]{3,2,1,0:T(8,128)(2,1)S(1)}, bf16[5,3,32,256]{3,2,1,0:T(8,128)(2,1)S(1)}, bf16[3,4,16,384]{3,2,1,0:T(8,128)(2,1)S(1)}) custom-call(bf16[4,8,32,128]{3,2,1,0:T(8,128)(2,1)S(1)} %collective-permute-done.1.arrived, bf16[3,4,32,256]{3,2,1,0:T(8,128)(2,1)S(1)} %get-tuple-element.14.own, ...), custom_call_target="tpu_custom_call" | custom-call | bytes 1024 | tf_op jit(solution)/shard_map/inner_near/pallas_call | solution.py:309
  14.1 0.6 %collective-permute-done.far = bf16[2,8,32,128]{3,2,1,0:T(8,128)(2,1)S(1)} collective-permute-done((bf16[2,8,32,128]{3,2,1,0:T(8,128)(2,1)S(1)}, bf16[2,8,32,128]{3,2,1,0:T(8,128)(2,1)S(1)}, u32[]{:S(2)}, u32[]{:S(2)}) %collective-permute-start) | collective-permute-done | bytes 131104 | tf_op jit(solution)/shard_map/ppermute | solution.py:18
  14.7 0.1 pack_up.1
  14.7 3.5 %collective-permute-start.3 = (bf16[9,3,32,128]{3,2,1,0:T(8,128)(2,1)S(1)}, bf16[9,3,32,128]{3,2,1,0:T(8,128)(2,1)S(1)}, u32[]{:S(2)}, u32[]{:S(2)}) collective-permute-start(bf16[9,3,32,128]{3,2,1,0:T(8,128)(2,1)S(1)} %get-tuple-element.22), channel_id=1, source_target_pairs={{0,1},{1,2},{2,3},{4,5},{5,6},{6,7},{8,9},{9,10},{10,11},{12,13},{... | collective-permute-start | bytes 663560 | tf_op jit(solution)/shard_map/ppermute | solution.py:18
  18.2 0.7 %inner_far.1.after.hidden_far = bf16[2,3,32,256]{3,2,1,0:T(8,128)(2,1)S(1)} custom-call(bf16[2,4,32,256]{3,2,1,0:T(8,128)(2,1)S(1)} %get-tuple-element.20.far, bf16[4,4,32,256]{3,2,1,0:T(8,128)(2,1)S(1)} %get-tuple-element.18.near, bf16[1536,768]{1,0:T(8,128)(2,1)S(1)} %get-tuple-element.15.wa, f32[1,128]{1,0:T(1,128)S(1)} %bitcast.10, ...), custom_call_target="tpu_custom_call" | custom-call | bytes 1024 | tf_op jit(solution)/shard_map/inner_far/pallas_call | solution.py:319
  18.9 2.4 %collective-permute-start.2 = (bf16[9,2,32,128]{3,2,1,0:T(8,128)(2,1)S(1)}, bf16[9,2,32,128]{3,2,1,0:T(8,128)(2,1)S(1)}, u32[]{:S(2)}, u32[]{:S(2)}) collective-permute-start(bf16[9,2,32,128]{3,2,1,0:T(8,128)(2,1)S(1)} %pack_down.1), channel_id=1, source_target_pairs={{1,0},{2,1},{3,2},{5,4},{6,5},{7,6},{9,8},{10,9},{11,10},{13,12},{... | collective-permute-start | bytes 442376 | tf_op jit(solution)/shard_map/ppermute | solution.py:18
  21.3 0.5 %inner_mixed.1.taps_far = bf16[2,4,16,384]{3,2,1,0:T(8,128)(2,1)S(1)} custom-call(bf16[4,4,32,256]{3,2,1,0:T(8,128)(2,1)S(1)} %get-tuple-element.18.near, bf16[1536,768]{1,0:T(8,128)(2,1)S(1)} %get-tuple-element.16.wb, f32[1,128]{1,0:T(1,128)S(1)} %bitcast.14, f32[4,8,128]{2,1,0:T(8,128)S(1)} %get-tuple-element.17.flags, ...), custom_call_target="tpu_custom_call" | custom-call | bytes 1024 | tf_op jit(solution)/shard_map/inner_mixed/pallas_call | solution.py:322
  21.8 0.0 copy-start
  21.8 0.0 copy-start.3
  21.9 1.4 %collective-permute-done.3.above = bf16[9,3,32,128]{3,2,1,0:T(8,128)(2,1)S(1)} collective-permute-done((bf16[9,3,32,128]{3,2,1,0:T(8,128)(2,1)S(1)}, bf16[9,3,32,128]{3,2,1,0:T(8,128)(2,1)S(1)}, u32[]{:S(2)}, u32[]{:S(2)}) %collective-permute-start.3) | collective-permute-done | bytes 221216 | tf_op jit(solution)/shard_map/ppermute | solution.py:18
  23.3 2.3 %top_part.1.top_taps = bf16[5,3,16,384]{3,2,1,0:T(8,128)(2,1)S(1)} custom-call(bf16[2,4,32,256]{3,2,1,0:T(8,128)(2,1)S(1)} %get-tuple-element.20.far, bf16[4,4,32,256]{3,2,1,0:T(8,128)(2,1)S(1)} %get-tuple-element.18.near, bf16[3,4,32,256]{3,2,1,0:T(8,128)(2,1)S(1)} %get-tuple-element.14.own, bf16[9,3,32,128]{3,2,1,0:T(8,128)(2,1)S(1)} %collective-permute-done.3.above, ...), custom_call_target="tpu_custom_call" | custom-call | bytes 1024 | tf_op jit(solution)/shard_map/top_part/pallas_call | solution.py:325
  25.6 0.4 %collective-permute-done.2.below = bf16[9,2,32,128]{3,2,1,0:T(8,128)(2,1)S(1)} collective-permute-done((bf16[9,2,32,128]{3,2,1,0:T(8,128)(2,1)S(1)}, bf16[9,2,32,128]{3,2,1,0:T(8,128)(2,1)S(1)}, u32[]{:S(2)}, u32[]{:S(2)}) %collective-permute-start.2) | collective-permute-done | bytes 147488 | tf_op jit(solution)/shard_map/ppermute | solution.py:18
  26.0 0.0 copy-done
  26.0 0.0 copy-done.3
  26.0 2.5 %bottom_part.1 = bf16[2,2,8,512]{3,2,1,0:T(8,128)(2,1)} custom-call(bf16[2,4,32,256]{3,2,1,0:T(8,128)(2,1)S(1)} %get-tuple-element.20.far, bf16[4,4,32,256]{3,2,1,0:T(8,128)(2,1)S(1)} %get-tuple-element.18.near, bf16[3,4,32,256]{3,2,1,0:T(8,128)(2,1)S(1)} %get-tuple-element.14.own, bf16[9,2,32,128]{3,2,1,0:T(8,128)(2,1)S(1)} %collective-permute-done.2.below, ...), custom_call_target="tpu_custom_call" | custom-call | bytes 1024 | tf_op jit(solution)/shard_map/bottom_part/pallas_call | solution.py:331
  (1 shorter events, 0.0 us)
Async XLA Ops:
  0.0 11.9 %copy-start.1 = (f32[128]{0:T(128)S(1)}, f32[128]{0:T(128)}, u32[]{:S(2)}) copy-start(f32[128]{0:T(128)} %param.13) | copy-start | bytes 1540
  0.0 11.9 %copy-start.2 = (f32[128]{0:T(128)S(1)}, f32[128]{0:T(128)}, u32[]{:S(2)}) copy-start(f32[128]{0:T(128)} %param.15) | copy-start | bytes 1540
  0.0 11.9 %collective-permute-start.1 = (bf16[4,8,32,128]{3,2,1,0:T(8,128)(2,1)}, bf16[4,8,32,128]{3,2,1,0:T(8,128)(2,1)S(1)}, u32[]{:S(2)}, u32[]{:S(2)}) collective-permute-start(bf16[4,8,32,128]{3,2,1,0:T(8,128)(2,1)} %bitcast.18), channel_id=1, source_target_pairs={{0,4},{4,8},{8,12},{12,16},{16,20},{20,24},{24,28},{28,32},{32,36}... | collective-permute-start | bytes 786440 | tf_op jit(solution)/shard_map/ppermute | solution.py:18
  3.0 11.7 %collective-permute-start = (bf16[2,8,32,128]{3,2,1,0:T(8,128)(2,1)S(1)}, bf16[2,8,32,128]{3,2,1,0:T(8,128)(2,1)S(1)}, u32[]{:S(2)}, u32[]{:S(2)}) collective-permute-start(bf16[2,8,32,128]{3,2,1,0:T(8,128)(2,1)S(1)} %last_frames.1), channel_id=1, source_target_pairs={{0,8},{4,12},{8,16},{12,20},{16,24},{20,28},{24,32},{28,36},{32,40... | collective-permute-start | bytes 393224 | tf_op jit(solution)/shard_map/ppermute | solution.py:18
  14.7 8.6 %collective-permute-start.3 = (bf16[9,3,32,128]{3,2,1,0:T(8,128)(2,1)S(1)}, bf16[9,3,32,128]{3,2,1,0:T(8,128)(2,1)S(1)}, u32[]{:S(2)}, u32[]{:S(2)}) collective-permute-start(bf16[9,3,32,128]{3,2,1,0:T(8,128)(2,1)S(1)} %get-tuple-element.22), channel_id=1, source_target_pairs={{0,1},{1,2},{2,3},{4,5},{5,6},{6,7},{8,9},{9,10},{10,11},{12,13},{... | collective-permute-start | bytes 663560 | tf_op jit(solution)/shard_map/ppermute | solution.py:18
  18.9 7.0 %collective-permute-start.2 = (bf16[9,2,32,128]{3,2,1,0:T(8,128)(2,1)S(1)}, bf16[9,2,32,128]{3,2,1,0:T(8,128)(2,1)S(1)}, u32[]{:S(2)}, u32[]{:S(2)}) collective-permute-start(bf16[9,2,32,128]{3,2,1,0:T(8,128)(2,1)S(1)} %pack_down.1), channel_id=1, source_target_pairs={{1,0},{2,1},{3,2},{5,4},{6,5},{7,6},{9,8},{10,9},{11,10},{13,12},{... | collective-permute-start | bytes 442376 | tf_op jit(solution)/shard_map/ppermute | solution.py:18
  21.8 4.1 %copy-start = (bf16[3,3,3,128,128]{4,3,2,1,0:T(8,128)(2,1)S(1)}, bf16[3,3,3,128,128]{4,3,2,1,0:T(8,128)(2,1)}, u32[]{:S(2)}) copy-start(bf16[3,3,3,128,128]{4,3,2,1,0:T(8,128)(2,1)} %param.16) | copy-start | bytes 2654212
  21.8 4.1 %copy-start.3 = (f32[128]{0:T(128)S(1)}, f32[128]{0:T(128)}, u32[]{:S(2)}) copy-start(f32[128]{0:T(128)} %param.17) | copy-start | bytes 1540

commit v5 on v4

--- a/solution.py
+++ b/solution.py
@@ -28,9 +28,15 @@
 
 
 def last_frames(features, out, sem):
-    copy = pltpu.make_async_copy(features.at[pl.ds(2, 2)], out, sem)
-    copy.start()
-    copy.wait()
+    copies = [
+        pltpu.make_async_copy(features.at[2 + f, pl.ds(4 * part, 4)], out.at[f, pl.ds(4 * part, 4)], sem.at[2 * f + part])
+        for f in range(2)
+        for part in range(2)
+    ]
+    for copy in copies:
+        copy.start()
+    for copy in copies:
+        copy.wait()
 
 
 def prepare(lengths, order, features, a, b, pa, pb, pairs, flags, smem, own, taps, sem):
@@ -68,7 +74,8 @@
                     for j in range(2):
                         k = i - j
                         value = taps[n, t * 9 + k * 3 + w] if 0 <= k <= 2 else jnp.zeros((C, C), BF)
-                        dst[pl.ds((t * 4 + i) * C, C), pl.ds((w * 2 + j) * C, C)] = value
+                        at = (i // 2 * 3 + t) * 2 + i % 2
+                        dst[pl.ds(at * C, C), pl.ds((j * 3 + w) * C, C)] = value
 
 
 def pack_up(far, near, own, flags, after, up, pairs):
@@ -85,7 +92,7 @@
             up[2 + f, row - 5] = near[f, row // 2, :, lanes] if f < 4 else own[f - 4, row // 2, :, lanes]
 
 
-def pack_down(far, near, own, after, down):
+def pack_down(far, near, own, down):
     for f in range(9):
         for row in range(2):
             src, at = (far, f) if f < 2 else (near, f - 2) if f < 6 else (own, f - 6)
@@ -96,51 +103,58 @@
     return jnp.concatenate([bias[...], bias[...]], axis=1)
 
 
-def conv(blocks, fetch, weight):
+def conv(blocks, fetch, weight, sides=(0, 1), lower=False):
     rows = len(blocks) * 32
     lhs = jnp.concatenate(
         [
-            jnp.concatenate([fetch(f - 2 + t, q + h) for f, q in blocks], axis=0)
+            jnp.concatenate([fetch(f - 2 + t, q + side) for f, q in blocks], axis=0)
+            for side in sides
             for t in range(3)
-            for h in range(2)
         ],
         axis=1,
     )
-    y = jnp.dot(lhs, weight[...], preferred_element_type=F32)
-    col = lax.broadcasted_iota(jnp.int32, (rows, 2 * C), 0) % 32
-    left = jnp.where(col == 0, 0.0, pltpu.roll(y[:, : 2 * C], 1, 0))
-    right = jnp.where(col == 31, 0.0, pltpu.roll(y[:, 4 * C :], rows - 1, 0))
-    return y[:, 2 * C : 4 * C] + left + right
-
-
-def hidden_blocks(blocks, fetch, weight, bias, flags, put):
-    v = conv(blocks, fetch, weight) + bias
+    rhs = weight[pl.ds(sides[0] * 6 * C, len(sides) * 6 * C), pl.ds(3 * C if lower else 0, 3 * C if lower else 6 * C)]
+    y = jnp.dot(lhs, rhs, preferred_element_type=F32).reshape(len(blocks), 32, -1)
+    col = lax.broadcasted_iota(jnp.int32, (1, 32, C), 1)
+    out = []
+    for at in range(0, y.shape[2], 3 * C):
+        left = jnp.where(col == 0, 0.0, pltpu.roll(y[:, :, at : at + C], 1, 1))
+        right = jnp.where(col == 31, 0.0, pltpu.roll(y[:, :, at + 2 * C : at + 3 * C], 31, 1))
+        out.append(y[:, :, at + C : at + 2 * C] + left + right)
+    return (out[0] if lower else jnp.concatenate(out, axis=2)).reshape(rows, -1)
+
+
+def hidden_blocks(blocks, sums, bias, flags, put):
+    lower = sums.shape[1] == C
+    v = sums + (bias[...] if lower else twice(bias))
     v = v / (1.0 + jnp.exp(-v))
     keep, top, bottom = (flags[i, 0:1, :] for i in (0, 2, 3))
     one = jnp.ones_like(top)
     for i, (f, q) in enumerate(blocks):
         value = v[i * 32 : i * 32 + 32]
         if q == 0:
-            value = value * jnp.concatenate([top, top], axis=1)
+            value = value * top
         elif q == 1:
             value = value * jnp.concatenate([top, one], axis=1)
         elif q == 5:
             value = value * jnp.concatenate([one, bottom], axis=1)
         if f < 0:
-            value = value * jnp.concatenate([keep, keep], axis=1)
+            value = value * (keep if lower else jnp.concatenate([keep, keep], axis=1))
         put(f, q, value.astype(BF))
 
 
-def mixed_blocks(blocks, fetch, residual, weight, bias, flags, put):
-    v = conv(blocks, fetch, weight) + bias
+def mixed_blocks(blocks, sums, residual, bias, flags, put):
+    lower = sums.shape[1] == C
+    v = sums + (bias[...] if lower else twice(bias))
     keep, top = flags[0, 0:1, :], flags[2, 0:1, :]
     for i, (f, p) in enumerate(blocks):
-        value = residual(f, p + 1).astype(F32) + v[i * 32 : i * 32 + 32]
+        x = residual(f, p + 1).astype(F32)
+        value = (x[:, C:] if lower else x) + v[i * 32 : i * 32 + 32]
         value = value.astype(BF).astype(F32)
         if f < 0:
-            value = value * jnp.concatenate([keep, keep], axis=1)
+            value = value * (keep if lower else jnp.concatenate([keep, keep], axis=1))
         if p == 0:
-            put(f, 0, value[:, C:] * top)
+            put(f, 0, value * top)
         else:
             put(f, 2 * p - 1, value[:, :C])
             put(f, 2 * p, value[:, C:])
@@ -176,9 +190,11 @@
         m[f, r - 3] = value
 
     for frames in ((-2, -1), (0, 1, 2)):
-        hidden_blocks([(f, q) for f in frames for q in (2, 3, 4)], feature, wa, twice(ba), flags, put_hidden)
+        blocks = [(f, q) for f in frames for q in (2, 3, 4)]
+        hidden_blocks(blocks, conv(blocks, feature, wa), ba, flags, put_hidden)
     blocks = [(f, p) for f in range(3) for p in (2, 3)]
-    mixed_blocks(blocks, lambda f, q: hidden[f + 2, q - 2], feature, wb, twice(bb), flags, put_mixed)
+    sums = conv(blocks, lambda f, q: hidden[f + 2, q - 2], wb)
+    mixed_blocks(blocks, sums, feature, bb, flags, put_mixed)
     for f in range(3):
         for r in range(4):
             taps[f, r] = column_taps(m.at[f, r])
@@ -189,7 +205,7 @@
         hidden[f + 4, q - 2] = value
 
     blocks = [(f, q) for f in (-4, -3) for q in (2, 3, 4)]
-    hidden_blocks(blocks, own_feature(far, near, None), wa, twice(ba), flags, put_hidden)
+    hidden_blocks(blocks, conv(blocks, own_feature(far, near, None), wa), ba, flags, put_hidden)
 
 
 def inner_mixed(near, wb, bb, flags, hidden_far, hidden_near, taps, m):
@@ -200,51 +216,84 @@
         m[f + 2, r - 3] = value
 
     blocks = [(f, p) for f in (-2, -1) for p in (2, 3)]
-    mixed_blocks(blocks, hidden, own_feature(None, near, None), wb, twice(bb), flags, put_mixed)
+    mixed_blocks(blocks, conv(blocks, hidden, wb), own_feature(None, near, None), bb, flags, put_mixed)
     for f in range(2):
         for r in range(4):
             taps[f, r] = column_taps(m.at[f, r])
 
 
-def edge(far, near, own, wa, ba, wb, bb, flags, hidden_far, hidden_near, h, m, halo, q_edge, p_edge, row):
+HIDDEN = range(-4, 3)
+MIXED = range(-2, 3)
+
+
+def inner_hidden(hidden_far, hidden_near):
+    def hidden(f, q):
+        return hidden_far[f + 4, q - 2] if f < -2 else hidden_near[f + 2, q - 2]
+
+    return hidden
+
+
+def early_part(far, near, own, wa, wb, hidden_far, hidden_near, after, top_hidden, top_mixed, bottom_hidden, bottom_mixed):
+    feature = own_feature(far, near, own)
+    hidden = inner_hidden(hidden_far, hidden_near)
+    top_hidden[...] = conv([(f, 1) for f in HIDDEN], feature, wa, (1,))
+    top_mixed[...] = conv([(f, 1) for f in MIXED], hidden, wb, (1,))
+    bottom_hidden[...] = conv([(f, 5) for f in HIDDEN], feature, wa, (0,))
+    bottom_mixed[...] = conv([(f, 4) for f in MIXED], hidden, wb, (0,))
+
+
+def top_part(far, near, own, above, wa, ba, wb, bb, flags, part_hidden, part_mixed, taps, h, m):
+    inside = own_feature(far, near, own)
+
     def feature(f, g):
-        return own_feature(far, near, own)(f, g) if 2 <= g <= 5 else halo(f + 6, g)
+        if g >= 2:
+            return inside(f, g)
+        upper = jnp.zeros((32, C), BF) if g == 0 else above[f + 6, 1]
+        return jnp.concatenate([upper, above[f + 6, 2 * g]], axis=1)
 
     def put_hidden(f, q, value):
-        h[f + 4, q_edge.index(q)] = value
+        if q == 0:
+            h[f + 4, 0, :, pl.ds(0, C)] = jnp.zeros((32, C), BF)
+            h[f + 4, 0, :, pl.ds(C, C)] = value
+        else:
+            h[f + 4, 1] = value
+
+    def put_mixed(f, r, value):
+        m[f + 2, r] = value
 
     def hidden(f, q):
-        if 2 <= q <= 4:
-            return hidden_far[f + 4, q - 2] if f < -2 else hidden_near[f + 2, q - 2]
-        return h[f + 4, q_edge.index(q)]
-
-    def put_mixed(f, r, value):
-        m[f + 2, r - row] = value
-
-    split = ((-4, -3, -2), (-1, 0, 1, 2)) if len(q_edge) > 1 else (range(-4, 3),)
-    for frames in split:
-        hidden_blocks([(f, q) for f in frames for q in q_edge], feature, wa, twice(ba), flags, put_hidden)
-    mixed_blocks([(f, p) for f in range(-2, 3) for p in p_edge], hidden, feature, wb, twice(bb), flags, put_mixed)
-
-
-def top_part(far, near, own, above, wa, ba, wb, bb, flags, hidden_far, hidden_near, taps, h, m):
-    def halo(i, g):
-        upper = jnp.zeros((32, C), BF) if g == 0 else above[i, 1]
-        return jnp.concatenate([upper, above[i, 2 * g]], axis=1)
-
-    edge(far, near, own, wa, ba, wb, bb, flags, hidden_far, hidden_near, h, m, halo, (0, 1), (0, 1), 0)
+        return h[f + 4, q]
+
+    blocks = [(f, 1) for f in HIDDEN]
+    hidden_blocks(blocks, conv(blocks, feature, wa, (0,)) + part_hidden[...], ba, flags, put_hidden)
+    blocks = [(f, 0) for f in HIDDEN]
+    hidden_blocks(blocks, conv(blocks, feature, wa, lower=True), ba, flags, put_hidden)
+    blocks = [(f, 1) for f in MIXED]
+    mixed_blocks(blocks, conv(blocks, hidden, wb, (0,)) + part_mixed[...], feature, bb, flags, put_mixed)
+    blocks = [(f, 0) for f in MIXED]
+    mixed_blocks(blocks, conv(blocks, hidden, wb, lower=True), feature, bb, flags, put_mixed)
     for f in range(5):
         for r in range(3):
             taps[f, r] = column_taps(m.at[f, r])
 
 
 def bottom_part(
-    far, near, own, below, wa, ba, wb, bb, wd, bd, flags, hidden_far, hidden_near, top_taps, taps_far, taps_near, out, h, m
+    far, near, own, below, wa, ba, wb, bb, wd, bd, flags, part_hidden, part_mixed, top_taps, taps_far, taps_near, out, h, m
 ):
-    def halo(i, g):
-        return jnp.concatenate([below[i, 0], below[i, 1]], axis=1)
-
-    edge(far, near, own, wa, ba, wb, bb, flags, hidden_far, hidden_near, h, m, halo, (5,), (4,), 7)
+    def feature(f, g):
+        return jnp.concatenate([below[f + 6, 0], below[f + 6, 1]], axis=1)
+
+    def put_hidden(f, q, value):
+        h[f + 4] = value
+
+    def put_mixed(f, r, value):
+        m[f + 2, r - 7] = value
+
+    blocks = [(f, 5) for f in HIDDEN]
+    hidden_blocks(blocks, conv(blocks, feature, wa, (1,)) + part_hidden[...], ba, flags, put_hidden)
+    blocks = [(f, 4) for f in MIXED]
+    sums = conv(blocks, lambda f, q: h[f + 4], wb, (1,)) + part_mixed[...]
+    mixed_blocks(blocks, sums, own_feature(far, near, own), bb, flags, put_mixed)
     frames = []
     for f in range(5):
         rows = [top_taps[f, r] for r in range(3)] + [taps_far[f, r] if f < 2 else taps_near[f - 2, r] for r in range(4)]
@@ -291,7 +340,7 @@
         last_frames,
         [((2, 8, 32, C), BF)],
         [HBM],
-        [pltpu.SemaphoreType.DMA],
+        [pltpu.SemaphoreType.DMA((4,))],
     )(stay[2])
     far = shifted(tail, "span", 2)
     packed = ((12 * C, 6 * C), BF)
@@ -316,25 +365,30 @@
         pack_up, [((9, 3, 32, C), BF), ((2, 4, 32, 2 * C), BF)], [VMEM] * 5
     )(far, near, own, flags, taps_near)
     above = shifted(up, "row", 1)
+    (down,) = kernel(pack_down, [((9, 2, 32, C), BF)], [VMEM] * 3)(far, near, own)
+    below = shifted(down, "row", -1)
     (hidden_far,) = kernel(inner_far, [((2, 3, 32, 2 * C), BF)], [VMEM] * 5)(far, near, wa, ba, flags)
-    (down,) = kernel(pack_down, [((9, 2, 32, C), BF)], [VMEM] * 4)(far, near, own, hidden_far)
-    below = shifted(down, "row", -1)
     (taps_far,) = kernel(
         inner_mixed, [((2, 4, 16, 3 * C), BF)], [VMEM] * 6, [pltpu.VMEM((2, 4, 32, C), F32)]
     )(near, wb, bb, flags, hidden_far, hidden_near)
+    sums_hidden = ((7 * 32, 2 * C), F32)
+    sums_mixed = ((5 * 32, 2 * C), F32)
+    top_hidden, top_mixed, bottom_hidden, bottom_mixed = kernel(
+        early_part, [sums_hidden, sums_mixed] * 2, [VMEM] * 8
+    )(far, near, own, wa, wb, hidden_far, hidden_near, taps_far)
     (top_taps,) = kernel(
         top_part,
         [((5, 3, 16, 3 * C), BF)],
         [VMEM] * 11,
         [pltpu.VMEM((7, 2, 32, 2 * C), BF), pltpu.VMEM((5, 3, 32, C), F32)],
-    )(far, near, own, above, wa, ba, wb, bb, flags, hidden_far, hidden_near)
+    )(far, near, own, above, wa, ba, wb, bb, flags, top_hidden, top_mixed)
     (out,) = kernel(
         bottom_part,
         [((2, 2, 8, 4 * C), BF)],
         [VMEM] * 16,
-        [pltpu.VMEM((7, 1, 32, 2 * C), BF), pltpu.VMEM((5, 2, 32, C), F32)],
+        [pltpu.VMEM((7, 32, 2 * C), BF), pltpu.VMEM((5, 2, 32, C), F32)],
     )(
-        far, near, own, below, wa, ba, wb, bb, wd, bd, flags, hidden_far, hidden_near, top_taps, taps_far, taps_near
+        far, near, own, below, wa, ba, wb, bb, wd, bd, flags, bottom_hidden, bottom_mixed, top_taps, taps_far, taps_near
     )
     return out[None]
 

time: 28.7 us -> 27.5 us (0.958)
  waiting for transfers between devices: 5.68 us -> 4.98 us
  Pallas kernels: 10.9 us -> 10.4 us
    pallas_call x2 -> x3, Pallas kernels: 0.94 us -> 1.97 us  [the longest x1 1.1 us: per_device(): kernel(early_part, [sums_hidden, sums_mixed] * 2, [VMEM] * 8)]
    pallas_call x1, Pallas kernels: 2.29 us -> 1.29 us  [per_device(): kernel(top_part, [((5, 3, 16, 3 * C), BF)], [VMEM] * 11, [pltpu.VMEM((7,...]
    ppermute x4, waiting for transfers between devices: 5.68 us -> 4.98 us  [shifted(): return lax.ppermute(x, axis, pairs)]
    pallas_call x1, Pallas kernels: 2.45 us -> 1.88 us  [per_device(): kernel(bottom_part, [((2, 2, 8, 4 * C), BF)], [VMEM] * 16, [pltpu.VMEM((7...]
  transfers between devices with their start and end apart: 4 -> 4, of which waited for: 4 -> 4; matrix products, arithmetic and copies ran while one was open for 0% -> 0% of each run, Pallas kernels for 30% -> 31%
where the time goes in v5:
time: 27.5 us; the launch traced here: 27.2 us
  starting transfers between devices  11.7 us (43%)
  Pallas kernels  10.4 us (38%)
  waiting for transfers between devices  4.98 us (18%)
    ppermute x4, starting transfers between devices, shifted(): return lax.ppermute(x, axis, pairs)  11.7 us
    ppermute x4, waiting for transfers between devices, shifted(): return lax.ppermute(x, axis, pairs)  4.98 us
    pallas_call x1, Pallas kernels, per_device(): kernel(inner_near, [((4, 4, 32, 2 * C), BF), ((5, 3, 32, 2 * C), BF), ((3...  2.2 us
    pallas_call x1, Pallas kernels, per_device(): kernel(bottom_part, [((2, 2, 8, 4 * C), BF)], [VMEM] * 16, [pltpu.VMEM((7...  1.88 us
    pallas_call x1, Pallas kernels, per_device(): kernel(prepare, [packed, packed, ((3, 4, 32, 2 * C), BF), ((4, 8, C), F32...  1.77 us
    pallas_call x1, Pallas kernels, per_device(): kernel(top_part, [((5, 3, 16, 3 * C), BF)], [VMEM] * 11, [pltpu.VMEM((7,...  1.29 us
    pallas_call x1, Pallas kernels, per_device(): kernel(early_part, [sums_hidden, sums_mixed] * 2, [VMEM] * 8)  1.1 us
    pallas_call x1, Pallas kernels, per_device(): kernel(last_frames, [((2, 8, 32, C), BF)], [HBM], [pltpu.SemaphoreType.DM...  0.84 us
  transfers between devices with their start and end apart: 4, of which 4 were waited for; matrix products, arithmetic and copies ran while one was open for 0% of the time, Pallas kernels for 31%

profile of v5, /device:TPU:14, one launch (start us, length us, event | category | flops | bytes accessed | tf_op | source)
XLA Modules:
  0.0 27.2 jit_solution(12864856383432247991)
XLA Ops:
  0.0 0.0 copy-start.1
  0.0 0.0 copy-start.2
  0.0 2.0 %collective-permute-start.1 = (bf16[4,8,32,128]{3,2,1,0:T(8,128)(2,1)}, bf16[4,8,32,128]{3,2,1,0:T(8,128)(2,1)S(1)}, u32[]{:S(2)}, u32[]{:S(2)}) collective-permute-start(bf16[4,8,32,128]{3,2,1,0:T(8,128)(2,1)} %bitcast.18), channel_id=1, source_target_pairs={{0,4},{4,8},{8,12},{12,16},{16,20},{20,24},{24,28},{28,32},{32,36}... | collective-permute-start | bytes 786440 | tf_op jit(solution)/shard_map/ppermute | solution.py:18
  2.1 0.8 %last_frames.1 = bf16[2,8,32,128]{3,2,1,0:T(8,128)(2,1)S(1)} custom-call(bf16[4,8,32,128]{3,2,1,0:T(8,128)(2,1)} %bitcast.19), custom_call_target="tpu_custom_call" | custom-call | bytes 1024 | tf_op jit(solution)/shard_map/last_frames/pallas_call | solution.py:339
  2.9 3.8 %collective-permute-start = (bf16[2,8,32,128]{3,2,1,0:T(8,128)(2,1)S(1)}, bf16[2,8,32,128]{3,2,1,0:T(8,128)(2,1)S(1)}, u32[]{:S(2)}, u32[]{:S(2)}) collective-permute-start(bf16[2,8,32,128]{3,2,1,0:T(8,128)(2,1)S(1)} %last_frames.1), channel_id=1, source_target_pairs={{0,8},{4,12},{8,16},{12,20},{16,24},{20,28},{24,32},{28,36},{32,40... | collective-permute-start | bytes 393224 | tf_op jit(solution)/shard_map/ppermute | solution.py:18
  6.7 1.8 %prepare.1 = (bf16[1536,768]{1,0:T(8,128)(2,1)S(1)}, bf16[1536,768]{1,0:T(8,128)(2,1)S(1)}, bf16[3,4,32,256]{3,2,1,0:T(8,128)(2,1)S(1)}, f32[4,8,128]{2,1,0:T(8,128)S(1)}) custom-call(s32[16]{0:T(128)} %lengths.1, s32[16]{0:T(128)} %order.1, bf16[4,8,32,128]{3,2,1,0:T(8,128)(2,1)} %bitcast.20, bf16[27,128,128]{2,1,0:T(8,128)(2,1)} %bitcast.21, ...), custom_call_target="tpu_custom_call" | custom-call | bytes 1024 | tf_op jit(solution)/shard_map/prepare/pallas_call | solution.py:347
  8.5 3.3 %collective-permute-done.1.arrived = bf16[4,8,32,128]{3,2,1,0:T(8,128)(2,1)S(1)} collective-permute-done((bf16[4,8,32,128]{3,2,1,0:T(8,128)(2,1)}, bf16[4,8,32,128]{3,2,1,0:T(8,128)(2,1)S(1)}, u32[]{:S(2)}, u32[]{:S(2)}) %collective-permute-start.1) | collective-permute-done | bytes 262176 | tf_op jit(solution)/shard_map/ppermute | solution.py:18
  11.9 0.0 copy-done.1
  11.9 0.0 copy-done.2
  11.9 2.2 %inner_near.1 = (bf16[4,4,32,256]{3,2,1,0:T(8,128)(2,1)S(1)}, bf16[5,3,32,256]{3,2,1,0:T(8,128)(2,1)S(1)}, bf16[3,4,16,384]{3,2,1,0:T(8,128)(2,1)S(1)}) custom-call(bf16[4,8,32,128]{3,2,1,0:T(8,128)(2,1)S(1)} %collective-permute-done.1.arrived, bf16[3,4,32,256]{3,2,1,0:T(8,128)(2,1)S(1)} %get-tuple-element.18.own, ...), custom_call_target="tpu_custom_call" | custom-call | bytes 1024 | tf_op jit(solution)/shard_map/inner_near/pallas_call | solution.py:358
  14.1 0.6 %collective-permute-done.far = bf16[2,8,32,128]{3,2,1,0:T(8,128)(2,1)S(1)} collective-permute-done((bf16[2,8,32,128]{3,2,1,0:T(8,128)(2,1)S(1)}, bf16[2,8,32,128]{3,2,1,0:T(8,128)(2,1)S(1)}, u32[]{:S(2)}, u32[]{:S(2)}) %collective-permute-start) | collective-permute-done | bytes 131104 | tf_op jit(solution)/shard_map/ppermute | solution.py:18
  14.7 0.1 pack_up.1
  14.7 3.5 %collective-permute-start.3 = (bf16[9,3,32,128]{3,2,1,0:T(8,128)(2,1)S(1)}, bf16[9,3,32,128]{3,2,1,0:T(8,128)(2,1)S(1)}, u32[]{:S(2)}, u32[]{:S(2)}) collective-permute-start(bf16[9,3,32,128]{3,2,1,0:T(8,128)(2,1)S(1)} %get-tuple-element.28), channel_id=1, source_target_pairs={{0,1},{1,2},{2,3},{4,5},{5,6},{6,7},{8,9},{9,10},{10,11},{12,13},{... | collective-permute-start | bytes 663560 | tf_op jit(solution)/shard_map/ppermute | solution.py:18
  18.2 2.4 %collective-permute-start.2 = (bf16[9,2,32,128]{3,2,1,0:T(8,128)(2,1)S(1)}, bf16[9,2,32,128]{3,2,1,0:T(8,128)(2,1)S(1)}, u32[]{:S(2)}, u32[]{:S(2)}) collective-permute-start(bf16[9,2,32,128]{3,2,1,0:T(8,128)(2,1)S(1)} %pack_down.1), channel_id=1, source_target_pairs={{1,0},{2,1},{3,2},{5,4},{6,5},{7,6},{9,8},{10,9},{11,10},{13,12},{... | collective-permute-start | bytes 442376 | tf_op jit(solution)/shard_map/ppermute | solution.py:18
  20.6 0.7 %inner_far.1.hidden_far = bf16[2,3,32,256]{3,2,1,0:T(8,128)(2,1)S(1)} custom-call(bf16[2,4,32,256]{3,2,1,0:T(8,128)(2,1)S(1)} %get-tuple-element.24.far, bf16[4,4,32,256]{3,2,1,0:T(8,128)(2,1)S(1)} %get-tuple-element.22.near, bf16[1536,768]{1,0:T(8,128)(2,1)S(1)} %get-tuple-element.19.wa, f32[1,128]{1,0:T(1,128)S(1)} %bitcast.10, ...), custom_call_target="tpu_custom_call" | custom-call | bytes 1024 | tf_op jit(solution)/shard_map/inner_far/pallas_call | solution.py:370
  21.3 0.5 %inner_mixed.1.after.taps_far = bf16[2,4,16,384]{3,2,1,0:T(8,128)(2,1)S(1)} custom-call(bf16[4,4,32,256]{3,2,1,0:T(8,128)(2,1)S(1)} %get-tuple-element.22.near, bf16[1536,768]{1,0:T(8,128)(2,1)S(1)} %get-tuple-element.20.wb, f32[1,128]{1,0:T(1,128)S(1)} %bitcast.14, f32[4,8,128]{2,1,0:T(8,128)S(1)} %get-tuple-element.21.flags, ...), custom_call_target="tpu_custom_call" | custom-call | bytes 1024 | tf_op jit(solution)/shard_map/inner_mixed/pallas_call | solution.py:371
  21.8 1.1 %early_part.1 = (f32[224,256]{1,0:T(8,128)S(1)}, f32[160,256]{1,0:T(8,128)S(1)}, f32[224,256]{1,0:T(8,128)S(1)}, f32[160,256]{1,0:T(8,128)S(1)}) custom-call(bf16[2,4,32,256]{3,2,1,0:T(8,128)(2,1)S(1)} %get-tuple-element.24.far, bf16[4,4,32,256]{3,2,1,0:T(8,128)(2,1)S(1)} %get-tuple-element.22.near, bf16[3,4,32,256]{3,2,1,0:T(8,128)(2,1)S(1)} %get-tuple-element.18.own, ...), custom_call_target="tpu_custom_call" | custom-call | bytes 1024 | tf_op jit(solution)/shard_map/early_part/pallas_call | solution.py:376
  22.9 0.4 %collective-permute-done.3.above = bf16[9,3,32,128]{3,2,1,0:T(8,128)(2,1)S(1)} collective-permute-done((bf16[9,3,32,128]{3,2,1,0:T(8,128)(2,1)S(1)}, bf16[9,3,32,128]{3,2,1,0:T(8,128)(2,1)S(1)}, u32[]{:S(2)}, u32[]{:S(2)}) %collective-permute-start.3) | collective-permute-done | bytes 221216 | tf_op jit(solution)/shard_map/ppermute | solution.py:18
  23.4 0.0 copy-start
  23.4 0.0 copy-start.3
  23.4 1.3 %top_part.1.top_taps = bf16[5,3,16,384]{3,2,1,0:T(8,128)(2,1)S(1)} custom-call(bf16[2,4,32,256]{3,2,1,0:T(8,128)(2,1)S(1)} %get-tuple-element.24.far, bf16[4,4,32,256]{3,2,1,0:T(8,128)(2,1)S(1)} %get-tuple-element.22.near, bf16[3,4,32,256]{3,2,1,0:T(8,128)(2,1)S(1)} %get-tuple-element.18.own, bf16[9,3,32,128]{3,2,1,0:T(8,128)(2,1)S(1)} %collective-permute-done.3.above, ...), custom_call_target="tpu_custom_call" | custom-call | bytes 1024 | tf_op jit(solution)/shard_map/top_part/pallas_call | solution.py:379
  24.7 0.6 %collective-permute-done.2.below = bf16[9,2,32,128]{3,2,1,0:T(8,128)(2,1)S(1)} collective-permute-done((bf16[9,2,32,128]{3,2,1,0:T(8,128)(2,1)S(1)}, bf16[9,2,32,128]{3,2,1,0:T(8,128)(2,1)S(1)}, u32[]{:S(2)}, u32[]{:S(2)}) %collective-permute-start.2) | collective-permute-done | bytes 147488 | tf_op jit(solution)/shard_map/ppermute | solution.py:18
  25.3 0.0 copy-done
  25.3 0.0 copy-done.3
  25.3 1.9 %bottom_part.1 = bf16[2,2,8,512]{3,2,1,0:T(8,128)(2,1)} custom-call(bf16[2,4,32,256]{3,2,1,0:T(8,128)(2,1)S(1)} %get-tuple-element.24.far, bf16[4,4,32,256]{3,2,1,0:T(8,128)(2,1)S(1)} %get-tuple-element.22.near, bf16[3,4,32,256]{3,2,1,0:T(8,128)(2,1)S(1)} %get-tuple-element.18.own, bf16[9,2,32,128]{3,2,1,0:T(8,128)(2,1)S(1)} %collective-permute-done.2.below, ...), custom_call_target="tpu_custom_call" | custom-call | bytes 1024 | tf_op jit(solution)/shard_map/bottom_part/pallas_call | solution.py:385
  (1 shorter events, 0.0 us)
Async XLA Ops:
  0.0 11.9 %copy-start.1 = (f32[128]{0:T(128)S(1)}, f32[128]{0:T(128)}, u32[]{:S(2)}) copy-start(f32[128]{0:T(128)} %param.13) | copy-start | bytes 1540
  0.0 11.9 %copy-start.2 = (f32[128]{0:T(128)S(1)}, f32[128]{0:T(128)}, u32[]{:S(2)}) copy-start(f32[128]{0:T(128)} %param.15) | copy-start | bytes 1540
  0.0 11.9 %collective-permute-start.1 = (bf16[4,8,32,128]{3,2,1,0:T(8,128)(2,1)}, bf16[4,8,32,128]{3,2,1,0:T(8,128)(2,1)S(1)}, u32[]{:S(2)}, u32[]{:S(2)}) collective-permute-start(bf16[4,8,32,128]{3,2,1,0:T(8,128)(2,1)} %bitcast.18), channel_id=1, source_target_pairs={{0,4},{4,8},{8,12},{12,16},{16,20},{20,24},{24,28},{28,32},{32,36}... | collective-permute-start | bytes 786440 | tf_op jit(solution)/shard_map/ppermute | solution.py:18
  2.9 11.8 %collective-permute-start = (bf16[2,8,32,128]{3,2,1,0:T(8,128)(2,1)S(1)}, bf16[2,8,32,128]{3,2,1,0:T(8,128)(2,1)S(1)}, u32[]{:S(2)}, u32[]{:S(2)}) collective-permute-start(bf16[2,8,32,128]{3,2,1,0:T(8,128)(2,1)S(1)} %last_frames.1), channel_id=1, source_target_pairs={{0,8},{4,12},{8,16},{12,20},{16,24},{20,28},{24,32},{28,36},{32,40... | collective-permute-start | bytes 393224 | tf_op jit(solution)/shard_map/ppermute | solution.py:18
  14.7 8.7 %collective-permute-start.3 = (bf16[9,3,32,128]{3,2,1,0:T(8,128)(2,1)S(1)}, bf16[9,3,32,128]{3,2,1,0:T(8,128)(2,1)S(1)}, u32[]{:S(2)}, u32[]{:S(2)}) collective-permute-start(bf16[9,3,32,128]{3,2,1,0:T(8,128)(2,1)S(1)} %get-tuple-element.28), channel_id=1, source_target_pairs={{0,1},{1,2},{2,3},{4,5},{5,6},{6,7},{8,9},{9,10},{10,11},{12,13},{... | collective-permute-start | bytes 663560 | tf_op jit(solution)/shard_map/ppermute | solution.py:18
  18.2 7.0 %collective-permute-start.2 = (bf16[9,2,32,128]{3,2,1,0:T(8,128)(2,1)S(1)}, bf16[9,2,32,128]{3,2,1,0:T(8,128)(2,1)S(1)}, u32[]{:S(2)}, u32[]{:S(2)}) collective-permute-start(bf16[9,2,32,128]{3,2,1,0:T(8,128)(2,1)S(1)} %pack_down.1), channel_id=1, source_target_pairs={{1,0},{2,1},{3,2},{5,4},{6,5},{7,6},{9,8},{10,9},{11,10},{13,12},{... | collective-permute-start | bytes 442376 | tf_op jit(solution)/shard_map/ppermute | solution.py:18
  23.4 1.9 %copy-start = (bf16[3,3,3,128,128]{4,3,2,1,0:T(8,128)(2,1)S(1)}, bf16[3,3,3,128,128]{4,3,2,1,0:T(8,128)(2,1)}, u32[]{:S(2)}) copy-start(bf16[3,3,3,128,128]{4,3,2,1,0:T(8,128)(2,1)} %param.16) | copy-start | bytes 2654212
  23.4 1.9 %copy-start.3 = (f32[128]{0:T(128)S(1)}, f32[128]{0:T(128)}, u32[]{:S(2)}) copy-start(f32[128]{0:T(128)} %param.17) | copy-start | bytes 1540

commit v6 on v5

--- a/solution.py
+++ b/solution.py
@@ -242,7 +242,9 @@
     bottom_mixed[...] = conv([(f, 4) for f in MIXED], hidden, wb, (0,))
 
 
-def top_part(far, near, own, above, wa, ba, wb, bb, flags, part_hidden, part_mixed, taps, h, m):
+def top_part(
+    far, near, own, above, wa, ba, wb, bb, wd, bd, flags, part_hidden, part_mixed, taps_far, taps_near, sums, h, m
+):
     inside = own_feature(far, near, own)
 
     def feature(f, g):
@@ -272,44 +274,53 @@
     mixed_blocks(blocks, conv(blocks, hidden, wb, (0,)) + part_mixed[...], feature, bb, flags, put_mixed)
     blocks = [(f, 0) for f in MIXED]
     mixed_blocks(blocks, conv(blocks, hidden, wb, lower=True), feature, bb, flags, put_mixed)
-    for f in range(5):
-        for r in range(3):
-            taps[f, r] = column_taps(m.at[f, r])
-
-
-def bottom_part(
-    far, near, own, below, wa, ba, wb, bb, wd, bd, flags, part_hidden, part_mixed, top_taps, taps_far, taps_near, out, h, m
-):
-    def feature(f, g):
-        return jnp.concatenate([below[f + 6, 0], below[f + 6, 1]], axis=1)
-
-    def put_hidden(f, q, value):
-        h[f + 4] = value
-
-    def put_mixed(f, r, value):
-        m[f + 2, r - 7] = value
-
-    blocks = [(f, 5) for f in HIDDEN]
-    hidden_blocks(blocks, conv(blocks, feature, wa, (1,)) + part_hidden[...], ba, flags, put_hidden)
-    blocks = [(f, 4) for f in MIXED]
-    sums = conv(blocks, lambda f, q: h[f + 4], wb, (1,)) + part_mixed[...]
-    mixed_blocks(blocks, sums, own_feature(far, near, own), bb, flags, put_mixed)
+    none = jnp.zeros((16, 3 * C), BF)
     frames = []
     for f in range(5):
-        rows = [top_taps[f, r] for r in range(3)] + [taps_far[f, r] if f < 2 else taps_near[f - 2, r] for r in range(4)]
-        rows += [column_taps(m.at[f, r]) for r in range(2)]
+        rows = [column_taps(m.at[f, r]) for r in range(3)]
+        rows += [taps_far[f, r] if f < 2 else taps_near[f - 2, r] for r in range(4)] + [none, none]
         frames.append(
             jnp.concatenate(
                 [jnp.concatenate([rows[2 * j + k] for k in range(3)], axis=1) for j in range(4)], axis=0
             )
         )
     lhs = jnp.concatenate([jnp.concatenate(frames[t : t + 3], axis=1) for t in (0, 2)], axis=0)
-    v = jnp.dot(lhs, wd[...], preferred_element_type=F32) + bd[...]
-    v = v.astype(BF).astype(F32)
+    sums[...] = jnp.dot(lhs, wd[...], preferred_element_type=F32) + bd[...]
+
+
+def bottom_part(
+    far, near, own, below, wa, ba, wb, bb, wd, flags, part_hidden, part_mixed, sums, out, h, m
+):
+    def feature(f, g):
+        return jnp.concatenate([below[f + 6, 0], below[f + 6, 1]], axis=1)
+
+    def put_hidden(f, q, value):
+        h[f + 4] = value
+
+    def put_mixed(f, r, value):
+        m[f + 2, r - 7] = value
+
+    blocks = [(f, 5) for f in HIDDEN]
+    hidden_blocks(blocks, conv(blocks, feature, wa, (1,)) + part_hidden[...], ba, flags, put_hidden)
+    blocks = [(f, 4) for f in MIXED]
+    total = conv(blocks, lambda f, q: h[f + 4], wb, (1,)) + part_mixed[...]
+    mixed_blocks(blocks, total, own_feature(far, near, own), bb, flags, put_mixed)
+    rows = [jnp.concatenate([column_taps(m.at[f, r]) for r in range(2)], axis=1) for f in range(5)]
+    low = sum(
+        jnp.dot(
+            jnp.concatenate([rows[t], rows[t + 2]], axis=0),
+            wd[pl.ds((9 * t + 3) * C, 6 * C), :],
+            preferred_element_type=F32,
+        )
+        for t in range(3)
+    )
     for t in range(2):
         for i in range(2):
             at = t * 64 + i * 32
-            out[t, i] = jnp.concatenate([v[at + k * 8 : at + k * 8 + 8] for k in range(4)], axis=1).astype(BF)
+            v = sums[at : at + 32]
+            if i == 1:
+                v = jnp.concatenate([v[:16], v[16:] + low[t * 16 : t * 16 + 16]], axis=0)
+            out[t, i] = jnp.concatenate([v[k * 8 : k * 8 + 8] for k in range(4)], axis=1).astype(BF)
 
 
 def kernel(body, outs, ins, scratch=(), flops=0):
@@ -376,20 +387,18 @@
     top_hidden, top_mixed, bottom_hidden, bottom_mixed = kernel(
         early_part, [sums_hidden, sums_mixed] * 2, [VMEM] * 8
     )(far, near, own, wa, wb, hidden_far, hidden_near, taps_far)
-    (top_taps,) = kernel(
+    (sums,) = kernel(
         top_part,
-        [((5, 3, 16, 3 * C), BF)],
-        [VMEM] * 11,
+        [((128, C), F32)],
+        [VMEM] * 15,
         [pltpu.VMEM((7, 2, 32, 2 * C), BF), pltpu.VMEM((5, 3, 32, C), F32)],
-    )(far, near, own, above, wa, ba, wb, bb, flags, top_hidden, top_mixed)
+    )(far, near, own, above, wa, ba, wb, bb, wd, bd, flags, top_hidden, top_mixed, taps_far, taps_near)
     (out,) = kernel(
         bottom_part,
         [((2, 2, 8, 4 * C), BF)],
-        [VMEM] * 16,
+        [VMEM] * 13,
         [pltpu.VMEM((7, 32, 2 * C), BF), pltpu.VMEM((5, 2, 32, C), F32)],
-    )(
-        far, near, own, below, wa, ba, wb, bb, wd, bd, flags, bottom_hidden, bottom_mixed, top_taps, taps_far, taps_near
-    )
+    )(far, near, own, below, wa, ba, wb, bb, wd, flags, bottom_hidden, bottom_mixed, sums)
     return out[None]
 
 

time: 27.5 us -> 27.3 us (level)
  waiting for transfers between devices: 4.98 us -> 4.58 us
    ppermute x4, waiting for transfers between devices: 4.98 us -> 4.58 us  [shifted(): return lax.ppermute(x, axis, pairs)]
  transfers between devices with their start and end apart: 4 -> 4, of which waited for: 4 -> 4; matrix products, arithmetic and copies ran while one was open for 0% -> 0% of each run, Pallas kernels for 31% -> 33%
where the time goes in v6:
time: 27.3 us; the launch traced here: 27 us
  starting transfers between devices  11.7 us (43%)
  Pallas kernels  10.6 us (39%)
  waiting for transfers between devices  4.58 us (17%)
    ppermute x4, starting transfers between devices, shifted(): return lax.ppermute(x, axis, pairs)  11.7 us
    ppermute x4, waiting for transfers between devices, shifted(): return lax.ppermute(x, axis, pairs)  4.58 us
    pallas_call x1, Pallas kernels, per_device(): kernel(inner_near, [((4, 4, 32, 2 * C), BF), ((5, 3, 32, 2 * C), BF), ((3...  2.22 us
    pallas_call x1, Pallas kernels, per_device(): kernel(prepare, [packed, packed, ((3, 4, 32, 2 * C), BF), ((4, 8, C), F32...  1.77 us
    pallas_call x1, Pallas kernels, per_device(): kernel(bottom_part, [((2, 2, 8, 4 * C), BF)], [VMEM] * 13, [pltpu.VMEM((7...  1.74 us
    pallas_call x1, Pallas kernels, per_device(): kernel(top_part, [((128, C), F32)], [VMEM] * 15, [pltpu.VMEM((7, 2, 32, 2...  1.64 us
    pallas_call x1, Pallas kernels, per_device(): kernel(early_part, [sums_hidden, sums_mixed] * 2, [VMEM] * 8)  1.11 us
    pallas_call x1, Pallas kernels, per_device(): kernel(last_frames, [((2, 8, 32, C), BF)], [HBM], [pltpu.SemaphoreType.DM...  0.84 us
  transfers between devices with their start and end apart: 4, of which 4 were waited for; matrix products, arithmetic and copies ran while one was open for 0% of the time, Pallas kernels for 33%

profile of v6, /device:TPU:14, one launch (start us, length us, event | category | flops | bytes accessed | tf_op | source)
XLA Modules:
  0.0 27.0 jit_solution(4632075127137622305)
XLA Ops:
  0.0 0.0 copy-start.1
  0.0 0.0 copy-start.2
  0.0 2.0 %collective-permute-start.1 = (bf16[4,8,32,128]{3,2,1,0:T(8,128)(2,1)}, bf16[4,8,32,128]{3,2,1,0:T(8,128)(2,1)S(1)}, u32[]{:S(2)}, u32[]{:S(2)}) collective-permute-start(bf16[4,8,32,128]{3,2,1,0:T(8,128)(2,1)} %bitcast.19), channel_id=1, source_target_pairs={{0,4},{4,8},{8,12},{12,16},{16,20},{20,24},{24,28},{28,32},{32,36}... | collective-permute-start | bytes 786440 | tf_op jit(solution)/shard_map/ppermute | solution.py:18
  2.1 0.8 %last_frames.1 = bf16[2,8,32,128]{3,2,1,0:T(8,128)(2,1)S(1)} custom-call(bf16[4,8,32,128]{3,2,1,0:T(8,128)(2,1)} %bitcast.20), custom_call_target="tpu_custom_call" | custom-call | bytes 1024 | tf_op jit(solution)/shard_map/last_frames/pallas_call | solution.py:350
  2.9 3.8 %collective-permute-start = (bf16[2,8,32,128]{3,2,1,0:T(8,128)(2,1)S(1)}, bf16[2,8,32,128]{3,2,1,0:T(8,128)(2,1)S(1)}, u32[]{:S(2)}, u32[]{:S(2)}) collective-permute-start(bf16[2,8,32,128]{3,2,1,0:T(8,128)(2,1)S(1)} %last_frames.1), channel_id=1, source_target_pairs={{0,8},{4,12},{8,16},{12,20},{16,24},{20,28},{24,32},{28,36},{32,40... | collective-permute-start | bytes 393224 | tf_op jit(solution)/shard_map/ppermute | solution.py:18
  6.7 1.8 %prepare.1 = (bf16[1536,768]{1,0:T(8,128)(2,1)S(1)}, bf16[1536,768]{1,0:T(8,128)(2,1)S(1)}, bf16[3,4,32,256]{3,2,1,0:T(8,128)(2,1)S(1)}, f32[4,8,128]{2,1,0:T(8,128)S(1)}) custom-call(s32[16]{0:T(128)} %lengths.1, s32[16]{0:T(128)} %order.1, bf16[4,8,32,128]{3,2,1,0:T(8,128)(2,1)} %bitcast.21, bf16[27,128,128]{2,1,0:T(8,128)(2,1)} %bitcast.22, ...), custom_call_target="tpu_custom_call" | custom-call | bytes 1024 | tf_op jit(solution)/shard_map/prepare/pallas_call | solution.py:358
  8.5 3.3 %collective-permute-done.1.arrived = bf16[4,8,32,128]{3,2,1,0:T(8,128)(2,1)S(1)} collective-permute-done((bf16[4,8,32,128]{3,2,1,0:T(8,128)(2,1)}, bf16[4,8,32,128]{3,2,1,0:T(8,128)(2,1)S(1)}, u32[]{:S(2)}, u32[]{:S(2)}) %collective-permute-start.1) | collective-permute-done | bytes 262176 | tf_op jit(solution)/shard_map/ppermute | solution.py:18
  11.9 0.0 copy-done.1
  11.9 0.0 copy-done.2
  11.9 2.2 %inner_near.1 = (bf16[4,4,32,256]{3,2,1,0:T(8,128)(2,1)S(1)}, bf16[5,3,32,256]{3,2,1,0:T(8,128)(2,1)S(1)}, bf16[3,4,16,384]{3,2,1,0:T(8,128)(2,1)S(1)}) custom-call(bf16[4,8,32,128]{3,2,1,0:T(8,128)(2,1)S(1)} %collective-permute-done.1.arrived, bf16[3,4,32,256]{3,2,1,0:T(8,128)(2,1)S(1)} %get-tuple-element.18.own, ...), custom_call_target="tpu_custom_call" | custom-call | bytes 1024 | tf_op jit(solution)/shard_map/inner_near/pallas_call | solution.py:369
  14.1 0.6 %collective-permute-done.far = bf16[2,8,32,128]{3,2,1,0:T(8,128)(2,1)S(1)} collective-permute-done((bf16[2,8,32,128]{3,2,1,0:T(8,128)(2,1)S(1)}, bf16[2,8,32,128]{3,2,1,0:T(8,128)(2,1)S(1)}, u32[]{:S(2)}, u32[]{:S(2)}) %collective-permute-start) | collective-permute-done | bytes 131104 | tf_op jit(solution)/shard_map/ppermute | solution.py:18
  14.7 0.1 pack_up.1
  14.7 3.5 %collective-permute-start.3 = (bf16[9,3,32,128]{3,2,1,0:T(8,128)(2,1)S(1)}, bf16[9,3,32,128]{3,2,1,0:T(8,128)(2,1)S(1)}, u32[]{:S(2)}, u32[]{:S(2)}) collective-permute-start(bf16[9,3,32,128]{3,2,1,0:T(8,128)(2,1)S(1)} %get-tuple-element.28), channel_id=1, source_target_pairs={{0,1},{1,2},{2,3},{4,5},{5,6},{6,7},{8,9},{9,10},{10,11},{12,13},{... | collective-permute-start | bytes 663560 | tf_op jit(solution)/shard_map/ppermute | solution.py:18
  18.2 2.4 %collective-permute-start.2 = (bf16[9,2,32,128]{3,2,1,0:T(8,128)(2,1)S(1)}, bf16[9,2,32,128]{3,2,1,0:T(8,128)(2,1)S(1)}, u32[]{:S(2)}, u32[]{:S(2)}) collective-permute-start(bf16[9,2,32,128]{3,2,1,0:T(8,128)(2,1)S(1)} %pack_down.1), channel_id=1, source_target_pairs={{1,0},{2,1},{3,2},{5,4},{6,5},{7,6},{9,8},{10,9},{11,10},{13,12},{... | collective-permute-start | bytes 442376 | tf_op jit(solution)/shard_map/ppermute | solution.py:18
  20.6 0.7 %inner_far.1.hidden_far = bf16[2,3,32,256]{3,2,1,0:T(8,128)(2,1)S(1)} custom-call(bf16[2,4,32,256]{3,2,1,0:T(8,128)(2,1)S(1)} %get-tuple-element.24.far, bf16[4,4,32,256]{3,2,1,0:T(8,128)(2,1)S(1)} %get-tuple-element.22.near, bf16[1536,768]{1,0:T(8,128)(2,1)S(1)} %get-tuple-element.19.wa, f32[1,128]{1,0:T(1,128)S(1)} %bitcast.11, ...), custom_call_target="tpu_custom_call" | custom-call | bytes 1024 | tf_op jit(solution)/shard_map/inner_far/pallas_call | solution.py:381
  21.3 0.5 %inner_mixed.1.after.taps_far = bf16[2,4,16,384]{3,2,1,0:T(8,128)(2,1)S(1)} custom-call(bf16[4,4,32,256]{3,2,1,0:T(8,128)(2,1)S(1)} %get-tuple-element.22.near, bf16[1536,768]{1,0:T(8,128)(2,1)S(1)} %get-tuple-element.20.wb, f32[1,128]{1,0:T(1,128)S(1)} %bitcast.15, f32[4,8,128]{2,1,0:T(8,128)S(1)} %get-tuple-element.21.flags, ...), custom_call_target="tpu_custom_call" | custom-call | bytes 1024 | tf_op jit(solution)/shard_map/inner_mixed/pallas_call | solution.py:382
  21.8 0.0 copy-start
  21.9 0.0 copy-start.3
  21.9 1.1 %early_part.1 = (f32[224,256]{1,0:T(8,128)S(1)}, f32[160,256]{1,0:T(8,128)S(1)}, f32[224,256]{1,0:T(8,128)S(1)}, f32[160,256]{1,0:T(8,128)S(1)}) custom-call(bf16[2,4,32,256]{3,2,1,0:T(8,128)(2,1)S(1)} %get-tuple-element.24.far, bf16[4,4,32,256]{3,2,1,0:T(8,128)(2,1)S(1)} %get-tuple-element.22.near, bf16[3,4,32,256]{3,2,1,0:T(8,128)(2,1)S(1)} %get-tuple-element.18.own, ...), custom_call_target="tpu_custom_call" | custom-call | bytes 1024 | tf_op jit(solution)/shard_map/early_part/pallas_call | solution.py:387
  23.0 0.4 %collective-permute-done.3.above = bf16[9,3,32,128]{3,2,1,0:T(8,128)(2,1)S(1)} collective-permute-done((bf16[9,3,32,128]{3,2,1,0:T(8,128)(2,1)S(1)}, bf16[9,3,32,128]{3,2,1,0:T(8,128)(2,1)S(1)}, u32[]{:S(2)}, u32[]{:S(2)}) %collective-permute-start.3) | collective-permute-done | bytes 221216 | tf_op jit(solution)/shard_map/ppermute | solution.py:18
  23.4 0.0 copy-done
  23.4 0.0 copy-done.3
  23.4 1.6 %top_part.1.sums = f32[128,128]{1,0:T(8,128)S(1)} custom-call(bf16[2,4,32,256]{3,2,1,0:T(8,128)(2,1)S(1)} %get-tuple-element.24.far, bf16[4,4,32,256]{3,2,1,0:T(8,128)(2,1)S(1)} %get-tuple-element.22.near, bf16[3,4,32,256]{3,2,1,0:T(8,128)(2,1)S(1)} %get-tuple-element.18.own, bf16[9,3,32,128]{3,2,1,0:T(8,128)(2,1)S(1)} %collective-permute-done.3.above, ...), custom_call_target="tpu_custom_call" | custom-call | bytes 1024 | tf_op jit(solution)/shard_map/top_part/pallas_call | solution.py:390
  25.0 0.3 collective-permute-done.2.below
  25.3 1.7 %bottom_part.1 = bf16[2,2,8,512]{3,2,1,0:T(8,128)(2,1)} custom-call(bf16[2,4,32,256]{3,2,1,0:T(8,128)(2,1)S(1)} %get-tuple-element.24.far, bf16[4,4,32,256]{3,2,1,0:T(8,128)(2,1)S(1)} %get-tuple-element.22.near, bf16[3,4,32,256]{3,2,1,0:T(8,128)(2,1)S(1)} %get-tuple-element.18.own, bf16[9,2,32,128]{3,2,1,0:T(8,128)(2,1)S(1)} %collective-permute-done.2.below, ...), custom_call_target="tpu_custom_call" | custom-call | bytes 1024 | tf_op jit(solution)/shard_map/bottom_part/pallas_call | solution.py:396
  (1 shorter events, 0.0 us)
Async XLA Ops:
  0.0 11.9 %copy-start.1 = (f32[128]{0:T(128)S(1)}, f32[128]{0:T(128)}, u32[]{:S(2)}) copy-start(f32[128]{0:T(128)} %param.13) | copy-start | bytes 1540
  0.0 11.9 %copy-start.2 = (f32[128]{0:T(128)S(1)}, f32[128]{0:T(128)}, u32[]{:S(2)}) copy-start(f32[128]{0:T(128)} %param.15) | copy-start | bytes 1540
  0.0 11.9 %collective-permute-start.1 = (bf16[4,8,32,128]{3,2,1,0:T(8,128)(2,1)}, bf16[4,8,32,128]{3,2,1,0:T(8,128)(2,1)S(1)}, u32[]{:S(2)}, u32[]{:S(2)}) collective-permute-start(bf16[4,8,32,128]{3,2,1,0:T(8,128)(2,1)} %bitcast.19), channel_id=1, source_target_pairs={{0,4},{4,8},{8,12},{12,16},{16,20},{20,24},{24,28},{28,32},{32,36}... | collective-permute-start | bytes 786440 | tf_op jit(solution)/shard_map/ppermute | solution.py:18
  2.9 11.8 %collective-permute-start = (bf16[2,8,32,128]{3,2,1,0:T(8,128)(2,1)S(1)}, bf16[2,8,32,128]{3,2,1,0:T(8,128)(2,1)S(1)}, u32[]{:S(2)}, u32[]{:S(2)}) collective-permute-start(bf16[2,8,32,128]{3,2,1,0:T(8,128)(2,1)S(1)} %last_frames.1), channel_id=1, source_target_pairs={{0,8},{4,12},{8,16},{12,20},{16,24},{20,28},{24,32},{28,36},{32,40... | collective-permute-start | bytes 393224 | tf_op jit(solution)/shard_map/ppermute | solution.py:18
  14.7 8.7 %collective-permute-start.3 = (bf16[9,3,32,128]{3,2,1,0:T(8,128)(2,1)S(1)}, bf16[9,3,32,128]{3,2,1,0:T(8,128)(2,1)S(1)}, u32[]{:S(2)}, u32[]{:S(2)}) collective-permute-start(bf16[9,3,32,128]{3,2,1,0:T(8,128)(2,1)S(1)} %get-tuple-element.28), channel_id=1, source_target_pairs={{0,1},{1,2},{2,3},{4,5},{5,6},{6,7},{8,9},{9,10},{10,11},{12,13},{... | collective-permute-start | bytes 663560 | tf_op jit(solution)/shard_map/ppermute | solution.py:18
  18.2 7.0 %collective-permute-start.2 = (bf16[9,2,32,128]{3,2,1,0:T(8,128)(2,1)S(1)}, bf16[9,2,32,128]{3,2,1,0:T(8,128)(2,1)S(1)}, u32[]{:S(2)}, u32[]{:S(2)}) collective-permute-start(bf16[9,2,32,128]{3,2,1,0:T(8,128)(2,1)S(1)} %pack_down.1), channel_id=1, source_target_pairs={{1,0},{2,1},{3,2},{5,4},{6,5},{7,6},{9,8},{10,9},{11,10},{13,12},{... | collective-permute-start | bytes 442376 | tf_op jit(solution)/shard_map/ppermute | solution.py:18
  21.8 1.5 %copy-start = (bf16[3,3,3,128,128]{4,3,2,1,0:T(8,128)(2,1)S(1)}, bf16[3,3,3,128,128]{4,3,2,1,0:T(8,128)(2,1)}, u32[]{:S(2)}) copy-start(bf16[3,3,3,128,128]{4,3,2,1,0:T(8,128)(2,1)} %param.16) | copy-start | bytes 2654212
  21.9 1.5 %copy-start.3 = (f32[128]{0:T(128)S(1)}, f32[128]{0:T(128)}, u32[]{:S(2)}) copy-start(f32[128]{0:T(128)} %param.17) | copy-start | bytes 1540

commit v7 on v6

--- a/solution.py
+++ b/solution.py
@@ -233,13 +233,17 @@
     return hidden
 
 
-def early_part(far, near, own, wa, wb, hidden_far, hidden_near, after, top_hidden, top_mixed, bottom_hidden, bottom_mixed):
+def early_part(
+    far, near, own, wa, wb, wd, hidden_far, hidden_near, after, top_hidden, top_mixed, bottom_hidden, bottom_mixed, low
+):
     feature = own_feature(far, near, own)
     hidden = inner_hidden(hidden_far, hidden_near)
     top_hidden[...] = conv([(f, 1) for f in HIDDEN], feature, wa, (1,))
     top_mixed[...] = conv([(f, 1) for f in MIXED], hidden, wb, (1,))
     bottom_hidden[...] = conv([(f, 5) for f in HIDDEN], feature, wa, (0,))
     bottom_mixed[...] = conv([(f, 4) for f in MIXED], hidden, wb, (0,))
+    for t in range(3):
+        low[:, pl.ds(t * C, C)] = wd[pl.ds((9 * t + 3) * C, 6 * C), :]
 
 
 def top_part(
@@ -289,7 +293,7 @@
 
 
 def bottom_part(
-    far, near, own, below, wa, ba, wb, bb, wd, flags, part_hidden, part_mixed, sums, out, h, m
+    far, near, own, below, wa, ba, wb, bb, wlow, flags, part_hidden, part_mixed, sums, out, h, m
 ):
     def feature(f, g):
         return jnp.concatenate([below[f + 6, 0], below[f + 6, 1]], axis=1)
@@ -306,20 +310,14 @@
     total = conv(blocks, lambda f, q: h[f + 4], wb, (1,)) + part_mixed[...]
     mixed_blocks(blocks, total, own_feature(far, near, own), bb, flags, put_mixed)
     rows = [jnp.concatenate([column_taps(m.at[f, r]) for r in range(2)], axis=1) for f in range(5)]
-    low = sum(
-        jnp.dot(
-            jnp.concatenate([rows[t], rows[t + 2]], axis=0),
-            wd[pl.ds((9 * t + 3) * C, 6 * C), :],
-            preferred_element_type=F32,
-        )
-        for t in range(3)
-    )
+    y = jnp.dot(jnp.concatenate(rows, axis=0), wlow[...], preferred_element_type=F32)
+    low = [sum(y[(2 * t + k) * 16 : (2 * t + k) * 16 + 16, k * C : k * C + C] for k in range(3)) for t in range(2)]
     for t in range(2):
         for i in range(2):
             at = t * 64 + i * 32
             v = sums[at : at + 32]
             if i == 1:
-                v = jnp.concatenate([v[:16], v[16:] + low[t * 16 : t * 16 + 16]], axis=0)
+                v = jnp.concatenate([v[:16], v[16:] + low[t]], axis=0)
             out[t, i] = jnp.concatenate([v[k * 8 : k * 8 + 8] for k in range(4)], axis=1).astype(BF)
 
 
@@ -384,9 +382,9 @@
     )(near, wb, bb, flags, hidden_far, hidden_near)
     sums_hidden = ((7 * 32, 2 * C), F32)
     sums_mixed = ((5 * 32, 2 * C), F32)
-    top_hidden, top_mixed, bottom_hidden, bottom_mixed = kernel(
-        early_part, [sums_hidden, sums_mixed] * 2, [VMEM] * 8
-    )(far, near, own, wa, wb, hidden_far, hidden_near, taps_far)
+    top_hidden, top_mixed, bottom_hidden, bottom_mixed, wlow = kernel(
+        early_part, [sums_hidden, sums_mixed] * 2 + [((6 * C, 3 * C), BF)], [VMEM] * 9
+    )(far, near, own, wa, wb, wd, hidden_far, hidden_near, taps_far)
     (sums,) = kernel(
         top_part,
         [((128, C), F32)],
@@ -398,7 +396,7 @@
         [((2, 2, 8, 4 * C), BF)],
         [VMEM] * 13,
         [pltpu.VMEM((7, 32, 2 * C), BF), pltpu.VMEM((5, 2, 32, C), F32)],
-    )(far, near, own, below, wa, ba, wb, bb, wd, flags, bottom_hidden, bottom_mixed, sums)
+    )(far, near, own, below, wa, ba, wb, bb, wlow, flags, bottom_hidden, bottom_mixed, sums)
     return out[None]
 
 

time: 27.3 us -> 27.5 us (level)
  transfers between devices with their start and end apart: 4 -> 4, of which waited for: 4 -> 4; matrix products, arithmetic and copies ran while one was open for 0% -> 0% of each run, Pallas kernels for 33% -> 32%
where the time goes in v7:
time: 27.5 us; the launch traced here: 27.2 us
  starting transfers between devices  11.9 us (43%)
  Pallas kernels  10.6 us (39%)
  waiting for transfers between devices  4.6 us (17%)
    ppermute x4, starting transfers between devices, shifted(): return lax.ppermute(x, axis, pairs)  11.9 us
    ppermute x4, waiting for transfers between devices, shifted(): return lax.ppermute(x, axis, pairs)  4.6 us
    pallas_call x1, Pallas kernels, per_device(): kernel(inner_near, [((4, 4, 32, 2 * C), BF), ((5, 3, 32, 2 * C), BF), ((3...  2.2 us
    pallas_call x1, Pallas kernels, per_device(): kernel(prepare, [packed, packed, ((3, 4, 32, 2 * C), BF), ((4, 8, C), F32...  1.77 us
    pallas_call x1, Pallas kernels, per_device(): kernel(bottom_part, [((2, 2, 8, 4 * C), BF)], [VMEM] * 13, [pltpu.VMEM((7...  1.76 us
    pallas_call x1, Pallas kernels, per_device(): kernel(top_part, [((128, C), F32)], [VMEM] * 15, [pltpu.VMEM((7, 2, 32, 2...  1.62 us
    pallas_call x1, Pallas kernels, per_device(): kernel(early_part, [sums_hidden, sums_mixed] * 2 + [((6 * C, 3 * C), BF)]...  1.12 us
    pallas_call x1, Pallas kernels, per_device(): kernel(last_frames, [((2, 8, 32, C), BF)], [HBM], [pltpu.SemaphoreType.DM...  0.84 us
  transfers between devices with their start and end apart: 4, of which 4 were waited for; matrix products, arithmetic and copies ran while one was open for 0% of the time, Pallas kernels for 32%

profile of v7, /device:TPU:14, one launch (start us, length us, event | category | flops | bytes accessed | tf_op | source)
XLA Modules:
  0.0 27.2 jit_solution(4227824261054803996)
XLA Ops:
  0.0 0.0 copy-start.1
  0.0 0.0 copy-start.2
  0.0 2.0 %collective-permute-start.1 = (bf16[4,8,32,128]{3,2,1,0:T(8,128)(2,1)}, bf16[4,8,32,128]{3,2,1,0:T(8,128)(2,1)S(1)}, u32[]{:S(2)}, u32[]{:S(2)}) collective-permute-start(bf16[4,8,32,128]{3,2,1,0:T(8,128)(2,1)} %bitcast.19), channel_id=1, source_target_pairs={{0,4},{4,8},{8,12},{12,16},{16,20},{20,24},{24,28},{28,32},{32,36}... | collective-permute-start | bytes 786440 | tf_op jit(solution)/shard_map/ppermute | solution.py:18
  2.1 0.8 %last_frames.1 = bf16[2,8,32,128]{3,2,1,0:T(8,128)(2,1)S(1)} custom-call(bf16[4,8,32,128]{3,2,1,0:T(8,128)(2,1)} %bitcast.20), custom_call_target="tpu_custom_call" | custom-call | bytes 1024 | tf_op jit(solution)/shard_map/last_frames/pallas_call | solution.py:348
  2.9 3.8 %collective-permute-start = (bf16[2,8,32,128]{3,2,1,0:T(8,128)(2,1)S(1)}, bf16[2,8,32,128]{3,2,1,0:T(8,128)(2,1)S(1)}, u32[]{:S(2)}, u32[]{:S(2)}) collective-permute-start(bf16[2,8,32,128]{3,2,1,0:T(8,128)(2,1)S(1)} %last_frames.1), channel_id=1, source_target_pairs={{0,8},{4,12},{8,16},{12,20},{16,24},{20,28},{24,32},{28,36},{32,40... | collective-permute-start | bytes 393224 | tf_op jit(solution)/shard_map/ppermute | solution.py:18
  6.7 1.8 %prepare.1 = (bf16[1536,768]{1,0:T(8,128)(2,1)S(1)}, bf16[1536,768]{1,0:T(8,128)(2,1)S(1)}, bf16[3,4,32,256]{3,2,1,0:T(8,128)(2,1)S(1)}, f32[4,8,128]{2,1,0:T(8,128)S(1)}) custom-call(s32[16]{0:T(128)} %lengths.1, s32[16]{0:T(128)} %order.1, bf16[4,8,32,128]{3,2,1,0:T(8,128)(2,1)} %bitcast.21, bf16[27,128,128]{2,1,0:T(8,128)(2,1)} %bitcast.22, ...), custom_call_target="tpu_custom_call" | custom-call | bytes 1024 | tf_op jit(solution)/shard_map/prepare/pallas_call | solution.py:356
  8.5 3.3 %collective-permute-done.1.arrived = bf16[4,8,32,128]{3,2,1,0:T(8,128)(2,1)S(1)} collective-permute-done((bf16[4,8,32,128]{3,2,1,0:T(8,128)(2,1)}, bf16[4,8,32,128]{3,2,1,0:T(8,128)(2,1)S(1)}, u32[]{:S(2)}, u32[]{:S(2)}) %collective-permute-start.1) | collective-permute-done | bytes 262176 | tf_op jit(solution)/shard_map/ppermute | solution.py:18
  11.9 0.0 copy-done.1
  11.9 0.0 copy-done.2
  11.9 2.2 %inner_near.1 = (bf16[4,4,32,256]{3,2,1,0:T(8,128)(2,1)S(1)}, bf16[5,3,32,256]{3,2,1,0:T(8,128)(2,1)S(1)}, bf16[3,4,16,384]{3,2,1,0:T(8,128)(2,1)S(1)}) custom-call(bf16[4,8,32,128]{3,2,1,0:T(8,128)(2,1)S(1)} %collective-permute-done.1.arrived, bf16[3,4,32,256]{3,2,1,0:T(8,128)(2,1)S(1)} %get-tuple-element.19.own, ...), custom_call_target="tpu_custom_call" | custom-call | bytes 1024 | tf_op jit(solution)/shard_map/inner_near/pallas_call | solution.py:367
  14.1 0.6 %collective-permute-done.far = bf16[2,8,32,128]{3,2,1,0:T(8,128)(2,1)S(1)} collective-permute-done((bf16[2,8,32,128]{3,2,1,0:T(8,128)(2,1)S(1)}, bf16[2,8,32,128]{3,2,1,0:T(8,128)(2,1)S(1)}, u32[]{:S(2)}, u32[]{:S(2)}) %collective-permute-start) | collective-permute-done | bytes 131104 | tf_op jit(solution)/shard_map/ppermute | solution.py:18
  14.7 0.1 pack_up.1
  14.7 3.5 %collective-permute-start.3 = (bf16[9,3,32,128]{3,2,1,0:T(8,128)(2,1)S(1)}, bf16[9,3,32,128]{3,2,1,0:T(8,128)(2,1)S(1)}, u32[]{:S(2)}, u32[]{:S(2)}) collective-permute-start(bf16[9,3,32,128]{3,2,1,0:T(8,128)(2,1)S(1)} %get-tuple-element.30), channel_id=1, source_target_pairs={{0,1},{1,2},{2,3},{4,5},{5,6},{6,7},{8,9},{9,10},{10,11},{12,13},{... | collective-permute-start | bytes 663560 | tf_op jit(solution)/shard_map/ppermute | solution.py:18
  18.2 0.0 copy-start
  18.3 2.5 %collective-permute-start.2 = (bf16[9,2,32,128]{3,2,1,0:T(8,128)(2,1)S(1)}, bf16[9,2,32,128]{3,2,1,0:T(8,128)(2,1)S(1)}, u32[]{:S(2)}, u32[]{:S(2)}) collective-permute-start(bf16[9,2,32,128]{3,2,1,0:T(8,128)(2,1)S(1)} %pack_down.1), channel_id=1, source_target_pairs={{1,0},{2,1},{3,2},{5,4},{6,5},{7,6},{9,8},{10,9},{11,10},{13,12},{... | collective-permute-start | bytes 442376 | tf_op jit(solution)/shard_map/ppermute | solution.py:18
  20.8 0.7 %inner_far.1.hidden_far = bf16[2,3,32,256]{3,2,1,0:T(8,128)(2,1)S(1)} custom-call(bf16[2,4,32,256]{3,2,1,0:T(8,128)(2,1)S(1)} %get-tuple-element.25.far, bf16[4,4,32,256]{3,2,1,0:T(8,128)(2,1)S(1)} %get-tuple-element.23.near, bf16[1536,768]{1,0:T(8,128)(2,1)S(1)} %get-tuple-element.20.wa, f32[1,128]{1,0:T(1,128)S(1)} %bitcast.11, ...), custom_call_target="tpu_custom_call" | custom-call | bytes 1024 | tf_op jit(solution)/shard_map/inner_far/pallas_call | solution.py:379
  21.5 0.5 %inner_mixed.1.after.taps_far = bf16[2,4,16,384]{3,2,1,0:T(8,128)(2,1)S(1)} custom-call(bf16[4,4,32,256]{3,2,1,0:T(8,128)(2,1)S(1)} %get-tuple-element.23.near, bf16[1536,768]{1,0:T(8,128)(2,1)S(1)} %get-tuple-element.21.wb, f32[1,128]{1,0:T(1,128)S(1)} %bitcast.15, f32[4,8,128]{2,1,0:T(8,128)S(1)} %get-tuple-element.22.flags, ...), custom_call_target="tpu_custom_call" | custom-call | bytes 1024 | tf_op jit(solution)/shard_map/inner_mixed/pallas_call | solution.py:380
  22.0 0.0 copy-done
  22.0 0.0 copy-start.3
  22.0 1.1 %early_part.1 = (f32[224,256]{1,0:T(8,128)S(1)}, f32[160,256]{1,0:T(8,128)S(1)}, f32[224,256]{1,0:T(8,128)S(1)}, f32[160,256]{1,0:T(8,128)S(1)}, bf16[768,384]{1,0:T(8,128)(2,1)S(1)}) custom-call(bf16[2,4,32,256]{3,2,1,0:T(8,128)(2,1)S(1)} %get-tuple-element.25.far, bf16[4,4,32,256]{3,2,1,0:T(8,128)(2,1)S(1)} %get-tuple-element.23.near, ...), custom_call_target="tpu_custom_call" | custom-call | bytes 1024 | tf_op jit(solution)/shard_map/early_part/pallas_call | solution.py:385
  23.1 0.2 collective-permute-done.3.above
  23.4 0.0 copy-done.3
  23.4 1.6 %top_part.1.sums = f32[128,128]{1,0:T(8,128)S(1)} custom-call(bf16[2,4,32,256]{3,2,1,0:T(8,128)(2,1)S(1)} %get-tuple-element.25.far, bf16[4,4,32,256]{3,2,1,0:T(8,128)(2,1)S(1)} %get-tuple-element.23.near, bf16[3,4,32,256]{3,2,1,0:T(8,128)(2,1)S(1)} %get-tuple-element.19.own, bf16[9,3,32,128]{3,2,1,0:T(8,128)(2,1)S(1)} %collective-permute-done.3.above, ...), custom_call_target="tpu_custom_call" | custom-call | bytes 1024 | tf_op jit(solution)/shard_map/top_part/pallas_call | solution.py:388
  25.0 0.4 %collective-permute-done.2.below = bf16[9,2,32,128]{3,2,1,0:T(8,128)(2,1)S(1)} collective-permute-done((bf16[9,2,32,128]{3,2,1,0:T(8,128)(2,1)S(1)}, bf16[9,2,32,128]{3,2,1,0:T(8,128)(2,1)S(1)}, u32[]{:S(2)}, u32[]{:S(2)}) %collective-permute-start.2) | collective-permute-done | bytes 147488 | tf_op jit(solution)/shard_map/ppermute | solution.py:18
  25.4 1.8 %bottom_part.1 = bf16[2,2,8,512]{3,2,1,0:T(8,128)(2,1)} custom-call(bf16[2,4,32,256]{3,2,1,0:T(8,128)(2,1)S(1)} %get-tuple-element.25.far, bf16[4,4,32,256]{3,2,1,0:T(8,128)(2,1)S(1)} %get-tuple-element.23.near, bf16[3,4,32,256]{3,2,1,0:T(8,128)(2,1)S(1)} %get-tuple-element.19.own, bf16[9,2,32,128]{3,2,1,0:T(8,128)(2,1)S(1)} %collective-permute-done.2.below, ...), custom_call_target="tpu_custom_call" | custom-call | bytes 1024 | tf_op jit(solution)/shard_map/bottom_part/pallas_call | solution.py:394
  (1 shorter events, 0.0 us)
Async XLA Ops:
  0.0 11.9 %copy-start.1 = (f32[128]{0:T(128)S(1)}, f32[128]{0:T(128)}, u32[]{:S(2)}) copy-start(f32[128]{0:T(128)} %param.13) | copy-start | bytes 1540
  0.0 11.9 %copy-start.2 = (f32[128]{0:T(128)S(1)}, f32[128]{0:T(128)}, u32[]{:S(2)}) copy-start(f32[128]{0:T(128)} %param.15) | copy-start | bytes 1540
  0.0 11.9 %collective-permute-start.1 = (bf16[4,8,32,128]{3,2,1,0:T(8,128)(2,1)}, bf16[4,8,32,128]{3,2,1,0:T(8,128)(2,1)S(1)}, u32[]{:S(2)}, u32[]{:S(2)}) collective-permute-start(bf16[4,8,32,128]{3,2,1,0:T(8,128)(2,1)} %bitcast.19), channel_id=1, source_target_pairs={{0,4},{4,8},{8,12},{12,16},{16,20},{20,24},{24,28},{28,32},{32,36}... | collective-permute-start | bytes 786440 | tf_op jit(solution)/shard_map/ppermute | solution.py:18
  2.9 11.8 %collective-permute-start = (bf16[2,8,32,128]{3,2,1,0:T(8,128)(2,1)S(1)}, bf16[2,8,32,128]{3,2,1,0:T(8,128)(2,1)S(1)}, u32[]{:S(2)}, u32[]{:S(2)}) collective-permute-start(bf16[2,8,32,128]{3,2,1,0:T(8,128)(2,1)S(1)} %last_frames.1), channel_id=1, source_target_pairs={{0,8},{4,12},{8,16},{12,20},{16,24},{20,28},{24,32},{28,36},{32,40... | collective-permute-start | bytes 393224 | tf_op jit(solution)/shard_map/ppermute | solution.py:18
  14.7 8.7 %collective-permute-start.3 = (bf16[9,3,32,128]{3,2,1,0:T(8,128)(2,1)S(1)}, bf16[9,3,32,128]{3,2,1,0:T(8,128)(2,1)S(1)}, u32[]{:S(2)}, u32[]{:S(2)}) collective-permute-start(bf16[9,3,32,128]{3,2,1,0:T(8,128)(2,1)S(1)} %get-tuple-element.30), channel_id=1, source_target_pairs={{0,1},{1,2},{2,3},{4,5},{5,6},{6,7},{8,9},{9,10},{10,11},{12,13},{... | collective-permute-start | bytes 663560 | tf_op jit(solution)/shard_map/ppermute | solution.py:18
  18.2 3.7 %copy-start = (bf16[3,3,3,128,128]{4,3,2,1,0:T(8,128)(2,1)S(1)}, bf16[3,3,3,128,128]{4,3,2,1,0:T(8,128)(2,1)}, u32[]{:S(2)}) copy-start(bf16[3,3,3,128,128]{4,3,2,1,0:T(8,128)(2,1)} %param.16) | copy-start | bytes 2654212
  18.3 7.2 %collective-permute-start.2 = (bf16[9,2,32,128]{3,2,1,0:T(8,128)(2,1)S(1)}, bf16[9,2,32,128]{3,2,1,0:T(8,128)(2,1)S(1)}, u32[]{:S(2)}, u32[]{:S(2)}) collective-permute-start(bf16[9,2,32,128]{3,2,1,0:T(8,128)(2,1)S(1)} %pack_down.1), channel_id=1, source_target_pairs={{1,0},{2,1},{3,2},{5,4},{6,5},{7,6},{9,8},{10,9},{11,10},{13,12},{... | collective-permute-start | bytes 442376 | tf_op jit(solution)/shard_map/ppermute | solution.py:18
  22.0 1.4 %copy-start.3 = (f32[128]{0:T(128)S(1)}, f32[128]{0:T(128)}, u32[]{:S(2)}) copy-start(f32[128]{0:T(128)} %param.17) | copy-start | bytes 1540

commit v8 on v7

--- a/solution.py
+++ b/solution.py
@@ -276,12 +276,13 @@
     hidden_blocks(blocks, conv(blocks, feature, wa, lower=True), ba, flags, put_hidden)
     blocks = [(f, 1) for f in MIXED]
     mixed_blocks(blocks, conv(blocks, hidden, wb, (0,)) + part_mixed[...], feature, bb, flags, put_mixed)
+    ready = [[column_taps(m.at[f, r]) for r in (1, 2)] for f in range(5)]
     blocks = [(f, 0) for f in MIXED]
     mixed_blocks(blocks, conv(blocks, hidden, wb, lower=True), feature, bb, flags, put_mixed)
     none = jnp.zeros((16, 3 * C), BF)
     frames = []
     for f in range(5):
-        rows = [column_taps(m.at[f, r]) for r in range(3)]
+        rows = [column_taps(m.at[f, 0])] + ready[f]
         rows += [taps_far[f, r] if f < 2 else taps_near[f - 2, r] for r in range(4)] + [none, none]
         frames.append(
             jnp.concatenate(

time: 27.5 us -> 27.5 us (level)
  no operation moved by 1% of the time
where the time goes in v8:
time: 27.5 us; the launch traced here: 27.2 us
  starting transfers between devices  11.9 us (43%)
  Pallas kernels  10.6 us (39%)
  waiting for transfers between devices  4.6 us (17%)
    ppermute x4, starting transfers between devices, shifted(): return lax.ppermute(x, axis, pairs)  11.9 us
    ppermute x4, waiting for transfers between devices, shifted(): return lax.ppermute(x, axis, pairs)  4.6 us
    pallas_call x1, Pallas kernels, per_device(): kernel(inner_near, [((4, 4, 32, 2 * C), BF), ((5, 3, 32, 2 * C), BF), ((3...  2.2 us
    pallas_call x1, Pallas kernels, per_device(): kernel(prepare, [packed, packed, ((3, 4, 32, 2 * C), BF), ((4, 8, C), F32...  1.77 us
    pallas_call x1, Pallas kernels, per_device(): kernel(bottom_part, [((2, 2, 8, 4 * C), BF)], [VMEM] * 13, [pltpu.VMEM((7...  1.76 us
    pallas_call x1, Pallas kernels, per_device(): kernel(top_part, [((128, C), F32)], [VMEM] * 15, [pltpu.VMEM((7, 2, 32, 2...  1.62 us
    pallas_call x1, Pallas kernels, per_device(): kernel(early_part, [sums_hidden, sums_mixed] * 2 + [((6 * C, 3 * C), BF)]...  1.12 us
    pallas_call x1, Pallas kernels, per_device(): kernel(last_frames, [((2, 8, 32, C), BF)], [HBM], [pltpu.SemaphoreType.DM...  0.84 us
  transfers between devices with their start and end apart: 4, of which 4 were waited for; matrix products, arithmetic and copies ran while one was open for 0% of the time, Pallas kernels for 32%

profile of v8, /device:TPU:14, one launch (start us, length us, event | category | flops | bytes accessed | tf_op | source)
XLA Modules:
  0.0 27.2 jit_solution(4227824261054803996)
XLA Ops:
  0.0 0.0 copy-start.1
  0.0 0.0 copy-start.2
  0.0 2.0 %collective-permute-start.1 = (bf16[4,8,32,128]{3,2,1,0:T(8,128)(2,1)}, bf16[4,8,32,128]{3,2,1,0:T(8,128)(2,1)S(1)}, u32[]{:S(2)}, u32[]{:S(2)}) collective-permute-start(bf16[4,8,32,128]{3,2,1,0:T(8,128)(2,1)} %bitcast.19), channel_id=1, source_target_pairs={{0,4},{4,8},{8,12},{12,16},{16,20},{20,24},{24,28},{28,32},{32,36}... | collective-permute-start | bytes 786440 | tf_op jit(solution)/shard_map/ppermute | solution.py:18
  2.1 0.8 %last_frames.1 = bf16[2,8,32,128]{3,2,1,0:T(8,128)(2,1)S(1)} custom-call(bf16[4,8,32,128]{3,2,1,0:T(8,128)(2,1)} %bitcast.20), custom_call_target="tpu_custom_call" | custom-call | bytes 1024 | tf_op jit(solution)/shard_map/last_frames/pallas_call | solution.py:349
  2.9 3.8 %collective-permute-start = (bf16[2,8,32,128]{3,2,1,0:T(8,128)(2,1)S(1)}, bf16[2,8,32,128]{3,2,1,0:T(8,128)(2,1)S(1)}, u32[]{:S(2)}, u32[]{:S(2)}) collective-permute-start(bf16[2,8,32,128]{3,2,1,0:T(8,128)(2,1)S(1)} %last_frames.1), channel_id=1, source_target_pairs={{0,8},{4,12},{8,16},{12,20},{16,24},{20,28},{24,32},{28,36},{32,40... | collective-permute-start | bytes 393224 | tf_op jit(solution)/shard_map/ppermute | solution.py:18
  6.7 1.8 %prepare.1 = (bf16[1536,768]{1,0:T(8,128)(2,1)S(1)}, bf16[1536,768]{1,0:T(8,128)(2,1)S(1)}, bf16[3,4,32,256]{3,2,1,0:T(8,128)(2,1)S(1)}, f32[4,8,128]{2,1,0:T(8,128)S(1)}) custom-call(s32[16]{0:T(128)} %lengths.1, s32[16]{0:T(128)} %order.1, bf16[4,8,32,128]{3,2,1,0:T(8,128)(2,1)} %bitcast.21, bf16[27,128,128]{2,1,0:T(8,128)(2,1)} %bitcast.22, ...), custom_call_target="tpu_custom_call" | custom-call | bytes 1024 | tf_op jit(solution)/shard_map/prepare/pallas_call | solution.py:357
  8.5 3.3 %collective-permute-done.1.arrived = bf16[4,8,32,128]{3,2,1,0:T(8,128)(2,1)S(1)} collective-permute-done((bf16[4,8,32,128]{3,2,1,0:T(8,128)(2,1)}, bf16[4,8,32,128]{3,2,1,0:T(8,128)(2,1)S(1)}, u32[]{:S(2)}, u32[]{:S(2)}) %collective-permute-start.1) | collective-permute-done | bytes 262176 | tf_op jit(solution)/shard_map/ppermute | solution.py:18
  11.9 0.0 copy-done.1
  11.9 0.0 copy-done.2
  11.9 2.2 %inner_near.1 = (bf16[4,4,32,256]{3,2,1,0:T(8,128)(2,1)S(1)}, bf16[5,3,32,256]{3,2,1,0:T(8,128)(2,1)S(1)}, bf16[3,4,16,384]{3,2,1,0:T(8,128)(2,1)S(1)}) custom-call(bf16[4,8,32,128]{3,2,1,0:T(8,128)(2,1)S(1)} %collective-permute-done.1.arrived, bf16[3,4,32,256]{3,2,1,0:T(8,128)(2,1)S(1)} %get-tuple-element.19.own, ...), custom_call_target="tpu_custom_call" | custom-call | bytes 1024 | tf_op jit(solution)/shard_map/inner_near/pallas_call | solution.py:368
  14.1 0.6 %collective-permute-done.far = bf16[2,8,32,128]{3,2,1,0:T(8,128)(2,1)S(1)} collective-permute-done((bf16[2,8,32,128]{3,2,1,0:T(8,128)(2,1)S(1)}, bf16[2,8,32,128]{3,2,1,0:T(8,128)(2,1)S(1)}, u32[]{:S(2)}, u32[]{:S(2)}) %collective-permute-start) | collective-permute-done | bytes 131104 | tf_op jit(solution)/shard_map/ppermute | solution.py:18
  14.7 0.1 pack_up.1
  14.7 3.5 %collective-permute-start.3 = (bf16[9,3,32,128]{3,2,1,0:T(8,128)(2,1)S(1)}, bf16[9,3,32,128]{3,2,1,0:T(8,128)(2,1)S(1)}, u32[]{:S(2)}, u32[]{:S(2)}) collective-permute-start(bf16[9,3,32,128]{3,2,1,0:T(8,128)(2,1)S(1)} %get-tuple-element.30), channel_id=1, source_target_pairs={{0,1},{1,2},{2,3},{4,5},{5,6},{6,7},{8,9},{9,10},{10,11},{12,13},{... | collective-permute-start | bytes 663560 | tf_op jit(solution)/shard_map/ppermute | solution.py:18
  18.2 0.0 copy-start
  18.3 2.5 %collective-permute-start.2 = (bf16[9,2,32,128]{3,2,1,0:T(8,128)(2,1)S(1)}, bf16[9,2,32,128]{3,2,1,0:T(8,128)(2,1)S(1)}, u32[]{:S(2)}, u32[]{:S(2)}) collective-permute-start(bf16[9,2,32,128]{3,2,1,0:T(8,128)(2,1)S(1)} %pack_down.1), channel_id=1, source_target_pairs={{1,0},{2,1},{3,2},{5,4},{6,5},{7,6},{9,8},{10,9},{11,10},{13,12},{... | collective-permute-start | bytes 442376 | tf_op jit(solution)/shard_map/ppermute | solution.py:18
  20.8 0.7 %inner_far.1.hidden_far = bf16[2,3,32,256]{3,2,1,0:T(8,128)(2,1)S(1)} custom-call(bf16[2,4,32,256]{3,2,1,0:T(8,128)(2,1)S(1)} %get-tuple-element.25.far, bf16[4,4,32,256]{3,2,1,0:T(8,128)(2,1)S(1)} %get-tuple-element.23.near, bf16[1536,768]{1,0:T(8,128)(2,1)S(1)} %get-tuple-element.20.wa, f32[1,128]{1,0:T(1,128)S(1)} %bitcast.11, ...), custom_call_target="tpu_custom_call" | custom-call | bytes 1024 | tf_op jit(solution)/shard_map/inner_far/pallas_call | solution.py:380
  21.5 0.5 %inner_mixed.1.after.taps_far = bf16[2,4,16,384]{3,2,1,0:T(8,128)(2,1)S(1)} custom-call(bf16[4,4,32,256]{3,2,1,0:T(8,128)(2,1)S(1)} %get-tuple-element.23.near, bf16[1536,768]{1,0:T(8,128)(2,1)S(1)} %get-tuple-element.21.wb, f32[1,128]{1,0:T(1,128)S(1)} %bitcast.15, f32[4,8,128]{2,1,0:T(8,128)S(1)} %get-tuple-element.22.flags, ...), custom_call_target="tpu_custom_call" | custom-call | bytes 1024 | tf_op jit(solution)/shard_map/inner_mixed/pallas_call | solution.py:381
  22.0 0.0 copy-done
  22.0 0.0 copy-start.3
  22.0 1.1 %early_part.1 = (f32[224,256]{1,0:T(8,128)S(1)}, f32[160,256]{1,0:T(8,128)S(1)}, f32[224,256]{1,0:T(8,128)S(1)}, f32[160,256]{1,0:T(8,128)S(1)}, bf16[768,384]{1,0:T(8,128)(2,1)S(1)}) custom-call(bf16[2,4,32,256]{3,2,1,0:T(8,128)(2,1)S(1)} %get-tuple-element.25.far, bf16[4,4,32,256]{3,2,1,0:T(8,128)(2,1)S(1)} %get-tuple-element.23.near, ...), custom_call_target="tpu_custom_call" | custom-call | bytes 1024 | tf_op jit(solution)/shard_map/early_part/pallas_call | solution.py:386
  23.1 0.2 collective-permute-done.3.above
  23.4 0.0 copy-done.3
  23.4 1.6 %top_part.1.sums = f32[128,128]{1,0:T(8,128)S(1)} custom-call(bf16[2,4,32,256]{3,2,1,0:T(8,128)(2,1)S(1)} %get-tuple-element.25.far, bf16[4,4,32,256]{3,2,1,0:T(8,128)(2,1)S(1)} %get-tuple-element.23.near, bf16[3,4,32,256]{3,2,1,0:T(8,128)(2,1)S(1)} %get-tuple-element.19.own, bf16[9,3,32,128]{3,2,1,0:T(8,128)(2,1)S(1)} %collective-permute-done.3.above, ...), custom_call_target="tpu_custom_call" | custom-call | bytes 1024 | tf_op jit(solution)/shard_map/top_part/pallas_call | solution.py:389
  25.0 0.4 %collective-permute-done.2.below = bf16[9,2,32,128]{3,2,1,0:T(8,128)(2,1)S(1)} collective-permute-done((bf16[9,2,32,128]{3,2,1,0:T(8,128)(2,1)S(1)}, bf16[9,2,32,128]{3,2,1,0:T(8,128)(2,1)S(1)}, u32[]{:S(2)}, u32[]{:S(2)}) %collective-permute-start.2) | collective-permute-done | bytes 147488 | tf_op jit(solution)/shard_map/ppermute | solution.py:18
  25.4 1.8 %bottom_part.1 = bf16[2,2,8,512]{3,2,1,0:T(8,128)(2,1)} custom-call(bf16[2,4,32,256]{3,2,1,0:T(8,128)(2,1)S(1)} %get-tuple-element.25.far, bf16[4,4,32,256]{3,2,1,0:T(8,128)(2,1)S(1)} %get-tuple-element.23.near, bf16[3,4,32,256]{3,2,1,0:T(8,128)(2,1)S(1)} %get-tuple-element.19.own, bf16[9,2,32,128]{3,2,1,0:T(8,128)(2,1)S(1)} %collective-permute-done.2.below, ...), custom_call_target="tpu_custom_call" | custom-call | bytes 1024 | tf_op jit(solution)/shard_map/bottom_part/pallas_call | solution.py:395
  (1 shorter events, 0.0 us)
Async XLA Ops:
  0.0 11.9 %copy-start.1 = (f32[128]{0:T(128)S(1)}, f32[128]{0:T(128)}, u32[]{:S(2)}) copy-start(f32[128]{0:T(128)} %param.13) | copy-start | bytes 1540
  0.0 11.9 %copy-start.2 = (f32[128]{0:T(128)S(1)}, f32[128]{0:T(128)}, u32[]{:S(2)}) copy-start(f32[128]{0:T(128)} %param.15) | copy-start | bytes 1540
  0.0 11.9 %collective-permute-start.1 = (bf16[4,8,32,128]{3,2,1,0:T(8,128)(2,1)}, bf16[4,8,32,128]{3,2,1,0:T(8,128)(2,1)S(1)}, u32[]{:S(2)}, u32[]{:S(2)}) collective-permute-start(bf16[4,8,32,128]{3,2,1,0:T(8,128)(2,1)} %bitcast.19), channel_id=1, source_target_pairs={{0,4},{4,8},{8,12},{12,16},{16,20},{20,24},{24,28},{28,32},{32,36}... | collective-permute-start | bytes 786440 | tf_op jit(solution)/shard_map/ppermute | solution.py:18
  2.9 11.8 %collective-permute-start = (bf16[2,8,32,128]{3,2,1,0:T(8,128)(2,1)S(1)}, bf16[2,8,32,128]{3,2,1,0:T(8,128)(2,1)S(1)}, u32[]{:S(2)}, u32[]{:S(2)}) collective-permute-start(bf16[2,8,32,128]{3,2,1,0:T(8,128)(2,1)S(1)} %last_frames.1), channel_id=1, source_target_pairs={{0,8},{4,12},{8,16},{12,20},{16,24},{20,28},{24,32},{28,36},{32,40... | collective-permute-start | bytes 393224 | tf_op jit(solution)/shard_map/ppermute | solution.py:18
  14.7 8.7 %collective-permute-start.3 = (bf16[9,3,32,128]{3,2,1,0:T(8,128)(2,1)S(1)}, bf16[9,3,32,128]{3,2,1,0:T(8,128)(2,1)S(1)}, u32[]{:S(2)}, u32[]{:S(2)}) collective-permute-start(bf16[9,3,32,128]{3,2,1,0:T(8,128)(2,1)S(1)} %get-tuple-element.30), channel_id=1, source_target_pairs={{0,1},{1,2},{2,3},{4,5},{5,6},{6,7},{8,9},{9,10},{10,11},{12,13},{... | collective-permute-start | bytes 663560 | tf_op jit(solution)/shard_map/ppermute | solution.py:18
  18.2 3.7 %copy-start = (bf16[3,3,3,128,128]{4,3,2,1,0:T(8,128)(2,1)S(1)}, bf16[3,3,3,128,128]{4,3,2,1,0:T(8,128)(2,1)}, u32[]{:S(2)}) copy-start(bf16[3,3,3,128,128]{4,3,2,1,0:T(8,128)(2,1)} %param.16) | copy-start | bytes 2654212
  18.3 7.2 %collective-permute-start.2 = (bf16[9,2,32,128]{3,2,1,0:T(8,128)(2,1)S(1)}, bf16[9,2,32,128]{3,2,1,0:T(8,128)(2,1)S(1)}, u32[]{:S(2)}, u32[]{:S(2)}) collective-permute-start(bf16[9,2,32,128]{3,2,1,0:T(8,128)(2,1)S(1)} %pack_down.1), channel_id=1, source_target_pairs={{1,0},{2,1},{3,2},{5,4},{6,5},{7,6},{9,8},{10,9},{11,10},{13,12},{... | collective-permute-start | bytes 442376 | tf_op jit(solution)/shard_map/ppermute | solution.py:18
  22.0 1.4 %copy-start.3 = (f32[128]{0:T(128)S(1)}, f32[128]{0:T(128)}, u32[]{:S(2)}) copy-start(f32[128]{0:T(128)} %param.17) | copy-start | bytes 1540
